TPU v7x, 128 devices: a whole 4x4x4 slice. The times are simulated.
128 devices in a mesh: row: 8 (over x, core), col: 16 (over y, z).
Axes of the slice: x: 4, y: 4, z: 4, core: 2. Of those that a mesh axis runs over, the one named last changes fastest.
Arguments:
- tokens: bfloat16 [8, 1152, 8192], P('row', None, 'col'), may hold values from -64 to 64
- norm_gain: bfloat16 [8192], replicated, may hold values from 0.25 to 1.75
- w_query: bfloat16 [8192, 8192], P('row', 'col'), may hold values from -0.0625 to 0.0625
- w_keyval: bfloat16 [8192, 2048], P('row', 'col'), may hold values from -0.0625 to 0.0625
- kv_cache: bfloat16 [8, 8192, 2048], P('row', None, 'col'), may hold values from -96 to 96
- selected: int32 [8, 1152], P('row'), may hold values from 0 to 8192, as said below
- anchor: int32 [8, 16], P('row'), may hold values from 0 to 8191
Outputs:
- attended: bfloat16 [8, 1152, 8192], P('row', None, 'col')
Inputs may be any that keep to these rules, and one draw needn't show every extreme that they name: Each prompt's row lists distinct positions in increasing order, followed by entries equal to 8192 in the unused slots; at least three quarters of the 1152 slots of a prompt are used and some prompt uses all of them; selected positions fall unevenly over the spans.
All inputs are finite; a program needn't handle non-finite values.
Results may differ from a plain program's by a relative error of at most 0.006.
The roundings to bfloat16 on the way count: a program that leaves them out, or rounds other values in their place, can miss the bound.
Values may be sent and summed in bfloat16 or wider, within the bound.
No kernel may reach another device: no remote copies, remote signals or barrier semaphores. Data moves between devices by JAX's collectives and lax.ppermute only.
A program may use at most 128 MiB of HBM per device.

v0:
```python
import math

import jax
import jax.numpy as jnp
from jax import lax
from jax.sharding import PartitionSpec as P

HD = 128
SPAN = 512
NCHUNK = 16


rope_base = 500000.0
epsilon = 1e-05
masked_score = -1e30


def total_of_pieces(x, axis):
    blocks = lax.all_gather(x, axis)
    return blocks.sum(axis=0)


def from_partner(value, axis, apart):
    mask = 2**apart
    pairs = [(source, source ^ mask) for source in range(lax.axis_size(axis))]
    return lax.ppermute(value, axis, pairs)


def angles(positions, width):
    half_width = width // 2
    exponents = jnp.arange(half_width, dtype=jnp.float32) * (-2.0 / width)
    frequency = jnp.exp(exponents * math.log(rope_base))
    phases = positions[..., None] * frequency
    phases = jnp.concatenate([phases, phases], axis=-1)
    return (jnp.cos(phases), jnp.sin(phases))


def rotate(vectors, cosine, sine_part):
    half_width = vectors.shape[-1] // 2
    turned = jnp.concatenate([-vectors[..., half_width:], vectors[..., :half_width]], axis=-1)
    return vectors * cosine + turned * sine_part


def blend_rows(table, fresh, chosen):
    return table.at[chosen].set(fresh, mode="drop")


def realign(stored, key_mask, anchor):
    prompt_count, length, columns = stored.shape
    parts_here = columns // HD
    offsets = (jnp.arange(NCHUNK, dtype=jnp.int32) * SPAN)[None, :] - anchor
    row_offsets = jnp.repeat(offsets, SPAN, axis=1).astype(jnp.float32)
    cache_cos, cache_sin = angles(row_offsets, HD)
    pieces = stored.reshape(prompt_count, length, parts_here, HD)
    turned = rotate(
        pieces.astype(jnp.float32), cache_cos[:, :, None], cache_sin[:, :, None]
    ).astype(jnp.bfloat16)
    return jnp.where(key_mask[None, None, :, None], turned, pieces)


def attend(queries_one, key_rows, value_rows, chosen):
    slot_count, head_count, _ = queries_one.shape
    length = key_rows.shape[0]
    query_size = slot_count // max(1, slot_count // 512)
    key_size = min(length, 1024)
    scale = HD ** (-0.5)
    results = []
    for offset in range(0, slot_count, query_size):
        part_chosen = chosen[offset : offset + query_size]
        query_block = jnp.transpose(queries_one[offset : offset + query_size], (1, 0, 2)).reshape(
            head_count * query_size, HD
        )
        row_limit = jnp.tile(part_chosen, head_count)
        farthest = jnp.max(jnp.where(part_chosen < length, part_chosen, 0))
        key_blocks = farthest // key_size + 1

        def advance(block_index, carry):
            running_max, denominator, numerator = carry
            key_block = lax.dynamic_slice_in_dim(key_rows, block_index * key_size, key_size, 0)
            value_block = lax.dynamic_slice_in_dim(value_rows, block_index * key_size, key_size, 0)
            scores = (
                jnp.einsum("rd,kd->rk", query_block, key_block, preferred_element_type=jnp.float32)
                * scale
            )
            key_place = block_index * key_size + jnp.arange(key_size, dtype=jnp.int32)
            scores = jnp.where(key_place[None, :] <= row_limit[:, None], scores, masked_score)
            new_max = jnp.maximum(running_max, jnp.max(scores, axis=-1))
            rescale = jnp.exp(running_max - new_max)
            exponentials = jnp.exp(scores - new_max[:, None])
            denominator = denominator * rescale + jnp.sum(exponentials, axis=-1)
            weights = exponentials.astype(jnp.bfloat16)
            numerator = numerator * rescale[:, None] + jnp.dot(
                weights, value_block, preferred_element_type=jnp.float32
            )
            return (new_max, denominator, numerator)

        row_total = head_count * query_size
        initial = (
            jnp.full((row_total,), masked_score, jnp.float32),
            jnp.zeros((row_total,), jnp.float32),
            jnp.zeros((row_total, HD), jnp.float32),
        )
        running_max, denominator, numerator = lax.fori_loop(0, key_blocks, advance, initial)
        outcome = (numerator / denominator[:, None]).reshape(head_count, query_size, HD)
        results.append(jnp.transpose(outcome, (1, 0, 2)).reshape(query_size, head_count * HD))
    return jnp.concatenate(results, axis=0)


def shards(tokens, norm_gain, w_query, w_keyval, kv_cache, selected, anchor):
    col_index = lax.axis_index("col")
    query_rows, keyval_rows = (
        lax.all_gather(w_query, "row", axis=0, tiled=True),
        lax.all_gather(w_keyval, "row", axis=0, tiled=True),
    )
    prompt_count, slot_count, width = tokens.shape
    full_width = query_rows.shape[0]
    head_count = w_query.shape[1] // HD
    parts_here = w_keyval.shape[1] // HD
    length = kv_cache.shape[1]
    hidden = tokens.astype(jnp.float32)
    squares = total_of_pieces(jnp.sum(hidden * hidden, axis=-1, keepdims=True), "col")
    gain_here = lax.dynamic_slice_in_dim(norm_gain, col_index * width, width).astype(jnp.float32)
    normed = (hidden * lax.rsqrt(squares / full_width + epsilon) * gain_here).astype(jnp.bfloat16)
    piece = lax.all_gather(normed, "col", axis=2, tiled=True)
    piece_width = piece.shape[-1]
    flat_piece = piece.reshape(-1, piece_width)
    queries = jnp.dot(flat_piece, query_rows, preferred_element_type=jnp.float32)
    keyval = jnp.dot(flat_piece, keyval_rows, preferred_element_type=jnp.float32)
    cosine, sine_part = angles(selected.astype(jnp.float32), HD)
    cosine = cosine[:, :, None]
    sine_part = sine_part[:, :, None]
    queries = rotate(
        queries.reshape(prompt_count, slot_count, head_count, HD), cosine, sine_part
    ).astype(jnp.bfloat16)
    block_ids = col_index * parts_here + jnp.arange(parts_here, dtype=jnp.int32)
    key_mask = block_ids % 2 == 0
    fresh = keyval.reshape(prompt_count, slot_count, parts_here, HD)
    fresh = jnp.where(
        key_mask[None, None, :, None], rotate(fresh, cosine, sine_part), fresh
    ).astype(jnp.bfloat16)
    mine = jax.vmap(blend_rows)(realign(kv_cache, key_mask, anchor), fresh, selected)
    partner = from_partner(mine, "col", 0)
    holds_key = key_mask[0]
    key_rows = jnp.where(holds_key, mine, partner)[:, :, 0]
    value_rows = jnp.where(holds_key, partner, mine)[:, :, 0]
    results = [attend(queries[0], key_rows[0], value_rows[0], selected[0])]
    attended = jnp.stack(results, axis=0)
    live = (selected < length)[:, :, None]
    return jnp.where(live, attended, 0.0).astype(jnp.bfloat16)


def solution(mesh):
    in_specs = (
        P("row", None, "col"),
        P(),
        P("row", "col"),
        P("row", "col"),
        P("row", None, "col"),
        P("row", None),
        P("row", None),
    )
    out_specs = P("row", None, "col")
    return jax.shard_map(shards, mesh=mesh, in_specs=in_specs, out_specs=out_specs, check_vma=False)
```

profile of v0, /device:TPU:0, one launch (start us, length us, event | category | flops | bytes accessed | tf_op | source)
XLA Modules:
  0.0 374.8 jit_solution(3374914254331183910)
XLA Ops:
  8.9 25.2 %all-gather.1 = f32[16,1,1152]{2,1,0:T(1,128)S(1)} all-gather(f32[1,1,1152]{2,1,0:T(1,128)S(1)} %reshape.649), channel_id=2, replica_groups=mesh['row'=8,'col'=16] {'col'}, dimensions={0}, use_global_device_ids=true | all-gather | bytes 78336 | tf_op jit(solution)/shard_map/all_gather | solution.py:19
  47.8 17.9 %fusion.41 = bf16[8192,128]{1,0:T(8,128)(2,1)S(1)} fusion(bf16[1,8192,128]{2,1,0:T(8,128)(2,1)S(1)} %copy-done.2, f32[1,8192,1,64]{3,1,2,0:T(8,128)S(1)} %get-tuple-element.200, f32[1,8192,1,64]{3,1,2,0:T(8,128)S(1)} %get-tuple-element.199, f32[1,8192,1,64]{3,1,2,0:T(8,128)S(1)} %multiply_bitcast_fusion, pred[]{:T(512)} %bitcast.1), kind=kLoop, calls=%fused_computation.55 | loop fusion | flops 8388608 | bytes 10485761
  65.7 105.6 %all-gather.6.cloned.1.call-done = bf16[1,1152,8192]{2,1,0:T(8,128)(2,1)} async-done(((bf16[1,1152,512]{2,1,0:T(8,128)(2,1)}), bf16[1,1152,8192]{2,1,0:T(8,128)(2,1)}) %all-gather.6.cloned.1.call-update) | async-done | bytes 18874384 | tf_op jit(solution)/shard_map/all_gather | solution.py:124
  171.3 11.0 %fusion.30 = f32[1152,128]{0,1:T(8,128)S(1)} fusion(bf16[8192,128]{1,0:T(8,128)(2,1)} %all-gather.8.cloned.1.call-done, bf16[1,1152,8192]{2,1,0:T(8,128)(2,1)} %all-gather.6.cloned.1.call-done), kind=kOutput, calls=%fused_computation.33 | convolution fusion | flops 2415919104 | bytes 21561344 | tf_op jit(solution)/shard_map/dot_general | solution.py:128
  182.4 4.1 %fusion.43 = (f32[1152,128]{0,1:T(8,128)S(1)}, bf16[1152,128]{0,1:T(8,128)(2,1)}, f32[1152,128]{0,1:T(8,128)S(1)}) fusion(f32[1152,64]{0,1:T(8,128)} %broadcast_multiply_fusion, f32[1152,128]{0,1:T(8,128)S(1)} %fusion.30, f32[1152,64]{0,1:T(8,128)S(1)} %get-tuple-element.206, f32[1152,64]{0,1:T(8,128)S(1)} %get-tuple-element.205, pred[]{:T(512)} %bitcast.1), kind=kLoop, calls=%fused_computation.63 | loop fusion | flops 1032192 | bytes 2949121 | tf_op jit(solution)/shard_map/cos | solution.py:35
  188.3 7.8 %scatter_fusion = bf16[8192,128]{1,0:T(8,128)(2,1)S(1)} fusion(bf16[8192,128]{1,0:T(8,128)(2,1)S(1)} %fusion.41, s32[1152]{0:T(1024)S(1)} %broadcast_select_fusion, bf16[1152,128]{1,0:T(8,128)(2,1)} %copy.17), kind=kCustom, calls=%fused_computation | custom fusion | bytes 889344
  197.4 24.6 %all-gather.10.cloned.1.call-done = bf16[8192,512]{1,0:T(8,128)(2,1)} async-done(((bf16[1024,512]{1,0:T(8,128)(2,1)}), bf16[8192,512]{1,0:T(8,128)(2,1)}) %all-gather.10.cloned.1.call-update) | async-done | bytes 8388624 | tf_op jit(solution)/shard_map/all_gather | solution.py:112
  222.0 17.6 %fusion.28 = f32[1152,512]{0,1:T(8,128)} fusion(bf16[8192,512]{1,0:T(8,128)(2,1)} %all-gather.10.cloned.1.call-done, bf16[1,1152,8192]{2,1,0:T(8,128)(2,1)} %all-gather.6.cloned.1.call-done), kind=kOutput, calls=%fused_computation.31 | convolution fusion | flops 9663676416 | bytes 29622272 | tf_op jit(solution)/shard_map/dot_general | solution.py:127
  244.1 3.9 %select_bitcast_fusion = (bf16[8192,128]{1,0:T(8,128)(2,1)}, bf16[8192,128]{1,0:T(8,128)(2,1)}) fusion(bf16[1,8192,1,128]{3,1,2,0:T(8,128)(2,1)} %collective-permute-done, pred[]{:T(512)} %bitcast.1, bf16[8192,128]{1,0:T(8,128)(2,1)S(1)} %scatter_fusion), kind=kLoop, calls=%fused_computation.53 | loop fusion | flops 2097152 | bytes 8388609 | tf_op jit(solution)/shard_map/squeeze;squeeze | solution.py:146
  248.1 54.5 %while.30 = (s32[]{:T(128)}, f32[2304]{0:T(1024)S(1)}, f32[2304]{0:T(1024)S(1)}, f32[2304,128]{1,0:T(8,128)S(1)}, s32[]{:T(128)}, /*index=5*/bf16[8192,128]{1,0:...) while((s32[]{:T(128)}, f32[2304]{0:T(1024)S(1)}, ...), condition=%wide.region_7.8_spmd.clone, body=%wide.region_4.7_spmd.clone.sunk | while | flops 1227429376 | bytes 31979960 | solution.py:103
  252.6 3.4 fusion.75
  256.2 2.8 fusion.73
  260.4 3.4 fusion.75
  263.9 2.8 fusion.73
  268.1 3.4 fusion.75
  271.7 2.8 fusion.73
  275.9 3.4 fusion.75
  279.4 2.8 fusion.73
  283.6 3.4 fusion.75
  287.2 2.8 fusion.73
  291.4 3.4 fusion.75
  295.0 2.8 fusion.73
  299.1 3.4 fusion.75
  303.8 62.0 %while.31 = (s32[]{:T(128)}, f32[2304]{0:T(1024)S(1)}, f32[2304]{0:T(1024)S(1)}, f32[2304,128]{1,0:T(8,128)S(1)}, s32[]{:T(128)}, /*index=5*/bf16[8192,128]{1,0:...) while((s32[]{:T(128)}, f32[2304]{0:T(1024)S(1)}, ...), condition=%wide.region_12.13_spmd.clone, body=%wide.region_9.12_spmd.clone.sunk | while | flops 1227429376 | bytes 31979960 | solution.py:103
  308.1 3.4 fusion.81
  315.8 3.4 fusion.81
  323.6 3.4 fusion.81
  331.3 3.4 fusion.81
  339.1 3.4 fusion.81
  346.8 3.4 fusion.81
  354.6 3.4 fusion.81
  362.3 3.4 fusion.81
  (185 shorter events, 68.9 us)
Async XLA Ops:
  6.5 28.4 %copy-start.3 = (bf16[1,1152,512]{2,1,0:T(8,128)(2,1)S(1)}, bf16[1,1152,512]{2,1,0:T(8,128)(2,1)}, u32[]{:S(2)}) copy-start(bf16[1,1152,512]{2,1,0:T(8,128)(2,1)} %param.11) | copy-start | bytes 3538948
  6.5 59.2 %all-gather.8.cloned.1.call-start = ((), (), s32[]{:S(2)}) async-start(), calls=%async_computation.1 | async-start | bytes 2359296 | tf_op jit(solution)/shard_map/all_gather | solution.py:113
  7.3 164.1 %all-gather.6.cloned.1.call-start = ((), (), s32[]{:S(2)}) async-start(), calls=%async_computation | async-start | bytes 20054016 | tf_op jit(solution)/shard_map/all_gather | solution.py:124
  34.1 3.0 copy-start.5
  34.2 8.9 %copy-start.9 = (s32[1,16]{1,0:T(1,128)S(1)}, s32[1,16]{1,0:T(1,128)}, u32[]{:S(2)}) copy-start(s32[1,16]{1,0:T(1,128)} %param.17) | copy-start | bytes 196
  35.0 8.8 %copy-start.8 = (s32[2]{0:T(128)S(1)}, s32[2]{0:T(128)}, u32[]{:S(2)}) copy-start(s32[2]{0:T(128)} %constant.110) | copy-start | bytes 28
  35.0 8.9 %copy-start.7 = (s32[2]{0:T(128)S(1)}, s32[2]{0:T(128)}, u32[]{:S(2)}) copy-start(s32[2]{0:T(128)} %constant.113) | copy-start | bytes 28
  36.4 185.6 %all-gather.10.cloned.1.call-start = ((), (), s32[]{:S(2)}) async-start(), calls=%async_computation.2 | async-start | bytes 9437184 | tf_op jit(solution)/shard_map/all_gather | solution.py:112
  43.1 2.8 copy-start.1
  46.2 1.6 copy-start.2
  196.1 48.0 %collective-permute-start = (bf16[1,8192,1,128]{3,1,2,0:T(8,128)(2,1)S(1)}, bf16[1,8192,1,128]{3,1,2,0:T(8,128)(2,1)}, u32[]{:S(2)}, u32[]{:S(2)}) collective-permute-start(bf16[1,8192,1,128]{3,1,2,0:T(8,128)(2,1)S(1)} %bitcast.68), channel_id=1, source_target_pairs={{0,1},{1,0},{2,3},{3,2},{4,5},{5,4},{6,7},{7,6},{8,9},{9,8},{10,11... | collective-permute-start | bytes 6291464 | tf_op jit(solution)/shard_map/ppermute | solution.py:26
  239.6 2.4 copy-start
  244.1 4.0 %copy-start.4 = (bf16[4,576,128]{2,1,0:T(8,128)(2,1)S(1)}, bf16[4,576,128]{2,1,0:T(8,128)(2,1)}, u32[]{:S(2)}) copy-start(bf16[4,576,128]{2,1,0:T(8,128)(2,1)} %copy.18) | copy-start | bytes 1769476
  365.8 1.1 copy-start.6
Sparse Core Ops, SparseCore 0:
  9.1 27.5 all-gather.7
  38.8 132.4 all-gather.5
  173.0 48.9 all-gather.9
where the time goes:
time: 372 us; the launch traced here: 375 us
  waiting for transfers between devices  132 us (35%)
  matrix products  122 us (33%)
  other arithmetic  59 us (16%)
  blocking collectives  25.2 us (7%)
  between operations  18.6 us (5%)
  local copies, waits for them, and re-layouts  15.1 us (4%)
    all_gather x1, waiting for transfers between devices, shards(): piece = lax.all_gather(normed, 'col', axis=2, tiled=True)  106 us
    dot_general x15, matrix products, advance(): jnp.dot(weights, value_block, preferred_element_type=jnp.float32)  51.3 us
    dot_general x15, matrix products, advance(): jnp.einsum('rd,kd->rk', query_block, key_block, preferred_element_type=jn...  42.6 us
    all_gather x1, blocking collectives, total_of_pieces(): blocks = lax.all_gather(x, axis)  25.2 us
    all_gather x1, waiting for transfers between devices, shards(): lax.all_gather(w_query, 'row', axis=0, tiled=True)  24.6 us
    reduce_sum x15, other arithmetic, advance(): denominator = denominator * rescale + jnp.sum(exponentials, axis=-1)  19.7 us
    unnamed x4, other arithmetic  18 us
    dot_general x1, matrix products, shards(): jnp.dot(flat_piece, query_rows, preferred_element_type=jnp.float32)  17.6 us
  transfers between devices with their start and end apart: 4, of which 2 were waited for; matrix products, arithmetic and copies ran while one was open for 20% of the time, Pallas kernels for 0%

commit v1 on v0

v1 whole, which is shorter than its diff:
```python
import functools
import math

import jax
import jax.numpy as jnp
from jax import lax
from jax.experimental import pallas as pl
from jax.experimental.pallas import tpu as pltpu
from jax.sharding import PartitionSpec as P

HD = 128
SPAN = 512
NCHUNK = 16
LENGTH = SPAN * NCHUNK
HEADS = 4
KEYS = 512
SLOTS = 128
HIDDEN_POSITION = 4 * LENGTH

rope_base = 500000.0
epsilon = 1e-05
masked_score = -1e30
exponent_scale = HD ** (-0.5) * math.log2(math.e)


def col_shift(dy, dz):
    return [(4 * y + z, 4 * ((y + dy) % 4) + (z + dz) % 4) for y in range(4) for z in range(4)]


def row_shift(dx):
    return [(2 * x + core, 2 * ((x + dx) % 4) + core) for x in range(4) for core in range(2)]


def flipped(count):
    return [(place, place ^ 1) for place in range(count)]


def angles(positions, width):
    half_width = width // 2
    exponents = jnp.arange(half_width, dtype=jnp.float32) * (-2.0 / width)
    frequency = jnp.exp(exponents * math.log(rope_base))
    phases = positions[..., None] * frequency
    cosine, sine_part = jnp.cos(phases), jnp.sin(phases)
    return (
        jnp.concatenate([cosine, cosine], axis=-1),
        jnp.concatenate([-sine_part, sine_part], axis=-1),
    )


def rotate(vectors, cosine, signed_sine):
    return vectors * cosine + pltpu.roll(vectors, HD // 2, 1) * signed_sine


def prepare_kernel(
    holds_key_ref, own_ref, partner_ref, cosine_ref, sine_ref, chosen_ref, key_ref, value_ref, place_ref
):
    step = pl.program_id(0)
    holds_key = holds_key_ref[0] == 1
    own = own_ref[...]
    partner = partner_ref[...]
    stored_key = jnp.where(holds_key, own, partner).astype(jnp.float32)
    stored_value = jnp.where(holds_key, partner, own).astype(jnp.float32)
    key_ref[...] = rotate(stored_key, cosine_ref[0], sine_ref[0]).astype(jnp.bfloat16)
    value_ref[...] = stored_value.T.astype(jnp.bfloat16)
    place = step * SPAN + lax.broadcasted_iota(jnp.int32, (SPAN, HD), 0)
    seen = jnp.zeros((SPAN, HD), jnp.int32)
    for start in range(0, chosen_ref.shape[1], HD):
        seen = jnp.where(place == chosen_ref[0:1, start : start + HD], 1, seen)
    replaced = jnp.max(seen, axis=1, keepdims=True) > 0
    place_ref[...] = jnp.where(replaced, HIDDEN_POSITION, place)


def prepare(holds_key, own, partner, cosine, signed_sine, chosen):
    block = pl.BlockSpec((SPAN, HD), lambda step, flag: (step, 0))
    angle = pl.BlockSpec((1, 1, HD), lambda step, flag: (step, 0, 0))
    return pl.pallas_call(
        prepare_kernel,
        out_shape=(
            jax.ShapeDtypeStruct((LENGTH, HD), jnp.bfloat16),
            jax.ShapeDtypeStruct((HD, LENGTH), jnp.bfloat16),
            jax.ShapeDtypeStruct((LENGTH, HD), jnp.int32),
        ),
        grid_spec=pltpu.PrefetchScalarGridSpec(
            num_scalar_prefetch=1,
            grid=(NCHUNK,),
            in_specs=[
                block,
                block,
                angle,
                angle,
                pl.BlockSpec((1, chosen.shape[1]), lambda step, flag: (0, 0)),
            ],
            out_specs=(
                block,
                pl.BlockSpec((HD, SPAN), lambda step, flag: (0, step)),
                block,
            ),
        ),
        cost_estimate=pl.CostEstimate(flops=10**7, bytes_accessed=12 * 2**20, transcendentals=0),
        name="prepare",
    )(holds_key, own, partner, cosine, signed_sine, chosen)


def project_kernel(pieces, place_ref, *refs):
    token_ref, gain_ref, cosine_ref, sine_ref = refs[:4]
    weight_refs = refs[4 : 4 + pieces]
    query_ref, key_ref, value_ref = refs[4 + pieces : 7 + pieces]
    held, weights, total, squares, token_sem, weight_sem = refs[7 + pieces :]
    blocks, slots, width = held.shape
    copies = [
        pltpu.make_async_copy(token_ref.at[block], held.at[block], token_sem.at[block])
        for block in range(blocks)
    ]
    for copy in copies:
        copy.start()
    weight_copies = []
    for piece, ref in enumerate(weight_refs):
        start = pl.multiple_of(place_ref[piece] * width, width)
        copy = pltpu.make_async_copy(
            ref, weights.at[pl.ds(start, ref.shape[0]), :], weight_sem.at[piece]
        )
        copy.start()
        weight_copies.append(copy)
    squares[...] = jnp.zeros_like(squares)
    for block in range(blocks):
        copies[block].wait()
        hidden = held[block].astype(jnp.float32)
        hidden = hidden * hidden
        part = hidden[:, :HD]
        for start in range(HD, width, HD):
            part = part + hidden[:, start : start + HD]
        squares[...] += part
    mean_square = jnp.sum(squares[...], axis=1, keepdims=True) * (1.0 / (blocks * width))
    squares[...] = jnp.broadcast_to(lax.rsqrt(mean_square + epsilon), squares.shape)
    for copy in weight_copies:
        copy.wait()
    total[...] = jnp.zeros_like(total)

    def add_block(block, carry):
        start = pl.multiple_of(block * width, width)
        scale = squares[:, 0:1]
        hidden = held[block].astype(jnp.float32) * scale * gain_ref[block].astype(jnp.float32)
        total[...] += jnp.dot(
            hidden.astype(jnp.bfloat16),
            weights[pl.ds(start, width), :],
            preferred_element_type=jnp.float32,
        )
        return carry

    lax.fori_loop(0, blocks, add_block, 0)
    cosine, signed_sine = cosine_ref[...], sine_ref[...]
    for head in range(HEADS):
        part = total[:, head * HD : (head + 1) * HD]
        query_ref[head] = rotate(part, cosine, signed_sine).astype(jnp.bfloat16)
    key_ref[...] = rotate(total[:, HEADS * HD : (HEADS + 1) * HD], cosine, signed_sine).astype(
        jnp.bfloat16
    )
    value_ref[...] = total[:, (HEADS + 1) * HD :].T.astype(jnp.bfloat16)


def project(tokens, gain, cosine, signed_sine, weight_pieces, places):
    blocks, slots, width = tokens.shape
    columns = (HEADS + 2) * HD
    pieces = len(weight_pieces)
    whole = pl.BlockSpec(memory_space=pltpu.VMEM)
    remote = pl.BlockSpec(memory_space=pl.ANY)
    return pl.pallas_call(
        functools.partial(project_kernel, pieces),
        out_shape=(
            jax.ShapeDtypeStruct((HEADS, slots, HD), jnp.bfloat16),
            jax.ShapeDtypeStruct((slots, HD), jnp.bfloat16),
            jax.ShapeDtypeStruct((HD, slots), jnp.bfloat16),
        ),
        in_specs=[pl.BlockSpec(memory_space=pltpu.SMEM), remote, whole, whole, whole]
        + [remote] * pieces,
        out_specs=(whole, whole, whole),
        scratch_shapes=[
            pltpu.VMEM((blocks, slots, width), jnp.bfloat16),
            pltpu.VMEM((blocks * width, columns), jnp.bfloat16),
            pltpu.VMEM((slots, columns), jnp.float32),
            pltpu.VMEM((slots, HD), jnp.float32),
            pltpu.SemaphoreType.DMA((blocks,)),
            pltpu.SemaphoreType.DMA((pieces,)),
        ],
        compiler_params=pltpu.CompilerParams(vmem_limit_bytes=58 * 2**20),
        cost_estimate=pl.CostEstimate(
            flops=2 * slots * blocks * width * columns,
            bytes_accessed=2 * blocks * width * (slots + columns),
            transcendentals=0,
        ),
        name="project",
    )(places, tokens, gain, cosine, signed_sine, *weight_pieces)


def attend_kernel(
    first,
    blocks_ref,
    query_ref,
    chosen_ref,
    key_ref,
    value_ref,
    place_ref,
    fresh_key_ref,
    fresh_value_ref,
    fresh_place_ref,
    out_ref,
    peak,
    denominator,
    numerator,
    held,
):
    step = pl.program_id(0)
    rows = HEADS * SLOTS
    peak[...] = jnp.full_like(peak, masked_score)
    denominator[...] = jnp.zeros_like(denominator)
    numerator[...] = jnp.zeros_like(numerator)
    queries = query_ref[...].reshape(rows, HD)
    limit = jnp.concatenate([chosen_ref[...]] * HEADS, axis=1)

    def score(keys, block, slot):
        start = pl.multiple_of(block * KEYS, KEYS)
        held[slot] = lax.dot_general(
            keys[pl.ds(start, KEYS), :],
            queries,
            (((1,), (1,)), ((), ())),
            preferred_element_type=jnp.float32,
        )

    def gather(values, places, block, slot):
        start = pl.multiple_of(block * KEYS, KEYS)
        place = jnp.concatenate([places[pl.ds(start, KEYS), :]] * HEADS, axis=1)
        scores = jnp.where(place <= limit, held[slot], masked_score)
        old_peak = peak[...]
        new_peak = jnp.maximum(old_peak, jnp.max(scores, axis=0, keepdims=True))
        rescale = jnp.exp2((old_peak - new_peak) * exponent_scale)
        weights = jnp.exp2((scores - new_peak) * exponent_scale)
        denominator[...] = denominator[...] * rescale + jnp.sum(weights, axis=0, keepdims=True)
        numerator[...] = numerator[...] * rescale + jnp.dot(
            values[:, pl.ds(start, KEYS)],
            weights.astype(jnp.bfloat16),
            preferred_element_type=jnp.float32,
        )
        peak[...] = new_peak

    def walk(keys, values, places, count):
        last = jnp.maximum(count - 1, 0)
        score(keys, 0, 0)

        def pair(turn, carry):
            block = 2 * turn
            score(keys, jnp.minimum(block + 1, last), 1)
            gather(values, places, block, 0)
            score(keys, jnp.minimum(block + 2, last), 0)
            gather(values, places, block + 1, 1)
            return carry

        lax.fori_loop(0, count // 2, pair, 0)

        @pl.when(count % 2 == 1)
        def _():
            gather(values, places, count - 1, 0)

    walk(key_ref, value_ref, place_ref, blocks_ref[step])
    walk(
        fresh_key_ref,
        fresh_value_ref,
        fresh_place_ref,
        ((first + step + 1) * SLOTS + KEYS - 1) // KEYS,
    )
    outcome = jnp.where(limit < LENGTH, numerator[...] / denominator[...], 0.0)
    for head in range(HEADS):
        part = outcome[:, head * SLOTS : (head + 1) * SLOTS]
        out_ref[:, head * HD : (head + 1) * HD] = part.T.astype(jnp.bfloat16)


def attend(first, key_blocks, queries, chosen, keys, values, places, fresh_keys, fresh_values, fresh_places):
    slots = queries.shape[1]
    rows = HEADS * SLOTS

    def still(array):
        return pl.BlockSpec(
            array.shape, lambda step, counts: (0, 0), pipeline_mode=pl.Buffered(1)
        )

    return pl.pallas_call(
        functools.partial(attend_kernel, first),
        out_shape=jax.ShapeDtypeStruct((slots, HEADS * HD), jnp.bfloat16),
        grid_spec=pltpu.PrefetchScalarGridSpec(
            num_scalar_prefetch=1,
            grid=(slots // SLOTS,),
            in_specs=[
                pl.BlockSpec((HEADS, SLOTS, HD), lambda step, counts: (0, step, 0)),
                pl.BlockSpec((1, SLOTS), lambda step, counts: (0, step)),
                still(keys),
                still(values),
                still(places),
                still(fresh_keys),
                still(fresh_values),
                still(fresh_places),
            ],
            out_specs=pl.BlockSpec((SLOTS, HEADS * HD), lambda step, counts: (step, 0)),
            scratch_shapes=[
                pltpu.VMEM((1, rows), jnp.float32),
                pltpu.VMEM((1, rows), jnp.float32),
                pltpu.VMEM((HD, rows), jnp.float32),
                pltpu.VMEM((2, KEYS, rows), jnp.float32),
            ],
        ),
        compiler_params=pltpu.CompilerParams(vmem_limit_bytes=48 * 2**20),
        cost_estimate=pl.CostEstimate(
            flops=slots * HEADS * LENGTH * HD * 2,
            bytes_accessed=12 * 2**20,
            transcendentals=slots * HEADS * LENGTH // 2,
        ),
        name="attend",
    )(key_blocks, queries, chosen, keys, values, places, fresh_keys, fresh_values, fresh_places)


def shards(tokens, norm_gain, w_query, w_keyval, kv_cache, selected, anchor):
    row_index = lax.axis_index("row")
    col_index = lax.axis_index("col")
    own_x, own_core = row_index // 2, row_index % 2
    holds_key = col_index % 2 == 0
    own_cache = kv_cache[0]
    other_keyval = lax.ppermute(w_keyval, "col", flipped(16))
    other_cache = lax.ppermute(own_cache, "col", flipped(16))
    gathered = lax.all_gather(tokens[0], "col", axis=0)

    weights = jnp.concatenate(
        [
            w_query,
            jnp.where(holds_key, w_keyval, other_keyval),
            jnp.where(holds_key, other_keyval, w_keyval),
        ],
        axis=1,
    )
    half = weights.shape[0] // 2
    behind = lax.ppermute(weights, "row", row_shift(1))
    ahead = lax.ppermute(weights, "row", row_shift(-1))
    far_first = lax.ppermute(behind[:half], "row", row_shift(1))
    far_second = lax.ppermute(ahead[half:], "row", row_shift(-1))
    mine = [weights, behind, ahead, far_first, far_second]
    theirs = [lax.ppermute(piece, "row", flipped(8)) for piece in mine]
    steps_x = jnp.array([0, 3, 1, 2, 2], jnp.int32)
    second_half = jnp.array([0, 0, 0, 0, 1], jnp.int32)
    source_x = (own_x + steps_x) % 4
    places = jnp.concatenate(
        [
            (source_x * 2 + own_core) * 2 + second_half,
            (source_x * 2 + 1 - own_core) * 2 + second_half,
        ]
    )

    chosen = selected[0]
    slot_count = chosen.shape[0]
    cosine, signed_sine = angles(chosen.astype(jnp.float32), HD)
    offsets = jnp.arange(NCHUNK, dtype=jnp.int32) * SPAN - anchor[0]
    span_cosine, span_sine = angles(offsets.astype(jnp.float32), HD)
    keys, values, key_places = prepare(
        holds_key.astype(jnp.int32)[None],
        own_cache,
        other_cache,
        span_cosine[:, None],
        span_sine[:, None],
        chosen[None],
    )
    grouped = chosen.reshape(-1, SLOTS)
    farthest = jnp.max(jnp.where(grouped < LENGTH, grouped, -1), axis=1)
    key_blocks = (farthest + KEYS) // KEYS
    padded = -(-slot_count // KEYS) * KEYS - slot_count
    fresh_places = jnp.broadcast_to(
        jnp.pad(chosen, (0, padded), constant_values=HIDDEN_POSITION)[:, None],
        (slot_count + padded, HD),
    )

    gain = norm_gain.reshape(NCHUNK, 1, -1)
    queries, fresh_keys, fresh_values = project(
        gathered, gain, cosine, signed_sine, mine + theirs, places
    )
    fresh_keys = jnp.pad(fresh_keys, ((0, padded), (0, 0)))
    fresh_values = jnp.pad(fresh_values, ((0, 0), (0, padded)))
    attended = attend(
        0, key_blocks, queries, chosen[None], keys, values, key_places, fresh_keys, fresh_values, fresh_places
    )
    return attended[None]


def solution(mesh):
    in_specs = (
        P("row", None, "col"),
        P(),
        P("row", "col"),
        P("row", "col"),
        P("row", None, "col"),
        P("row", None),
        P("row", None),
    )
    out_specs = P("row", None, "col")
    return jax.shard_map(shards, mesh=mesh, in_specs=in_specs, out_specs=out_specs, check_vma=False)
```

time: 372 us -> 266 us (0.72)
  the two profiles are of different devices: /device:TPU:0 before, /device:TPU:23 now
where the time goes in v1:
time: 266 us; the launch traced here: 263 us
  Pallas kernels  111 us (42%)
  waiting for transfers between devices  110 us (41%)
  between operations  13.6 us (5%)
  starting transfers between devices  13 us (5%)
  local copies, waits for them, and re-layouts  7.58 us (3%)
  other arithmetic  7.44 us (3%)
    pallas_call x1, Pallas kernels, attend(): pl.pallas_call(functools.partial(attend_kernel, first), out_shape=jax.Sha...  62.7 us
    all_gather x1, waiting for transfers between devices, shards(): gathered = lax.all_gather(tokens[0], 'col', axis=0)  49.9 us
    pallas_call x1, Pallas kernels, project(): pl.pallas_call(functools.partial(project_kernel, pieces), out_shape=(jax....  33.1 us
    ppermute x1, waiting for transfers between devices, shards(): behind = lax.ppermute(weights, 'row', row_shift(1))  32.2 us
    ppermute x1, waiting for transfers between devices, shards(): other_cache = lax.ppermute(own_cache, 'col', flipped(16))  21.4 us
    pallas_call x1, Pallas kernels, prepare(): pl.pallas_call(prepare_kernel, out_shape=(jax.ShapeDtypeStruct((LENGTH, H...  14.9 us
    ppermute x5, starting transfers between devices, shards(): theirs = [lax.ppermute(piece, 'row', flipped(8)) for piece in mine]  8.21 us
    ppermute x1, waiting for transfers between devices, shards(): other_keyval = lax.ppermute(w_keyval, 'col', flipped(16))  6.03 us
  transfers between devices with their start and end apart: 12, of which 4 were waited for; matrix products, arithmetic and copies ran while one was open for 4% of the time, Pallas kernels for 6%

profile of v1, /device:TPU:23, one launch (start us, length us, event | category | flops | bytes accessed | tf_op | source)
XLA Modules:
  0.0 262.6 jit_solution(15958304812993239187)
XLA Ops:
  6.5 0.7 all-gather.2.cloned.1.call-update
  7.3 1.7 collective-permute-start
  9.0 0.1 collective-permute-start.10
  9.1 6.0 %collective-permute-done = bf16[1024,128]{1,0:T(8,128)(2,1)S(1)} collective-permute-done((bf16[1024,128]{1,0:T(8,128)(2,1)}, bf16[1024,128]{1,0:T(8,128)(2,1)S(1)}, u32[]{:S(2)}, u32[]{:S(2)}) %collective-permute-start) | collective-permute-done | bytes 262176 | tf_op jit(solution)/shard_map/ppermute | solution.py:325
  15.1 1.0 broadcast_select_fusion.1
  16.1 1.3 pad_maximum_fusion.refs_4_
  17.4 0.2 collective-permute-start.1
  17.6 1.3 collective-permute-start.2
  19.0 0.1 fusion.1
  19.2 32.2 %collective-permute-done.1.refs_5_ = bf16[1024,768]{1,0:T(8,128)(2,1)} collective-permute-done((bf16[1024,768]{1,0:T(8,128)(2,1)}, bf16[1024,768]{1,0:T(8,128)(2,1)}, u32[]{:S(2)}, u32[]{:S(2)}) %collective-permute-start.1) | collective-permute-done | bytes 1572896 | tf_op jit(solution)/shard_map/ppermute | solution.py:338
  51.4 1.2 slice.8
  52.5 1.5 collective-permute-start.3
  54.0 2.1 slice.9
  56.1 0.6 pad_add_fusion.place_ref
  56.8 0.6 reshape.26.refs_1_
  57.4 3.8 %collective-permute-start.5 = (bf16[1024,768]{1,0:T(8,128)(2,1)}, bf16[1024,768]{1,0:T(8,128)(2,1)}, u32[]{:S(2)}, u32[]{:S(2)}) collective-permute-start(bf16[1024,768]{1,0:T(8,128)(2,1)} %pad_maximum_fusion.refs_4_), channel_id=1, source_target_pairs={{0,16},{16,0},{32,48},{48,32},{64,80},{80,64},{96,112},{112,96},{1... | collective-permute-start | bytes 4718600 | tf_op jit(solution)/shard_map/ppermute | solution.py:343
  61.2 21.4 %collective-permute-done.10.partner_ref = bf16[8192,128]{1,0:T(8,128)(2,1)S(1)} collective-permute-done((bf16[8192,128]{1,0:T(8,128)(2,1)}, bf16[8192,128]{1,0:T(8,128)(2,1)S(1)}, u32[]{:S(2)}, u32[]{:S(2)}) %collective-permute-start.10) | collective-permute-done | bytes 2097184 | tf_op jit(solution)/shard_map/ppermute | solution.py:326
  82.6 3.8 %collective-permute-start.7 = (bf16[1024,768]{1,0:T(8,128)(2,1)}, bf16[1024,768]{1,0:T(8,128)(2,1)}, u32[]{:S(2)}, u32[]{:S(2)}) collective-permute-start(bf16[1024,768]{1,0:T(8,128)(2,1)} %collective-permute-done.2.refs_6_), channel_id=1, source_target_pairs={{0,16},{16,0},{32,48},{48,32},{64,80},{80,64},{96,112},{112,96},{1... | collective-permute-start | bytes 4718600 | tf_op jit(solution)/shard_map/ppermute | solution.py:343
  86.4 0.1 fusion.2
  86.6 0.7 pad_maximum_fusion.3
  87.3 0.3 collective-permute-start.8
  87.6 0.3 collective-permute-start.9
  87.9 2.1 fusion
  90.0 1.4 pad_maximum_fusion.1
  91.4 14.9 %prepare.1 = (bf16[8192,128]{1,0:T(8,128)(2,1)}, bf16[128,8192]{1,0:T(8,128)(2,1)}, s32[8192,128]{1,0:T(8,128)}) custom-call(s32[1]{0:T(128)} %bitcast.holds_key_ref, bf16[8192,128]{1,0:T(8,128)(2,1)} %bitcast.14, bf16[8192,128]{1,0:T(8,128)(2,1)} %copy-done.4, f32[16,1,128]{2,1,0:T(1,128)} %bitcast.15, f32[16,1,128]{2,1,0:T(1,128)} %bitcast.16, ...), custom_call_target="tpu_custom_call" | custom-call | flops 10000000 | bytes 12582912 | tf_op jit(solution)/shard_map/prepare/pallas_call | solution.py:76
  106.4 49.9 %all-gather.2.cloned.1.call-done.refs_0_ = bf16[16,1152,512]{2,1,0:T(8,128)(2,1)} async-done(((bf16[1,1152,512]{2,1,0:T(8,128)(2,1)}), bf16[16,1152,512]{2,1,0:T(8,128)(2,1)}) %all-gather.2.cloned.1.call-update) | async-done | bytes 18874384 | tf_op jit(solution)/shard_map/all_gather | solution.py:327
  156.2 33.1 %project.1 = (bf16[4,1152,128]{2,1,0:T(8,128)(2,1)}, bf16[1152,128]{1,0:T(8,128)(2,1)}, bf16[128,1152]{1,0:T(8,128)(2,1)}) custom-call(s32[10]{0:T(128)} %pad_add_fusion.place_ref, bf16[16,1152,512]{2,1,0:T(8,128)(2,1)} %all-gather.2.cloned.1.call-done.refs_0_, bf16[16,1,512]{2,1,0:T(2,128)(2,1)} %reshape.26.refs_1_, f32[1152,128]{1,0:T(8,128)} %get-tuple-element.27.refs_2_, ...), custom_call_target="tpu_custom_call" | custom-call | flops 14495514624 | bytes 31457280 | tf_op jit(solution)/shard_map/project/pallas_call | solution.py:167
  189.3 1.1 pad.12.fresh_key_ref
  190.5 1.0 pad.13.fresh_value_ref
  191.5 0.3 broadcast_in_dim.33.fresh_place_ref
  191.8 1.3 copy-done.3
  193.0 62.7 %attend.1 = bf16[1152,512]{1,0:T(8,128)(2,1)} custom-call(s32[9]{0:T(128)S(1)} %and_select_fusion.1.blocks_ref, bf16[4,1152,128]{2,1,0:T(8,128)(2,1)S(1)} %copy-done.3, s32[1,1152]{1,0:T(1,128)S(1)} %copy-done.1, bf16[8192,128]{1,0:T(8,128)(2,1)S(1)} %copy-done.2, bf16[128,8192]{1,0:T(8,128)(2,1)} %get-tuple-element.13.value_ref, ...), custom_call_target="tpu_custom_call" | custom-call | flops 9663676416 | bytes 12582912 | tf_op jit(solution)/shard_map/attend/pallas_call | solution.py:285
  (40 shorter events, 0.2 us)
Async XLA Ops:
  6.5 9.6 %copy-start.5 = (bf16[1024,512]{1,0:T(8,128)(2,1)S(1)}, bf16[1024,512]{1,0:T(8,128)(2,1)}, u32[]{:S(2)}) copy-start(bf16[1024,512]{1,0:T(8,128)(2,1)} %param.11) | copy-start | bytes 3145732
  6.5 149.7 %all-gather.2.cloned.1.call-start = ((), (), s32[]{:S(2)}) async-start(), calls=%async_computation | async-start | bytes 20054016 | tf_op jit(solution)/shard_map/all_gather | solution.py:327
  7.3 7.8 %collective-permute-start = (bf16[1024,128]{1,0:T(8,128)(2,1)}, bf16[1024,128]{1,0:T(8,128)(2,1)S(1)}, u32[]{:S(2)}, u32[]{:S(2)}) collective-permute-start(bf16[1024,128]{1,0:T(8,128)(2,1)} %param.12), channel_id=1, source_target_pairs={{0,1},{1,0},{2,3},{3,2},{4,5},{5,4},{6,7},{7,6},{8,9},{9,8},{10,11... | collective-permute-start | bytes 786440 | tf_op jit(solution)/shard_map/ppermute | solution.py:325
  9.0 73.6 %collective-permute-start.10 = (bf16[8192,128]{1,0:T(8,128)(2,1)}, bf16[8192,128]{1,0:T(8,128)(2,1)S(1)}, u32[]{:S(2)}, u32[]{:S(2)}) collective-permute-start(bf16[8192,128]{1,0:T(8,128)(2,1)} %bitcast.13), channel_id=1, source_target_pairs={{0,1},{1,0},{2,3},{3,2},{4,5},{5,4},{6,7},{7,6},{8,9},{9,8},{10,11... | collective-permute-start | bytes 6291464 | tf_op jit(solution)/shard_map/ppermute | solution.py:326
  16.1 2.8 %copy-start = (s32[1,1152]{1,0:T(1,128)S(1)}, s32[1,1152]{1,0:T(1,128)}, u32[]{:S(2)}) copy-start(s32[1,1152]{1,0:T(1,128)} %chosen_ref.3) | copy-start | bytes 13828
  16.1 3.0 %copy-start.7 = (s32[5]{0:T(128)S(1)}, s32[5]{0:T(128)}, u32[]{:S(2)}) copy-start(s32[5]{0:T(128)} %constant.88.clone) | copy-start | bytes 64
  16.1 3.0 %copy-start.8 = (s32[5]{0:T(128)S(1)}, s32[5]{0:T(128)}, u32[]{:S(2)}) copy-start(s32[5]{0:T(128)} %constant.87.clone) | copy-start | bytes 64
  17.4 33.9 %collective-permute-start.1 = (bf16[1024,768]{1,0:T(8,128)(2,1)}, bf16[1024,768]{1,0:T(8,128)(2,1)}, u32[]{:S(2)}, u32[]{:S(2)}) collective-permute-start(bf16[1024,768]{1,0:T(8,128)(2,1)} %pad_maximum_fusion.refs_4_), channel_id=1, source_target_pairs={{0,32},{16,48},{32,64},{48,80},{64,96},{80,112},{96,0},{112,16},{1... | collective-permute-start | bytes 4718600 | tf_op jit(solution)/shard_map/ppermute | solution.py:338
  17.6 36.4 %collective-permute-start.2 = (bf16[1024,768]{1,0:T(8,128)(2,1)}, bf16[1024,768]{1,0:T(8,128)(2,1)}, u32[]{:S(2)}, u32[]{:S(2)}) collective-permute-start(bf16[1024,768]{1,0:T(8,128)(2,1)} %pad_maximum_fusion.refs_4_), channel_id=1, source_target_pairs={{0,96},{16,112},{32,0},{48,16},{64,32},{80,48},{96,64},{112,80},{1... | collective-permute-start | bytes 4718600 | tf_op jit(solution)/shard_map/ppermute | solution.py:339
  19.1 37.6 %copy-start.6 = (bf16[8192]{0:T(1024)(128)(2,1)S(1)}, bf16[8192]{0:T(1024)(128)(2,1)}, u32[]{:S(2)}) copy-start(bf16[8192]{0:T(1024)(128)(2,1)} %param.10) | copy-start | bytes 49156
  19.1 67.3 %copy-start.10 = (s32[1,16]{1,0:T(1,128)S(1)}, s32[1,16]{1,0:T(1,128)}, u32[]{:S(2)}) copy-start(s32[1,16]{1,0:T(1,128)} %param.15) | copy-start | bytes 196
  52.5 34.7 %collective-permute-start.3 = (bf16[512,768]{1,0:T(8,128)(2,1)S(1)}, bf16[512,768]{1,0:T(8,128)(2,1)}, u32[]{:S(2)}, u32[]{:S(2)}) collective-permute-start(bf16[512,768]{1,0:T(8,128)(2,1)S(1)} %slice.8), channel_id=1, source_target_pairs={{0,32},{16,48},{32,64},{48,80},{64,96},{80,112},{96,0},{112,16},{1... | collective-permute-start | bytes 2359304 | tf_op jit(solution)/shard_map/ppermute | solution.py:340
  56.1 31.5 %collective-permute-start.4 = (bf16[512,768]{1,0:T(8,128)(2,1)}, bf16[512,768]{1,0:T(8,128)(2,1)}, u32[]{:S(2)}, u32[]{:S(2)}) collective-permute-start(bf16[512,768]{1,0:T(8,128)(2,1)} %slice.9), channel_id=1, source_target_pairs={{0,96},{16,112},{32,0},{48,16},{64,32},{80,48},{96,64},{112,80},{1... | collective-permute-start | bytes 2359304 | tf_op jit(solution)/shard_map/ppermute | solution.py:341
  57.4 49.0 %collective-permute-start.5 = (bf16[1024,768]{1,0:T(8,128)(2,1)}, bf16[1024,768]{1,0:T(8,128)(2,1)}, u32[]{:S(2)}, u32[]{:S(2)}) collective-permute-start(bf16[1024,768]{1,0:T(8,128)(2,1)} %pad_maximum_fusion.refs_4_), channel_id=1, source_target_pairs={{0,16},{16,0},{32,48},{48,32},{64,80},{80,64},{96,112},{112,96},{1... | collective-permute-start | bytes 4718600 | tf_op jit(solution)/shard_map/ppermute | solution.py:343
  61.2 45.2 %collective-permute-start.6 = (bf16[1024,768]{1,0:T(8,128)(2,1)}, bf16[1024,768]{1,0:T(8,128)(2,1)}, u32[]{:S(2)}, u32[]{:S(2)}) collective-permute-start(bf16[1024,768]{1,0:T(8,128)(2,1)} %collective-permute-done.1.refs_5_), channel_id=1, source_target_pairs={{0,16},{16,0},{32,48},{48,32},{64,80},{80,64},{96,112},{112,96},{1... | collective-permute-start | bytes 4718600 | tf_op jit(solution)/shard_map/ppermute | solution.py:343
  82.6 8.8 %copy-start.4 = (bf16[8192,128]{1,0:T(8,128)(2,1)}, bf16[8192,128]{1,0:T(8,128)(2,1)S(1)}, u32[]{:S(2)}) copy-start(bf16[8192,128]{1,0:T(8,128)(2,1)S(1)} %collective-permute-done.10.partner_ref) | copy-start | bytes 6291460
  82.6 23.8 %collective-permute-start.7 = (bf16[1024,768]{1,0:T(8,128)(2,1)}, bf16[1024,768]{1,0:T(8,128)(2,1)}, u32[]{:S(2)}, u32[]{:S(2)}) collective-permute-start(bf16[1024,768]{1,0:T(8,128)(2,1)} %collective-permute-done.2.refs_6_), channel_id=1, source_target_pairs={{0,16},{16,0},{32,48},{48,32},{64,80},{80,64},{96,112},{112,96},{1... | collective-permute-start | bytes 4718600 | tf_op jit(solution)/shard_map/ppermute | solution.py:343
  87.3 19.1 %collective-permute-start.8 = (bf16[512,768]{1,0:T(8,128)(2,1)}, bf16[512,768]{1,0:T(8,128)(2,1)S(1)}, u32[]{:S(2)}, u32[]{:S(2)}) collective-permute-start(bf16[512,768]{1,0:T(8,128)(2,1)} %collective-permute-done.3.refs_7_), channel_id=1, source_target_pairs={{0,16},{16,0},{32,48},{48,32},{64,80},{80,64},{96,112},{112,96},{1... | collective-permute-start | bytes 2359304 | tf_op jit(solution)/shard_map/ppermute | solution.py:343
  87.6 18.8 %collective-permute-start.9 = (bf16[512,768]{1,0:T(8,128)(2,1)}, bf16[512,768]{1,0:T(8,128)(2,1)}, u32[]{:S(2)}, u32[]{:S(2)}) collective-permute-start(bf16[512,768]{1,0:T(8,128)(2,1)} %collective-permute-done.4.refs_8_), channel_id=1, source_target_pairs={{0,16},{16,0},{32,48},{48,32},{64,80},{80,64},{96,112},{112,96},{1... | collective-permute-start | bytes 2359304 | tf_op jit(solution)/shard_map/ppermute | solution.py:343
  106.3 49.9 %copy-start.9 = (bf16[512,768]{1,0:T(8,128)(2,1)}, bf16[512,768]{1,0:T(8,128)(2,1)S(1)}, u32[]{:S(2)}) copy-start(bf16[512,768]{1,0:T(8,128)(2,1)S(1)} %collective-permute-done.8.refs_12_) | copy-start | bytes 2359300
  189.3 2.4 copy-start.1
  189.3 2.4 copy-start.2
  191.8 1.3 copy-start.3
Sparse Core Ops, SparseCore 0:
  9.5 146.6 all-gather.1

commit v2 on v1

--- a/solution.py
+++ b/solution.py
@@ -16,6 +16,8 @@
 KEYS = 512
 SLOTS = 128
 HIDDEN_POSITION = 4 * LENGTH
+EARLY = 5
+Y_FIRST = 2
 
 rope_base = 500000.0
 epsilon = 1e-05
@@ -101,35 +103,40 @@
     )(holds_key, own, partner, cosine, signed_sine, chosen)
 
 
-def project_kernel(pieces, place_ref, *refs):
-    token_ref, gain_ref, cosine_ref, sine_ref = refs[:4]
-    weight_refs = refs[4 : 4 + pieces]
-    query_ref, key_ref, value_ref = refs[4 + pieces : 7 + pieces]
-    held, weights, total, squares, token_sem, weight_sem = refs[7 + pieces :]
+def project_kernel(offsets, token_count, weight_count, done, *refs):
+    token_place_ref, weight_place_ref, gain_ref, cosine_ref, sine_ref, old_key_ref, old_value_ref = refs[:7]
+    refs = refs[7:]
+    token_refs, refs = refs[:token_count], refs[token_count:]
+    weight_refs, refs = refs[:weight_count], refs[weight_count:]
+    query_ref, key_ref, value_ref, held, weights, total, squares, token_sem, weight_sem = refs
     blocks, slots, width = held.shape
-    copies = [
-        pltpu.make_async_copy(token_ref.at[block], held.at[block], token_sem.at[block])
-        for block in range(blocks)
-    ]
-    for copy in copies:
-        copy.start()
+    token_copies = []
+    for piece, ref in enumerate(token_refs):
+        for part in range(ref.shape[0]):
+            number = len(token_copies)
+            where = held.at[token_place_ref[number], pl.ds(offsets[piece], ref.shape[1]), :]
+            token_copies.append(pltpu.make_async_copy(ref.at[part], where, token_sem.at[number]))
     weight_copies = []
     for piece, ref in enumerate(weight_refs):
-        start = pl.multiple_of(place_ref[piece] * width, width)
-        copy = pltpu.make_async_copy(
-            ref, weights.at[pl.ds(start, ref.shape[0]), :], weight_sem.at[piece]
-        )
+        start = pl.multiple_of(weight_place_ref[piece] * width, width)
+        where = weights.at[pl.ds(start, ref.shape[0]), :]
+        weight_copies.append(pltpu.make_async_copy(ref, where, weight_sem.at[piece]))
+    for copy in token_copies + weight_copies:
         copy.start()
-        weight_copies.append(copy)
+    for copy in token_copies:
+        copy.wait()
     squares[...] = jnp.zeros_like(squares)
-    for block in range(blocks):
-        copies[block].wait()
+
+    def add_squares(block, carry):
         hidden = held[block].astype(jnp.float32)
         hidden = hidden * hidden
         part = hidden[:, :HD]
         for start in range(HD, width, HD):
             part = part + hidden[:, start : start + HD]
         squares[...] += part
+        return carry
+
+    lax.fori_loop(0, blocks, add_squares, 0)
     mean_square = jnp.sum(squares[...], axis=1, keepdims=True) * (1.0 / (blocks * width))
     squares[...] = jnp.broadcast_to(lax.rsqrt(mean_square + epsilon), squares.shape)
     for copy in weight_copies:
@@ -138,7 +145,7 @@
 
     def add_block(block, carry):
         start = pl.multiple_of(block * width, width)
-        scale = squares[:, 0:1]
+        scale = jnp.concatenate([squares[...]] * (width // HD), axis=1)
         hidden = held[block].astype(jnp.float32) * scale * gain_ref[block].astype(jnp.float32)
         total[...] += jnp.dot(
             hidden.astype(jnp.bfloat16),
@@ -152,44 +159,53 @@
     for head in range(HEADS):
         part = total[:, head * HD : (head + 1) * HD]
         query_ref[head] = rotate(part, cosine, signed_sine).astype(jnp.bfloat16)
-    key_ref[...] = rotate(total[:, HEADS * HD : (HEADS + 1) * HD], cosine, signed_sine).astype(
-        jnp.bfloat16
-    )
-    value_ref[...] = total[:, (HEADS + 1) * HD :].T.astype(jnp.bfloat16)
-
-
-def project(tokens, gain, cosine, signed_sine, weight_pieces, places):
-    blocks, slots, width = tokens.shape
+    if done:
+        key_ref[:done, :] = old_key_ref[:done, :]
+        value_ref[:, :done] = old_value_ref[:, :done]
+    key_ref[done : done + slots, :] = rotate(
+        total[:, HEADS * HD : (HEADS + 1) * HD], cosine, signed_sine
+    ).astype(jnp.bfloat16)
+    value_ref[:, done : done + slots] = total[:, (HEADS + 1) * HD :].T.astype(jnp.bfloat16)
+    if done + slots < key_ref.shape[0]:
+        key_ref[done + slots :, :] = jnp.zeros_like(key_ref[done + slots :, :])
+        value_ref[:, done + slots :] = jnp.zeros_like(value_ref[:, done + slots :])
+
+
+def project(token_pieces, offsets, token_places, gain, cosine, signed_sine, weight_pieces, weight_places, done, old):
+    slots = cosine.shape[0]
+    width = token_pieces[0].shape[-1]
+    blocks = gain.shape[0]
     columns = (HEADS + 2) * HD
-    pieces = len(weight_pieces)
+    fresh = -(-(done + slots) // KEYS) * KEYS
     whole = pl.BlockSpec(memory_space=pltpu.VMEM)
     remote = pl.BlockSpec(memory_space=pl.ANY)
+    scalars = pl.BlockSpec(memory_space=pltpu.SMEM)
     return pl.pallas_call(
-        functools.partial(project_kernel, pieces),
+        functools.partial(project_kernel, offsets, len(token_pieces), len(weight_pieces), done),
         out_shape=(
             jax.ShapeDtypeStruct((HEADS, slots, HD), jnp.bfloat16),
-            jax.ShapeDtypeStruct((slots, HD), jnp.bfloat16),
-            jax.ShapeDtypeStruct((HD, slots), jnp.bfloat16),
-        ),
-        in_specs=[pl.BlockSpec(memory_space=pltpu.SMEM), remote, whole, whole, whole]
-        + [remote] * pieces,
+            jax.ShapeDtypeStruct((fresh, HD), jnp.bfloat16),
+            jax.ShapeDtypeStruct((HD, fresh), jnp.bfloat16),
+        ),
+        in_specs=[scalars, scalars, whole, whole, whole, whole, whole]
+        + [remote] * (len(token_pieces) + len(weight_pieces)),
         out_specs=(whole, whole, whole),
         scratch_shapes=[
             pltpu.VMEM((blocks, slots, width), jnp.bfloat16),
             pltpu.VMEM((blocks * width, columns), jnp.bfloat16),
             pltpu.VMEM((slots, columns), jnp.float32),
             pltpu.VMEM((slots, HD), jnp.float32),
-            pltpu.SemaphoreType.DMA((blocks,)),
-            pltpu.SemaphoreType.DMA((pieces,)),
+            pltpu.SemaphoreType.DMA((token_places.shape[0],)),
+            pltpu.SemaphoreType.DMA((len(weight_pieces),)),
         ],
-        compiler_params=pltpu.CompilerParams(vmem_limit_bytes=58 * 2**20),
+        compiler_params=pltpu.CompilerParams(vmem_limit_bytes=48 * 2**20),
         cost_estimate=pl.CostEstimate(
-            flops=2 * slots * blocks * width * columns,
+            flops=4 * slots * blocks * width * columns,
             bytes_accessed=2 * blocks * width * (slots + columns),
             transcendentals=0,
         ),
         name="project",
-    )(places, tokens, gain, cosine, signed_sine, *weight_pieces)
+    )(token_places, weight_places, gain, cosine, signed_sine, *old, *token_pieces, *weight_pieces)
 
 
 def attend_kernel(
@@ -316,15 +332,59 @@
     )(key_blocks, queries, chosen, keys, values, places, fresh_keys, fresh_values, fresh_places)
 
 
+def ring(block, axis, shift):
+    half = block.shape[-2] // 2
+    behind = lax.ppermute(block, axis, shift(1))
+    ahead = lax.ppermute(block, axis, shift(-1))
+    far_first = lax.ppermute(behind[..., :half, :], axis, shift(1))
+    far_second = lax.ppermute(ahead[..., half:, :], axis, shift(-1))
+    return [block, behind, ahead, far_first, far_second]
+
+
+def stacked(pieces):
+    far = jnp.concatenate(pieces[3:], axis=-2)
+    return jnp.stack([*pieces[:3], far])
+
+
+def along_y(steps):
+    return col_shift(steps, 0)
+
+
+def along_z(steps):
+    return col_shift(0, steps)
+
+
+def gather_by_permutes(part, y_first):
+    col_index = lax.axis_index("col")
+    own_y, own_z = col_index // 4, col_index % 4
+    slots = part.shape[0]
+    cut = y_first * SLOTS
+    near = jnp.array([0, 3, 1, 2], jnp.int32)[None, :]
+    far = jnp.array([0, 3, 1, 2, 2], jnp.int32)[:, None]
+    over_y = stacked(ring(part[:cut], "col", along_y))
+    over_z = stacked(ring(part[cut:], "col", along_z))
+    pieces = ring(over_y, "col", along_z) + ring(over_z, "col", along_y)
+    first = (own_y + near) % 4 * 4 + (own_z + far) % 4
+    second = (own_y + far) % 4 * 4 + (own_z + near) % 4
+    places = jnp.concatenate([first.reshape(-1), second.reshape(-1)])
+    middle = cut + (slots - cut) // 2
+    offsets = (0, 0, 0, 0, cut // 2, cut, cut, cut, cut, middle)
+    return pieces, offsets, places
+
+
 def shards(tokens, norm_gain, w_query, w_keyval, kv_cache, selected, anchor):
     row_index = lax.axis_index("row")
     col_index = lax.axis_index("col")
     own_x, own_core = row_index // 2, row_index % 2
     holds_key = col_index % 2 == 0
     own_cache = kv_cache[0]
+    chosen = selected[0]
+    slot_count = chosen.shape[0]
+    early = EARLY * SLOTS
     other_keyval = lax.ppermute(w_keyval, "col", flipped(16))
+    late_tokens = lax.all_gather(tokens[0, early:], "col", axis=0)
+    early_pieces, offsets, early_places = gather_by_permutes(tokens[0, :early], Y_FIRST)
     other_cache = lax.ppermute(own_cache, "col", flipped(16))
-    gathered = lax.all_gather(tokens[0], "col", axis=0)
 
     weights = jnp.concatenate(
         [
@@ -334,28 +394,21 @@
         ],
         axis=1,
     )
-    half = weights.shape[0] // 2
-    behind = lax.ppermute(weights, "row", row_shift(1))
-    ahead = lax.ppermute(weights, "row", row_shift(-1))
-    far_first = lax.ppermute(behind[:half], "row", row_shift(1))
-    far_second = lax.ppermute(ahead[half:], "row", row_shift(-1))
-    mine = [weights, behind, ahead, far_first, far_second]
+    mine = ring(weights, "row", row_shift)
     theirs = [lax.ppermute(piece, "row", flipped(8)) for piece in mine]
     steps_x = jnp.array([0, 3, 1, 2, 2], jnp.int32)
     second_half = jnp.array([0, 0, 0, 0, 1], jnp.int32)
     source_x = (own_x + steps_x) % 4
-    places = jnp.concatenate(
+    weight_places = jnp.concatenate(
         [
             (source_x * 2 + own_core) * 2 + second_half,
             (source_x * 2 + 1 - own_core) * 2 + second_half,
         ]
     )
 
-    chosen = selected[0]
-    slot_count = chosen.shape[0]
     cosine, signed_sine = angles(chosen.astype(jnp.float32), HD)
-    offsets = jnp.arange(NCHUNK, dtype=jnp.int32) * SPAN - anchor[0]
-    span_cosine, span_sine = angles(offsets.astype(jnp.float32), HD)
+    span_starts = jnp.arange(NCHUNK, dtype=jnp.int32) * SPAN - anchor[0]
+    span_cosine, span_sine = angles(span_starts.astype(jnp.float32), HD)
     keys, values, key_places = prepare(
         holds_key.astype(jnp.int32)[None],
         own_cache,
@@ -372,17 +425,41 @@
         jnp.pad(chosen, (0, padded), constant_values=HIDDEN_POSITION)[:, None],
         (slot_count + padded, HD),
     )
-
     gain = norm_gain.reshape(NCHUNK, 1, -1)
-    queries, fresh_keys, fresh_values = project(
-        gathered, gain, cosine, signed_sine, mine + theirs, places
-    )
-    fresh_keys = jnp.pad(fresh_keys, ((0, padded), (0, 0)))
-    fresh_values = jnp.pad(fresh_values, ((0, 0), (0, padded)))
-    attended = attend(
-        0, key_blocks, queries, chosen[None], keys, values, key_places, fresh_keys, fresh_values, fresh_places
-    )
-    return attended[None]
+    nothing = (jnp.zeros((16, HD), jnp.bfloat16), jnp.zeros((16, HD), jnp.bfloat16))
+    absolute = jnp.arange(NCHUNK, dtype=jnp.int32)
+    results = []
+    fresh = nothing
+    for start, stop, pieces, piece_offsets, piece_places in (
+        (0, early, early_pieces, offsets, early_places),
+        (early, slot_count, [late_tokens], (0,), absolute),
+    ):
+        queries, *fresh = project(
+            pieces,
+            piece_offsets,
+            piece_places,
+            gain,
+            cosine[start:stop],
+            signed_sine[start:stop],
+            mine + theirs,
+            weight_places,
+            start,
+            fresh,
+        )
+        results.append(
+            attend(
+                start // SLOTS,
+                key_blocks[start // SLOTS : stop // SLOTS],
+                queries,
+                chosen[None, start:stop],
+                keys,
+                values,
+                key_places,
+                *fresh,
+                fresh_places,
+            )
+        )
+    return jnp.concatenate(results, axis=0)[None]
 
 
 def solution(mesh):

time: 266 us -> 316 us (1.19)
  the two profiles are of different devices: /device:TPU:23 before, /device:TPU:4 now
where the time goes in v2:
time: 316 us; the launch traced here: 312 us
  waiting for transfers between devices  123 us (39%)
  Pallas kernels  115 us (36%)
  starting transfers between devices  36.1 us (11%)
  local copies, waits for them, and re-layouts  15.8 us (5%)
  between operations  13.8 us (4%)
  other arithmetic  8.78 us (3%)
    pallas_call x2, Pallas kernels, attend(): pl.pallas_call(functools.partial(attend_kernel, first), out_shape=jax.Sha...  62.4 us
    ppermute x5, waiting for transfers between devices, ring(): behind = lax.ppermute(block, axis, shift(1))  42.9 us
    pallas_call x2, Pallas kernels, project(): pl.pallas_call(functools.partial(project_kernel, offsets, len(token_piece...  37.7 us
    ppermute x5, waiting for transfers between devices, ring(): ahead = lax.ppermute(block, axis, shift(-1))  32.1 us
    ppermute x5, waiting for transfers between devices, ring(): far_first = lax.ppermute(behind[..., :half, :], axis, shift(1))  29.9 us
    ppermute x5, waiting for transfers between devices, ring(): far_second = lax.ppermute(ahead[..., half:, :], axis, shift(-1))  17.8 us
    pallas_call x1, Pallas kernels, prepare(): pl.pallas_call(prepare_kernel, out_shape=(jax.ShapeDtypeStruct((LENGTH, H...  14.7 us
    ppermute x5, starting transfers between devices, ring(): far_second = lax.ppermute(ahead[..., half:, :], axis, shift(-1))  13 us
  transfers between devices with their start and end apart: 28, of which 13 were waited for; matrix products, arithmetic and copies ran while one was open for 5% of the time, Pallas kernels for 20%

profile of v2, /device:TPU:4, one launch (start us, length us, event | category | flops | bytes accessed | tf_op | source)
XLA Modules:
  0.0 312.1 jit_solution(1928700772760834996)
XLA Ops:
  6.5 2.0 slice.95
  8.6 3.1 collective-permute-start.1
  13.6 3.6 %collective-permute-done.1 = bf16[256,512]{1,0:T(8,128)(2,1)S(1)} collective-permute-done((bf16[256,512]{1,0:T(8,128)(2,1)S(1)}, bf16[256,512]{1,0:T(8,128)(2,1)S(1)}, u32[]{:S(2)}, u32[]{:S(2)}) %collective-permute-start.1) | collective-permute-done | bytes 262176 | tf_op jit(solution)/shard_map/ppermute | solution.py:338
  17.3 3.8 %collective-permute-start.3 = (bf16[128,512]{1,0:T(8,128)(2,1)S(1)}, bf16[128,512]{1,0:T(8,128)(2,1)S(1)}, u32[]{:S(2)}, u32[]{:S(2)}) collective-permute-start(bf16[128,512]{1,0:T(8,128)(2,1)S(1)} %slice.102), channel_id=1, source_target_pairs={{0,12},{1,13},{2,14},{3,15},{4,0},{5,1},{6,2},{7,3},{8,4},{9,5},{1... | collective-permute-start | bytes 393224 | tf_op jit(solution)/shard_map/ppermute | solution.py:340
  25.0 5.1 %collective-permute-done.2 = bf16[128,512]{1,0:T(8,128)(2,1)S(1)} collective-permute-done((bf16[128,512]{1,0:T(8,128)(2,1)S(1)}, bf16[128,512]{1,0:T(8,128)(2,1)S(1)}, u32[]{:S(2)}, u32[]{:S(2)}) %collective-permute-start.2) | collective-permute-done | bytes 131104 | tf_op jit(solution)/shard_map/ppermute | solution.py:339
  30.2 2.0 collective-permute-start.4
  32.3 1.9 collective-permute-start.9
  34.4 3.1 collective-permute-start.5
  37.5 8.2 %collective-permute-done.9 = bf16[384,512]{1,0:T(8,128)(2,1)S(1)} collective-permute-done((bf16[384,512]{1,0:T(8,128)(2,1)S(1)}, bf16[384,512]{1,0:T(8,128)(2,1)S(1)}, u32[]{:S(2)}, u32[]{:S(2)}) %collective-permute-start.9) | collective-permute-done | bytes 393248 | tf_op jit(solution)/shard_map/ppermute | solution.py:338
  45.7 3.3 %collective-permute-start.11 = (bf16[192,512]{1,0:T(8,128)(2,1)S(1)}, bf16[192,512]{1,0:T(8,128)(2,1)S(1)}, u32[]{:S(2)}, u32[]{:S(2)}) collective-permute-start(bf16[192,512]{1,0:T(8,128)(2,1)S(1)} %slice.106), channel_id=1, source_target_pairs={{0,3},{1,0},{2,1},{3,2},{4,7},{5,4},{6,5},{7,6},{8,11},{9,8},{10,9... | collective-permute-start | bytes 589832 | tf_op jit(solution)/shard_map/ppermute | solution.py:340
  49.0 34.6 %collective-permute-done.8 = bf16[384,512]{1,0:T(8,128)(2,1)S(1)} collective-permute-done((bf16[384,512]{1,0:T(8,128)(2,1)S(1)}, bf16[384,512]{1,0:T(8,128)(2,1)S(1)}, u32[]{:S(2)}, u32[]{:S(2)}) %collective-permute-start.8) | collective-permute-done | bytes 393248 | tf_op jit(solution)/shard_map/ppermute | solution.py:337
  83.7 7.5 %collective-permute-done.11 = bf16[192,512]{1,0:T(8,128)(2,1)S(1)} collective-permute-done((bf16[192,512]{1,0:T(8,128)(2,1)S(1)}, bf16[192,512]{1,0:T(8,128)(2,1)S(1)}, u32[]{:S(2)}, u32[]{:S(2)}) %collective-permute-start.11) | collective-permute-done | bytes 196640 | tf_op jit(solution)/shard_map/ppermute | solution.py:340
  91.7 3.1 collective-permute-done.10
  96.5 3.2 %collective-permute-start.13 = (bf16[4,384,512]{2,1,0:T(8,128)(2,1)}, bf16[4,384,512]{2,1,0:T(8,128)(2,1)}, u32[]{:S(2)}, u32[]{:S(2)}) collective-permute-start(bf16[4,384,512]{2,1,0:T(8,128)(2,1)} %pad_maximum_fusion.refs_12_), channel_id=1, source_target_pairs={{0,12},{1,13},{2,14},{3,15},{4,0},{5,1},{6,2},{7,3},{8,4},{9,5},{1... | collective-permute-start | bytes 4718600 | tf_op jit(solution)/shard_map/ppermute | solution.py:338
  99.8 20.2 %collective-permute-done.18.refs_19_.refs_10_ = bf16[1024,768]{1,0:T(8,128)(2,1)} collective-permute-done((bf16[1024,768]{1,0:T(8,128)(2,1)}, bf16[1024,768]{1,0:T(8,128)(2,1)}, u32[]{:S(2)}, u32[]{:S(2)}) %collective-permute-start.18) | collective-permute-done | bytes 1572896 | tf_op jit(solution)/shard_map/ppermute | solution.py:338
  120.0 4.0 %collective-permute-start.6 = (bf16[4,128,512]{2,1,0:T(8,128)(2,1)S(1)}, bf16[4,128,512]{2,1,0:T(8,128)(2,1)S(1)}, u32[]{:S(2)}, u32[]{:S(2)}) collective-permute-start(bf16[4,128,512]{2,1,0:T(8,128)(2,1)S(1)} %slice.103), channel_id=1, source_target_pairs={{0,1},{1,2},{2,3},{3,0},{4,5},{5,6},{6,7},{7,4},{8,9},{9,10},{10,1... | collective-permute-start | bytes 1572872 | tf_op jit(solution)/shard_map/ppermute | solution.py:339
  124.0 8.3 %collective-permute-done.12.refs_13_ = bf16[4,384,512]{2,1,0:T(8,128)(2,1)} collective-permute-done((bf16[4,384,512]{2,1,0:T(8,128)(2,1)}, bf16[4,384,512]{2,1,0:T(8,128)(2,1)}, u32[]{:S(2)}, u32[]{:S(2)}) %collective-permute-start.12) | collective-permute-done | bytes 1572896 | tf_op jit(solution)/shard_map/ppermute | solution.py:337
  132.3 2.4 collective-permute-start.7
  134.8 2.1 slice.109
  136.9 2.1 slice.110
  139.0 2.1 slice.107
  142.1 15.6 %collective-permute-done.6.refs_10_ = bf16[4,128,512]{2,1,0:T(8,128)(2,1)S(1)} collective-permute-done((bf16[4,128,512]{2,1,0:T(8,128)(2,1)S(1)}, bf16[4,128,512]{2,1,0:T(8,128)(2,1)S(1)}, u32[]{:S(2)}, u32[]{:S(2)}) %collective-permute-start.6) | collective-permute-done | bytes 524320 | tf_op jit(solution)/shard_map/ppermute | solution.py:339
  161.7 2.1 slice.108
  163.8 3.1 collective-permute-start.15
  167.0 8.3 %collective-permute-done.20.refs_21_.refs_12_ = bf16[512,768]{1,0:T(8,128)(2,1)S(1)} collective-permute-done((bf16[512,768]{1,0:T(8,128)(2,1)}, bf16[512,768]{1,0:T(8,128)(2,1)S(1)}, u32[]{:S(2)}, u32[]{:S(2)}) %collective-permute-start.20) | collective-permute-done | bytes 786464 | tf_op jit(solution)/shard_map/ppermute | solution.py:340
  175.3 6.2 %collective-permute-done.14.refs_15_ = bf16[4,192,512]{2,1,0:T(8,128)(2,1)} collective-permute-done((bf16[4,192,512]{2,1,0:T(8,128)(2,1)}, bf16[4,192,512]{2,1,0:T(8,128)(2,1)}, u32[]{:S(2)}, u32[]{:S(2)}) %collective-permute-start.14) | collective-permute-done | bytes 786464 | tf_op jit(solution)/shard_map/ppermute | solution.py:339
  181.6 2.1 fusion.2
  184.2 14.7 %prepare.1 = (bf16[8192,128]{1,0:T(8,128)(2,1)}, bf16[128,8192]{1,0:T(8,128)(2,1)}, s32[8192,128]{1,0:T(8,128)}) custom-call(s32[1]{0:T(128)} %bitcast.8.holds_key_ref, bf16[8192,128]{1,0:T(8,128)(2,1)} %bitcast.9.own_ref, bf16[8192,128]{1,0:T(8,128)(2,1)} %collective-permute-done.26.partner_ref, f32[16,1,128]{2,1,0:T(1,128)} %bitcast.32, ...), custom_call_target="tpu_custom_call" | custom-call | flops 10000000 | bytes 12582912 | tf_op jit(solution)/shard_map/prepare/pallas_call | solution.py:78
  200.0 20.2 %project.2 = (bf16[4,640,128]{2,1,0:T(8,128)(2,1)S(1)}, bf16[1024,128]{1,0:T(8,128)(2,1)S(1)}, bf16[128,1024]{1,0:T(8,128)(2,1)S(1)}) custom-call(s32[40]{0:T(128)S(1)} %pad_add_fusion.refs_0_, s32[10]{0:T(128)S(1)} %pad_add_fusion.1.refs_1_, bf16[16,1,512]{2,1,0:T(2,128)(2,1)S(1)} %reshape.76.refs_2_, f32[640,128]{1,0:T(8,128)S(1)} %get-tuple-element.44.refs_3_, ...), custom_call_target="tpu_custom_call" | custom-call | flops 16106127360 | bytes 23068672 | tf_op jit(solution)/shard_map/project/pallas_call | solution.py:183
  221.1 27.1 %attend.2 = bf16[640,512]{1,0:T(8,128)(2,1)S(1)} custom-call(s32[5]{0:T(128)S(1)} %bitcast.27, bf16[4,640,128]{2,1,0:T(8,128)(2,1)S(1)} %get-tuple-element.14.query_ref, s32[1,640]{1,0:T(1,128)S(1)} %slice.91.chosen_ref, bf16[8192,128]{1,0:T(8,128)(2,1)S(1)} %copy-done, bf16[128,8192]{1,0:T(8,128)(2,1)} %get-tuple-element.16.value_ref, ...), custom_call_target="tpu_custom_call" | custom-call | flops 5368709120 | bytes 12582912 | tf_op jit(solution)/shard_map/attend/pallas_call | solution.py:301
  251.3 17.5 %project.3 = (bf16[4,512,128]{2,1,0:T(8,128)(2,1)S(1)}, bf16[1536,128]{1,0:T(8,128)(2,1)S(1)}, bf16[128,1536]{1,0:T(8,128)(2,1)S(1)}) custom-call(s32[16]{0:T(128)S(1)} %iota.18.refs_0_, s32[10]{0:T(128)S(1)} %pad_add_fusion.1.refs_1_, bf16[16,1,512]{2,1,0:T(2,128)(2,1)S(1)} %reshape.76.refs_2_, f32[512,128]{1,0:T(8,128)S(1)} %get-tuple-element.46.refs_3_, ...), custom_call_target="tpu_custom_call" | custom-call | flops 12884901888 | bytes 20971520 | tf_op jit(solution)/shard_map/project/pallas_call | solution.py:183
  268.8 35.3 %attend.3 = bf16[512,512]{1,0:T(8,128)(2,1)S(1)} custom-call(s32[4]{0:T(128)S(1)} %slice.92.blocks_ref, bf16[4,512,128]{2,1,0:T(8,128)(2,1)S(1)} %get-tuple-element.20.query_ref, s32[1,512]{1,0:T(1,128)S(1)} %slice.96.chosen_ref, bf16[8192,128]{1,0:T(8,128)(2,1)S(1)} %copy-done.1, bf16[128,8192]{1,0:T(8,128)(2,1)} %get-tuple-element.16.value_ref, ...), custom_call_target="tpu_custom_call" | custom-call | flops 4294967296 | bytes 12582912 | tf_op jit(solution)/shard_map/attend/pallas_call | solution.py:301
  (121 shorter events, 20.3 us)
Async XLA Ops:
  6.5 241.7 %all-gather.2.cloned.1.call-start = ((), (), s32[]{:S(2)}) async-start(), calls=%async_computation | async-start | bytes 8912896 | tf_op jit(solution)/shard_map/all_gather | solution.py:385
  8.6 8.6 %collective-permute-start.1 = (bf16[256,512]{1,0:T(8,128)(2,1)S(1)}, bf16[256,512]{1,0:T(8,128)(2,1)S(1)}, u32[]{:S(2)}, u32[]{:S(2)}) collective-permute-start(bf16[256,512]{1,0:T(8,128)(2,1)S(1)} %get-tuple-element.28), channel_id=1, source_target_pairs={{0,12},{1,13},{2,14},{3,15},{4,0},{5,1},{6,2},{7,3},{8,4},{9,5},{1... | collective-permute-start | bytes 786440 | tf_op jit(solution)/shard_map/ppermute | solution.py:338
  11.7 9.3 %collective-permute-start = (bf16[256,512]{1,0:T(8,128)(2,1)S(1)}, bf16[256,512]{1,0:T(8,128)(2,1)S(1)}, u32[]{:S(2)}, u32[]{:S(2)}) collective-permute-start(bf16[256,512]{1,0:T(8,128)(2,1)S(1)} %get-tuple-element.28), channel_id=1, source_target_pairs={{0,4},{1,5},{2,6},{3,7},{4,8},{5,9},{6,10},{7,11},{8,12},{9,13},{1... | collective-permute-start | bytes 786440 | tf_op jit(solution)/shard_map/ppermute | solution.py:337
  11.7 9.4 %collective-permute-start.16 = (bf16[1024,128]{1,0:T(8,128)(2,1)S(1)}, bf16[1024,128]{1,0:T(8,128)(2,1)}, u32[]{:S(2)}, u32[]{:S(2)}) collective-permute-start(bf16[1024,128]{1,0:T(8,128)(2,1)S(1)} %copy-done.15), channel_id=1, source_target_pairs={{0,1},{1,0},{2,3},{3,2},{4,5},{5,4},{6,7},{7,6},{8,9},{9,8},{10,11... | collective-permute-start | bytes 786440 | tf_op jit(solution)/shard_map/ppermute | solution.py:384
  17.3 7.7 %collective-permute-start.3 = (bf16[128,512]{1,0:T(8,128)(2,1)S(1)}, bf16[128,512]{1,0:T(8,128)(2,1)S(1)}, u32[]{:S(2)}, u32[]{:S(2)}) collective-permute-start(bf16[128,512]{1,0:T(8,128)(2,1)S(1)} %slice.102), channel_id=1, source_target_pairs={{0,12},{1,13},{2,14},{3,15},{4,0},{5,1},{6,2},{7,3},{8,4},{9,5},{1... | collective-permute-start | bytes 393224 | tf_op jit(solution)/shard_map/ppermute | solution.py:340
  21.0 9.0 %collective-permute-start.2 = (bf16[128,512]{1,0:T(8,128)(2,1)S(1)}, bf16[128,512]{1,0:T(8,128)(2,1)S(1)}, u32[]{:S(2)}, u32[]{:S(2)}) collective-permute-start(bf16[128,512]{1,0:T(8,128)(2,1)S(1)} %slice.101), channel_id=1, source_target_pairs={{0,4},{1,5},{2,6},{3,7},{4,8},{5,9},{6,10},{7,11},{8,12},{9,13},{1... | collective-permute-start | bytes 393224 | tf_op jit(solution)/shard_map/ppermute | solution.py:339
  23.4 73.0 %collective-permute-start.17 = (bf16[1024,768]{1,0:T(8,128)(2,1)}, bf16[1024,768]{1,0:T(8,128)(2,1)}, u32[]{:S(2)}, u32[]{:S(2)}) collective-permute-start(bf16[1024,768]{1,0:T(8,128)(2,1)} %pad_maximum_fusion.1.refs_17_.refs_8_), channel_id=1, source_target_pairs={{0,32},{16,48},{32,64},{48,80},{64,96},{80,112},{96,0},{112,16},{1... | collective-permute-start | bytes 4718600 | tf_op jit(solution)/shard_map/ppermute | solution.py:337
  30.2 66.0 %copy-start.12 = (bf16[4,256,512]{2,1,0:T(8,128)(2,1)}, bf16[4,256,512]{2,1,0:T(8,128)(2,1)S(1)}, u32[]{:S(2)}) copy-start(bf16[4,256,512]{2,1,0:T(8,128)(2,1)S(1)} %pad_maximum_fusion.2.refs_7_) | copy-start | bytes 3145732
  30.2 66.0 %collective-permute-start.4 = (bf16[4,256,512]{2,1,0:T(8,128)(2,1)S(1)}, bf16[4,256,512]{2,1,0:T(8,128)(2,1)S(1)}, u32[]{:S(2)}, u32[]{:S(2)}) collective-permute-start(bf16[4,256,512]{2,1,0:T(8,128)(2,1)S(1)} %pad_maximum_fusion.2.refs_7_), channel_id=1, source_target_pairs={{0,1},{1,2},{2,3},{3,0},{4,5},{5,6},{6,7},{7,4},{8,9},{9,10},{10,1... | collective-permute-start | bytes 3145736 | tf_op jit(solution)/shard_map/ppermute | solution.py:337
  32.3 13.4 %collective-permute-start.9 = (bf16[384,512]{1,0:T(8,128)(2,1)S(1)}, bf16[384,512]{1,0:T(8,128)(2,1)S(1)}, u32[]{:S(2)}, u32[]{:S(2)}) collective-permute-start(bf16[384,512]{1,0:T(8,128)(2,1)S(1)} %get-tuple-element.26), channel_id=1, source_target_pairs={{0,3},{1,0},{2,1},{3,2},{4,7},{5,4},{6,5},{7,6},{8,11},{9,8},{10,9... | collective-permute-start | bytes 1179656 | tf_op jit(solution)/shard_map/ppermute | solution.py:338
  34.2 49.4 %collective-permute-start.8 = (bf16[384,512]{1,0:T(8,128)(2,1)S(1)}, bf16[384,512]{1,0:T(8,128)(2,1)S(1)}, u32[]{:S(2)}, u32[]{:S(2)}) collective-permute-start(bf16[384,512]{1,0:T(8,128)(2,1)S(1)} %get-tuple-element.26), channel_id=1, source_target_pairs={{0,1},{1,2},{2,3},{3,0},{4,5},{5,6},{6,7},{7,4},{8,9},{9,10},{10,1... | collective-permute-start | bytes 1179656 | tf_op jit(solution)/shard_map/ppermute | solution.py:337
  34.4 62.0 %collective-permute-start.5 = (bf16[4,256,512]{2,1,0:T(8,128)(2,1)S(1)}, bf16[4,256,512]{2,1,0:T(8,128)(2,1)S(1)}, u32[]{:S(2)}, u32[]{:S(2)}) collective-permute-start(bf16[4,256,512]{2,1,0:T(8,128)(2,1)S(1)} %pad_maximum_fusion.2.refs_7_), channel_id=1, source_target_pairs={{0,3},{1,0},{2,1},{3,2},{4,7},{5,4},{6,5},{7,6},{8,11},{9,8},{10,9... | collective-permute-start | bytes 3145736 | tf_op jit(solution)/shard_map/ppermute | solution.py:338
  45.7 45.4 %collective-permute-start.11 = (bf16[192,512]{1,0:T(8,128)(2,1)S(1)}, bf16[192,512]{1,0:T(8,128)(2,1)S(1)}, u32[]{:S(2)}, u32[]{:S(2)}) collective-permute-start(bf16[192,512]{1,0:T(8,128)(2,1)S(1)} %slice.106), channel_id=1, source_target_pairs={{0,3},{1,0},{2,1},{3,2},{4,7},{5,4},{6,5},{7,6},{8,11},{9,8},{10,9... | collective-permute-start | bytes 589832 | tf_op jit(solution)/shard_map/ppermute | solution.py:340
  83.6 11.1 %collective-permute-start.10 = (bf16[192,512]{1,0:T(8,128)(2,1)S(1)}, bf16[192,512]{1,0:T(8,128)(2,1)S(1)}, u32[]{:S(2)}, u32[]{:S(2)}) collective-permute-start(bf16[192,512]{1,0:T(8,128)(2,1)S(1)} %slice.105), channel_id=1, source_target_pairs={{0,1},{1,2},{2,3},{3,0},{4,5},{5,6},{6,7},{7,4},{8,9},{9,10},{10,1... | collective-permute-start | bytes 589832 | tf_op jit(solution)/shard_map/ppermute | solution.py:339
  91.2 28.8 %collective-permute-start.18 = (bf16[1024,768]{1,0:T(8,128)(2,1)}, bf16[1024,768]{1,0:T(8,128)(2,1)}, u32[]{:S(2)}, u32[]{:S(2)}) collective-permute-start(bf16[1024,768]{1,0:T(8,128)(2,1)} %pad_maximum_fusion.1.refs_17_.refs_8_), channel_id=1, source_target_pairs={{0,96},{16,112},{32,0},{48,16},{64,32},{80,48},{96,64},{112,80},{1... | collective-permute-start | bytes 4718600 | tf_op jit(solution)/shard_map/ppermute | solution.py:338
  96.2 38.5 %copy-start.19 = (s32[4]{0:T(128)S(1)}, s32[4]{0:T(128)}, u32[]{:S(2)}) copy-start(s32[4]{0:T(128)} %constant.129.clone) | copy-start | bytes 52
  96.2 36.1 %collective-permute-start.12 = (bf16[4,384,512]{2,1,0:T(8,128)(2,1)}, bf16[4,384,512]{2,1,0:T(8,128)(2,1)}, u32[]{:S(2)}, u32[]{:S(2)}) collective-permute-start(bf16[4,384,512]{2,1,0:T(8,128)(2,1)} %pad_maximum_fusion.refs_12_), channel_id=1, source_target_pairs={{0,4},{1,5},{2,6},{3,7},{4,8},{5,9},{6,10},{7,11},{8,12},{9,13},{1... | collective-permute-start | bytes 4718600 | tf_op jit(solution)/shard_map/ppermute | solution.py:337
  96.2 63.6 %collective-permute-start.26 = (bf16[8192,128]{1,0:T(8,128)(2,1)}, bf16[8192,128]{1,0:T(8,128)(2,1)}, u32[]{:S(2)}, u32[]{:S(2)}) collective-permute-start(bf16[8192,128]{1,0:T(8,128)(2,1)} %bitcast.9.own_ref), channel_id=1, source_target_pairs={{0,1},{1,0},{2,3},{3,2},{4,5},{5,4},{6,7},{7,6},{8,9},{9,8},{10,11... | collective-permute-start | bytes 6291464 | tf_op jit(solution)/shard_map/ppermute | solution.py:387
  96.4 40.6 %copy-start.14 = (bf16[4,256,512]{2,1,0:T(8,128)(2,1)}, bf16[4,256,512]{2,1,0:T(8,128)(2,1)S(1)}, u32[]{:S(2)}) copy-start(bf16[4,256,512]{2,1,0:T(8,128)(2,1)S(1)} %collective-permute-done.5.refs_9_) | copy-start | bytes 3145732
  96.4 44.8 %collective-permute-start.21 = (bf16[1024,768]{1,0:T(8,128)(2,1)}, bf16[1024,768]{1,0:T(8,128)(2,1)}, u32[]{:S(2)}, u32[]{:S(2)}) collective-permute-start(bf16[1024,768]{1,0:T(8,128)(2,1)} %pad_maximum_fusion.1.refs_17_.refs_8_), channel_id=1, source_target_pairs={{0,16},{16,0},{32,48},{48,32},{64,80},{80,64},{96,112},{112,96},{1... | collective-permute-start | bytes 4718600 | tf_op jit(solution)/shard_map/ppermute | solution.py:398
  96.5 63.9 %collective-permute-start.13 = (bf16[4,384,512]{2,1,0:T(8,128)(2,1)}, bf16[4,384,512]{2,1,0:T(8,128)(2,1)}, u32[]{:S(2)}, u32[]{:S(2)}) collective-permute-start(bf16[4,384,512]{2,1,0:T(8,128)(2,1)} %pad_maximum_fusion.refs_12_), channel_id=1, source_target_pairs={{0,12},{1,13},{2,14},{3,15},{4,0},{5,1},{6,2},{7,3},{8,4},{9,5},{1... | collective-permute-start | bytes 4718600 | tf_op jit(solution)/shard_map/ppermute | solution.py:338
  120.0 37.7 %collective-permute-start.6 = (bf16[4,128,512]{2,1,0:T(8,128)(2,1)S(1)}, bf16[4,128,512]{2,1,0:T(8,128)(2,1)S(1)}, u32[]{:S(2)}, u32[]{:S(2)}) collective-permute-start(bf16[4,128,512]{2,1,0:T(8,128)(2,1)S(1)} %slice.103), channel_id=1, source_target_pairs={{0,1},{1,2},{2,3},{3,0},{4,5},{5,6},{6,7},{7,4},{8,9},{9,10},{10,1... | collective-permute-start | bytes 1572872 | tf_op jit(solution)/shard_map/ppermute | solution.py:339
  132.3 27.6 %collective-permute-start.7 = (bf16[4,128,512]{2,1,0:T(8,128)(2,1)S(1)}, bf16[4,128,512]{2,1,0:T(8,128)(2,1)S(1)}, u32[]{:S(2)}, u32[]{:S(2)}) collective-permute-start(bf16[4,128,512]{2,1,0:T(8,128)(2,1)S(1)} %slice.104), channel_id=1, source_target_pairs={{0,3},{1,0},{2,1},{3,2},{4,7},{5,4},{6,5},{7,6},{8,11},{9,8},{10,9... | collective-permute-start | bytes 1572872 | tf_op jit(solution)/shard_map/ppermute | solution.py:340
  139.0 42.6 %copy-start.17 = (bf16[8192]{0:T(1024)(128)(2,1)S(1)}, bf16[8192]{0:T(1024)(128)(2,1)}, u32[]{:S(2)}) copy-start(bf16[8192]{0:T(1024)(128)(2,1)} %param.12) | copy-start | bytes 49156
  141.1 22.7 %collective-permute-start.19 = (bf16[512,768]{1,0:T(8,128)(2,1)}, bf16[512,768]{1,0:T(8,128)(2,1)S(1)}, u32[]{:S(2)}, u32[]{:S(2)}) collective-permute-start(bf16[512,768]{1,0:T(8,128)(2,1)} %slice.109), channel_id=1, source_target_pairs={{0,32},{16,48},{32,64},{48,80},{64,96},{80,112},{96,0},{112,16},{1... | collective-permute-start | bytes 2359304 | tf_op jit(solution)/shard_map/ppermute | solution.py:339
  157.7 17.6 %collective-permute-start.20 = (bf16[512,768]{1,0:T(8,128)(2,1)}, bf16[512,768]{1,0:T(8,128)(2,1)S(1)}, u32[]{:S(2)}, u32[]{:S(2)}) collective-permute-start(bf16[512,768]{1,0:T(8,128)(2,1)} %slice.110), channel_id=1, source_target_pairs={{0,96},{16,112},{32,0},{48,16},{64,32},{80,48},{96,64},{112,80},{1... | collective-permute-start | bytes 2359304 | tf_op jit(solution)/shard_map/ppermute | solution.py:340
  159.9 39.1 %collective-permute-start.22 = (bf16[1024,768]{1,0:T(8,128)(2,1)}, bf16[1024,768]{1,0:T(8,128)(2,1)}, u32[]{:S(2)}, u32[]{:S(2)}) collective-permute-start(bf16[1024,768]{1,0:T(8,128)(2,1)} %collective-permute-done.17.refs_18_.refs_9_), channel_id=1, source_target_pairs={{0,16},{16,0},{32,48},{48,32},{64,80},{80,64},{96,112},{112,96},{1... | collective-permute-start | bytes 4718600 | tf_op jit(solution)/shard_map/ppermute | solution.py:398
  159.9 39.1 %collective-permute-start.23 = (bf16[1024,768]{1,0:T(8,128)(2,1)}, bf16[1024,768]{1,0:T(8,128)(2,1)}, u32[]{:S(2)}, u32[]{:S(2)}) collective-permute-start(bf16[1024,768]{1,0:T(8,128)(2,1)} %collective-permute-done.18.refs_19_.refs_10_), channel_id=1, source_target_pairs={{0,16},{16,0},{32,48},{48,32},{64,80},{80,64},{96,112},{112,96},{1... | collective-permute-start | bytes 4718600 | tf_op jit(solution)/shard_map/ppermute | solution.py:398
  160.4 21.1 %collective-permute-start.14 = (bf16[4,192,512]{2,1,0:T(8,128)(2,1)}, bf16[4,192,512]{2,1,0:T(8,128)(2,1)}, u32[]{:S(2)}, u32[]{:S(2)}) collective-permute-start(bf16[4,192,512]{2,1,0:T(8,128)(2,1)} %slice.107), channel_id=1, source_target_pairs={{0,4},{1,5},{2,6},{3,7},{4,8},{5,9},{6,10},{7,11},{8,12},{9,13},{1... | collective-permute-start | bytes 2359304 | tf_op jit(solution)/shard_map/ppermute | solution.py:339
  163.8 35.1 %collective-permute-start.15 = (bf16[4,192,512]{2,1,0:T(8,128)(2,1)}, bf16[4,192,512]{2,1,0:T(8,128)(2,1)}, u32[]{:S(2)}, u32[]{:S(2)}) collective-permute-start(bf16[4,192,512]{2,1,0:T(8,128)(2,1)} %slice.108), channel_id=1, source_target_pairs={{0,12},{1,13},{2,14},{3,15},{4,0},{5,1},{6,2},{7,3},{8,4},{9,5},{1... | collective-permute-start | bytes 2359304 | tf_op jit(solution)/shard_map/ppermute | solution.py:340
  175.3 23.7 %collective-permute-start.24 = (bf16[512,768]{1,0:T(8,128)(2,1)S(1)}, bf16[512,768]{1,0:T(8,128)(2,1)}, u32[]{:S(2)}, u32[]{:S(2)}) collective-permute-start(bf16[512,768]{1,0:T(8,128)(2,1)S(1)} %collective-permute-done.19.refs_20_.refs_11_), channel_id=1, source_target_pairs={{0,16},{16,0},{32,48},{48,32},{64,80},{80,64},{96,112},{112,96},{1... | collective-permute-start | bytes 2359304 | tf_op jit(solution)/shard_map/ppermute | solution.py:398
  181.4 17.5 %collective-permute-start.25 = (bf16[512,768]{1,0:T(8,128)(2,1)S(1)}, bf16[512,768]{1,0:T(8,128)(2,1)}, u32[]{:S(2)}, u32[]{:S(2)}) collective-permute-start(bf16[512,768]{1,0:T(8,128)(2,1)S(1)} %collective-permute-done.20.refs_21_.refs_12_), channel_id=1, source_target_pairs={{0,16},{16,0},{32,48},{48,32},{64,80},{80,64},{96,112},{112,96},{1... | collective-permute-start | bytes 2359304 | tf_op jit(solution)/shard_map/ppermute | solution.py:398
  (18 other events, 178.7 us)
Sparse Core Ops, SparseCore 0:
  9.5 102.9 all-gather.1

commit v3 on v2

--- a/solution.py
+++ b/solution.py
@@ -16,8 +16,10 @@
 KEYS = 512
 SLOTS = 128
 HIDDEN_POSITION = 4 * LENGTH
-EARLY = 5
-Y_FIRST = 2
+EARLY = 6
+TILE = 64
+ROWS = 384
+GROUP = 4
 
 rope_base = 500000.0
 epsilon = 1e-05
@@ -123,38 +125,54 @@
         weight_copies.append(pltpu.make_async_copy(ref, where, weight_sem.at[piece]))
     for copy in token_copies + weight_copies:
         copy.start()
-    for copy in token_copies:
-        copy.wait()
     squares[...] = jnp.zeros_like(squares)
-
-    def add_squares(block, carry):
-        hidden = held[block].astype(jnp.float32)
-        hidden = hidden * hidden
-        part = hidden[:, :HD]
-        for start in range(HD, width, HD):
-            part = part + hidden[:, start : start + HD]
-        squares[...] += part
-        return carry
-
-    lax.fori_loop(0, blocks, add_squares, 0)
+    number = 0
+    for piece, ref in enumerate(token_refs):
+        for _ in range(ref.shape[0]):
+            token_copies[number].wait()
+            block = token_place_ref[number]
+            number += 1
+
+            def add_squares(tile, carry, block=block, offset=offsets[piece]):
+                rows = pl.ds(pl.multiple_of(offset + tile * TILE, TILE), TILE)
+                hidden = held[block, rows, :].astype(jnp.float32)
+                hidden = hidden * hidden
+                part = hidden[:, :HD]
+                for start in range(HD, width, HD):
+                    part = part + hidden[:, start : start + HD]
+                squares[rows, :] += part
+                return carry
+
+            lax.fori_loop(0, ref.shape[1] // TILE, add_squares, 0)
     mean_square = jnp.sum(squares[...], axis=1, keepdims=True) * (1.0 / (blocks * width))
     squares[...] = jnp.broadcast_to(lax.rsqrt(mean_square + epsilon), squares.shape)
     for copy in weight_copies:
         copy.wait()
+
+    def project_rows(tile, carry):
+        rows = pl.ds(pl.multiple_of(tile * ROWS, ROWS), ROWS)
+        scale = jnp.concatenate([squares[rows, :]] * (width // HD), axis=1)
+
+        def add_blocks(group, carry):
+            normed = []
+            for part in range(GROUP):
+                block = group * GROUP + part
+                hidden = held[block, rows, :].astype(jnp.float32) * scale
+                normed.append((hidden * gain_ref[block].astype(jnp.float32)).astype(jnp.bfloat16))
+            depth = GROUP * width
+            start = pl.multiple_of(group * depth, depth)
+            product = jnp.dot(
+                jnp.concatenate(normed, axis=1),
+                weights[pl.ds(start, depth), :],
+                preferred_element_type=jnp.float32,
+            )
+            total[rows, :] = jnp.where(group == 0, 0.0, total[rows, :]) + product
+            return carry
+
+        return lax.fori_loop(0, blocks // GROUP, add_blocks, carry)
+
     total[...] = jnp.zeros_like(total)
-
-    def add_block(block, carry):
-        start = pl.multiple_of(block * width, width)
-        scale = jnp.concatenate([squares[...]] * (width // HD), axis=1)
-        hidden = held[block].astype(jnp.float32) * scale * gain_ref[block].astype(jnp.float32)
-        total[...] += jnp.dot(
-            hidden.astype(jnp.bfloat16),
-            weights[pl.ds(start, width), :],
-            preferred_element_type=jnp.float32,
-        )
-        return carry
-
-    lax.fori_loop(0, blocks, add_block, 0)
+    lax.fori_loop(0, slots // ROWS, project_rows, 0)
     cosine, signed_sine = cosine_ref[...], sine_ref[...]
     for head in range(HEADS):
         part = total[:, head * HD : (head + 1) * HD]
@@ -341,37 +359,6 @@
     return [block, behind, ahead, far_first, far_second]
 
 
-def stacked(pieces):
-    far = jnp.concatenate(pieces[3:], axis=-2)
-    return jnp.stack([*pieces[:3], far])
-
-
-def along_y(steps):
-    return col_shift(steps, 0)
-
-
-def along_z(steps):
-    return col_shift(0, steps)
-
-
-def gather_by_permutes(part, y_first):
-    col_index = lax.axis_index("col")
-    own_y, own_z = col_index // 4, col_index % 4
-    slots = part.shape[0]
-    cut = y_first * SLOTS
-    near = jnp.array([0, 3, 1, 2], jnp.int32)[None, :]
-    far = jnp.array([0, 3, 1, 2, 2], jnp.int32)[:, None]
-    over_y = stacked(ring(part[:cut], "col", along_y))
-    over_z = stacked(ring(part[cut:], "col", along_z))
-    pieces = ring(over_y, "col", along_z) + ring(over_z, "col", along_y)
-    first = (own_y + near) % 4 * 4 + (own_z + far) % 4
-    second = (own_y + far) % 4 * 4 + (own_z + near) % 4
-    places = jnp.concatenate([first.reshape(-1), second.reshape(-1)])
-    middle = cut + (slots - cut) // 2
-    offsets = (0, 0, 0, 0, cut // 2, cut, cut, cut, cut, middle)
-    return pieces, offsets, places
-
-
 def shards(tokens, norm_gain, w_query, w_keyval, kv_cache, selected, anchor):
     row_index = lax.axis_index("row")
     col_index = lax.axis_index("col")
@@ -382,8 +369,9 @@
     slot_count = chosen.shape[0]
     early = EARLY * SLOTS
     other_keyval = lax.ppermute(w_keyval, "col", flipped(16))
-    late_tokens = lax.all_gather(tokens[0, early:], "col", axis=0)
-    early_pieces, offsets, early_places = gather_by_permutes(tokens[0, :early], Y_FIRST)
+    early_tokens = lax.all_gather(tokens[0, :early], "col", axis=0)
+    late_tokens, other_keyval = lax.optimization_barrier((tokens[0, early:], other_keyval))
+    late_tokens = lax.all_gather(late_tokens, "col", axis=0)
     other_cache = lax.ppermute(own_cache, "col", flipped(16))
 
     weights = jnp.concatenate(
@@ -431,7 +419,7 @@
     results = []
     fresh = nothing
     for start, stop, pieces, piece_offsets, piece_places in (
-        (0, early, early_pieces, offsets, early_places),
+        (0, early, [early_tokens], (0,), absolute),
         (early, slot_count, [late_tokens], (0,), absolute),
     ):
         queries, *fresh = project(

time: 316 us -> 245 us (0.78)
  the two profiles are of different devices: /device:TPU:4 before, /device:TPU:5 now
where the time goes in v3:
time: 245 us; the launch traced here: 244 us
  Pallas kernels  111 us (45%)
  waiting for transfers between devices  89.1 us (36%)
  starting transfers between devices  16.5 us (7%)
  between operations  13.7 us (6%)
  local copies, waits for them, and re-layouts  8.68 us (4%)
  other arithmetic  4.89 us (2%)
    pallas_call x2, Pallas kernels, attend(): pl.pallas_call(functools.partial(attend_kernel, first), out_shape=jax.Sha...  63 us
    pallas_call x2, Pallas kernels, project(): pl.pallas_call(functools.partial(project_kernel, offsets, len(token_piece...  33.5 us
    ppermute x1, waiting for transfers between devices, ring(): behind = lax.ppermute(block, axis, shift(1))  31.9 us
    ppermute x1, waiting for transfers between devices, shards(): other_cache = lax.ppermute(own_cache, 'col', flipped(16))  28.4 us
    all_gather x1, waiting for transfers between devices, shards(): early_tokens = lax.all_gather(tokens[0, :early], 'col', axis=0)  15.4 us
    pallas_call x1, Pallas kernels, prepare(): pl.pallas_call(prepare_kernel, out_shape=(jax.ShapeDtypeStruct((LENGTH, H...  14.9 us
    ppermute x5, starting transfers between devices, shards(): theirs = [lax.ppermute(piece, 'row', flipped(8)) for piece in mine]  10.3 us
    all_gather x1, waiting for transfers between devices, shards(): late_tokens = lax.all_gather(late_tokens, 'col', axis=0)  9.29 us
  transfers between devices with their start and end apart: 13, of which 5 were waited for; matrix products, arithmetic and copies ran while one was open for 3% of the time, Pallas kernels for 28%

profile of v3, /device:TPU:5, one launch (start us, length us, event | category | flops | bytes accessed | tf_op | source)
XLA Modules:
  0.0 244.3 jit_solution(16671923212728925376)
XLA Ops:
  6.5 2.1 slice.41
  8.7 1.7 collective-permute-start
  10.4 1.8 slice_bitcast_fusion
  12.2 4.1 %collective-permute-done = bf16[1024,128]{1,0:T(8,128)(2,1)S(1)} collective-permute-done((bf16[1024,128]{1,0:T(8,128)(2,1)S(1)}, bf16[1024,128]{1,0:T(8,128)(2,1)S(1)}, u32[]{:S(2)}, u32[]{:S(2)}) %collective-permute-start) | collective-permute-done | bytes 262176 | tf_op jit(solution)/shard_map/ppermute | solution.py:371
  16.4 1.3 collective-permute-start.10
  17.8 0.1 pad_maximum_fusion.refs_8_
  17.9 1.0 collective-permute-start.1
  18.9 0.5 collective-permute-start.2
  19.5 0.1 fusion.4
  19.6 0.7 pad_maximum_fusion.3
  20.3 31.9 %collective-permute-done.1.refs_9_ = bf16[1024,768]{1,0:T(8,128)(2,1)S(1)} collective-permute-done((bf16[1024,768]{1,0:T(8,128)(2,1)S(1)}, bf16[1024,768]{1,0:T(8,128)(2,1)S(1)}, u32[]{:S(2)}, u32[]{:S(2)}) %collective-permute-start.1) | collective-permute-done | bytes 1572896 | tf_op jit(solution)/shard_map/ppermute | solution.py:355
  52.2 1.0 collective-permute-start.3
  53.2 2.1 slice.55
  55.3 0.5 collective-permute-start.4
  55.9 3.3 %collective-permute-start.5 = (bf16[1024,768]{1,0:T(8,128)(2,1)}, bf16[1024,768]{1,0:T(8,128)(2,1)}, u32[]{:S(2)}, u32[]{:S(2)}) collective-permute-start(bf16[1024,768]{1,0:T(8,128)(2,1)} %copy-done.5), channel_id=1, source_target_pairs={{0,16},{16,0},{32,48},{48,32},{64,80},{80,64},{96,112},{112,96},{1... | collective-permute-start | bytes 4718600 | tf_op jit(solution)/shard_map/ppermute | solution.py:386
  59.3 28.4 %collective-permute-done.10.partner_ref = bf16[8192,128]{1,0:T(8,128)(2,1)} collective-permute-done((bf16[8192,128]{1,0:T(8,128)(2,1)}, bf16[8192,128]{1,0:T(8,128)(2,1)}, u32[]{:S(2)}, u32[]{:S(2)}) %collective-permute-start.10) | collective-permute-done | bytes 2097184 | tf_op jit(solution)/shard_map/ppermute | solution.py:375
  87.6 6.4 %collective-permute-start.7 = (bf16[1024,768]{1,0:T(8,128)(2,1)}, bf16[1024,768]{1,0:T(8,128)(2,1)}, u32[]{:S(2)}, u32[]{:S(2)}) collective-permute-start(bf16[1024,768]{1,0:T(8,128)(2,1)} %collective-permute-done.2.refs_10_), channel_id=1, source_target_pairs={{0,16},{16,0},{32,48},{48,32},{64,80},{80,64},{96,112},{112,96},{1... | collective-permute-start | bytes 4718600 | tf_op jit(solution)/shard_map/ppermute | solution.py:386
  94.3 0.5 collective-permute-start.9
  95.0 2.1 fusion.2
  97.1 0.2 pad_maximum_fusion.1
  97.3 0.3 fusion
  97.6 14.9 %prepare.1 = (bf16[8192,128]{1,0:T(8,128)(2,1)}, bf16[128,8192]{1,0:T(8,128)(2,1)}, s32[8192,128]{1,0:T(8,128)}) custom-call(s32[1]{0:T(128)} %bitcast.1.holds_key_ref, bf16[8192,128]{1,0:T(8,128)(2,1)} %bitcast.2.own_ref, bf16[8192,128]{1,0:T(8,128)(2,1)} %collective-permute-done.10.partner_ref, f32[16,1,128]{2,1,0:T(1,128)} %bitcast.19, ...), custom_call_target="tpu_custom_call" | custom-call | flops 10000000 | bytes 12582912 | tf_op jit(solution)/shard_map/prepare/pallas_call | solution.py:80
  112.6 15.4 %all-gather.4.cloned.1.call-done.refs_7_ = bf16[16,768,512]{2,1,0:T(8,128)(2,1)} async-done(((bf16[1,768,512]{2,1,0:T(8,128)(2,1)}), bf16[16,768,512]{2,1,0:T(8,128)(2,1)}) %all-gather.4.cloned.1.call-update) | async-done | bytes 12582928 | tf_op jit(solution)/shard_map/all_gather | solution.py:372
  128.0 1.1 copy-done.3
  129.1 20.6 %project.2 = (bf16[4,768,128]{2,1,0:T(8,128)(2,1)S(1)}, bf16[1024,128]{1,0:T(8,128)(2,1)S(1)}, bf16[128,1024]{1,0:T(8,128)(2,1)S(1)}) custom-call(s32[16]{0:T(128)S(1)} %iota.18.refs_0_, s32[10]{0:T(128)S(1)} %pad_add_fusion.refs_1_, bf16[16,1,512]{2,1,0:T(2,128)(2,1)S(1)} %reshape.31.refs_2_, f32[768,128]{1,0:T(8,128)S(1)} %get-tuple-element.38.refs_3_, ...), custom_call_target="tpu_custom_call" | custom-call | flops 19327352832 | bytes 25165824 | tf_op jit(solution)/shard_map/project/pallas_call | solution.py:201
  149.7 0.3 broadcast_in_dim.35.fresh_place_ref
  150.0 34.1 %attend.2 = bf16[768,512]{1,0:T(8,128)(2,1)S(1)} custom-call(s32[6]{0:T(128)S(1)} %bitcast.18, bf16[4,768,128]{2,1,0:T(8,128)(2,1)S(1)} %get-tuple-element.17.query_ref, s32[1,768]{1,0:T(1,128)S(1)} %slice.45.chosen_ref, bf16[8192,128]{1,0:T(8,128)(2,1)S(1)} %copy-done, bf16[128,8192]{1,0:T(8,128)(2,1)} %get-tuple-element.19.value_ref, ...), custom_call_target="tpu_custom_call" | custom-call | flops 6442450944 | bytes 12582912 | tf_op jit(solution)/shard_map/attend/pallas_call | solution.py:319
  184.1 9.3 %all-gather.6.cloned.1.call-done = bf16[6144,512]{1,0:T(8,128)(2,1)} async-done(((bf16[384,512]{1,0:T(8,128)(2,1)}), bf16[6144,512]{1,0:T(8,128)(2,1)}) %all-gather.6.cloned.1.call-update) | async-done | bytes 6291472 | tf_op jit(solution)/shard_map/all_gather | solution.py:374
  193.4 1.1 copy-done.4
  194.5 12.9 %project.3 = (bf16[4,384,128]{2,1,0:T(8,128)(2,1)S(1)}, bf16[1536,128]{1,0:T(8,128)(2,1)S(1)}, bf16[128,1536]{1,0:T(8,128)(2,1)S(1)}) custom-call(s32[16]{0:T(128)S(1)} %iota.21.refs_0_, s32[10]{0:T(128)S(1)} %pad_add_fusion.refs_1_, bf16[16,1,512]{2,1,0:T(2,128)(2,1)S(1)} %reshape.31.refs_2_, f32[384,128]{1,0:T(8,128)S(1)} %get-tuple-element.40.refs_3_, ...), custom_call_target="tpu_custom_call" | custom-call | flops 9663676416 | bytes 18874368 | tf_op jit(solution)/shard_map/project/pallas_call | solution.py:201
  207.4 29.0 %attend.3 = bf16[384,512]{1,0:T(8,128)(2,1)S(1)} custom-call(s32[3]{0:T(128)S(1)} %slice.46.blocks_ref, bf16[4,384,128]{2,1,0:T(8,128)(2,1)S(1)} %get-tuple-element.24.query_ref, s32[1,384]{1,0:T(1,128)S(1)} %slice.49.chosen_ref, bf16[8192,128]{1,0:T(8,128)(2,1)S(1)} %copy-done.1, bf16[128,8192]{1,0:T(8,128)(2,1)} %get-tuple-element.19.value_ref, ...), custom_call_target="tpu_custom_call" | custom-call | flops 3221225472 | bytes 12582912 | tf_op jit(solution)/shard_map/attend/pallas_call | solution.py:319
  236.4 1.1 maximum_bitcast_fusion
  (59 shorter events, 0.8 us)
Async XLA Ops:
  6.5 2.2 copy-start.8
  6.5 121.4 %all-gather.4.cloned.1.call-start = ((), (), s32[]{:S(2)}) async-start(), calls=%async_computation | async-start | bytes 13369344 | tf_op jit(solution)/shard_map/all_gather | solution.py:372
  8.6 9.1 %copy-start.6 = (bf16[1024,512]{1,0:T(8,128)(2,1)S(1)}, bf16[1024,512]{1,0:T(8,128)(2,1)}, u32[]{:S(2)}) copy-start(bf16[1024,512]{1,0:T(8,128)(2,1)} %param.11) | copy-start | bytes 3145732
  8.7 184.7 %all-gather.6.cloned.1.call-start = ((), (), s32[]{:S(2)}) async-start(), calls=%async_computation.1 | async-start | bytes 6684672 | tf_op jit(solution)/shard_map/all_gather | solution.py:374
  8.7 7.6 %collective-permute-start = (bf16[1024,128]{1,0:T(8,128)(2,1)S(1)}, bf16[1024,128]{1,0:T(8,128)(2,1)S(1)}, u32[]{:S(2)}, u32[]{:S(2)}) collective-permute-start(bf16[1024,128]{1,0:T(8,128)(2,1)S(1)} %copy-done.8), channel_id=1, source_target_pairs={{0,1},{1,0},{2,3},{3,2},{4,5},{5,4},{6,7},{7,6},{8,9},{9,8},{10,11... | collective-permute-start | bytes 786440 | tf_op jit(solution)/shard_map/ppermute | solution.py:371
  16.4 71.3 %collective-permute-start.10 = (bf16[8192,128]{1,0:T(8,128)(2,1)}, bf16[8192,128]{1,0:T(8,128)(2,1)}, u32[]{:S(2)}, u32[]{:S(2)}) collective-permute-start(bf16[8192,128]{1,0:T(8,128)(2,1)} %bitcast.2.own_ref), channel_id=1, source_target_pairs={{0,1},{1,0},{2,3},{3,2},{4,5},{5,4},{6,7},{7,6},{8,9},{9,8},{10,11... | collective-permute-start | bytes 6291464 | tf_op jit(solution)/shard_map/ppermute | solution.py:375
  17.8 1.7 copy-start.13
  17.9 35.3 %copy-start.5 = (bf16[1024,768]{1,0:T(8,128)(2,1)}, bf16[1024,768]{1,0:T(8,128)(2,1)S(1)}, u32[]{:S(2)}) copy-start(bf16[1024,768]{1,0:T(8,128)(2,1)S(1)} %pad_maximum_fusion.refs_8_) | copy-start | bytes 4718596
  17.9 34.2 %collective-permute-start.1 = (bf16[1024,768]{1,0:T(8,128)(2,1)S(1)}, bf16[1024,768]{1,0:T(8,128)(2,1)S(1)}, u32[]{:S(2)}, u32[]{:S(2)}) collective-permute-start(bf16[1024,768]{1,0:T(8,128)(2,1)S(1)} %pad_maximum_fusion.refs_8_), channel_id=1, source_target_pairs={{0,32},{16,48},{32,64},{48,80},{64,96},{80,112},{96,0},{112,16},{1... | collective-permute-start | bytes 4718600 | tf_op jit(solution)/shard_map/ppermute | solution.py:355
  18.9 34.3 %collective-permute-start.2 = (bf16[1024,768]{1,0:T(8,128)(2,1)S(1)}, bf16[1024,768]{1,0:T(8,128)(2,1)}, u32[]{:S(2)}, u32[]{:S(2)}) collective-permute-start(bf16[1024,768]{1,0:T(8,128)(2,1)S(1)} %pad_maximum_fusion.refs_8_), channel_id=1, source_target_pairs={{0,96},{16,112},{32,0},{48,16},{64,32},{80,48},{96,64},{112,80},{1... | collective-permute-start | bytes 4718600 | tf_op jit(solution)/shard_map/ppermute | solution.py:356
  20.3 35.6 %copy-start.9 = (s32[1,1152]{1,0:T(1,128)S(1)}, s32[1,1152]{1,0:T(1,128)}, u32[]{:S(2)}) copy-start(s32[1,1152]{1,0:T(1,128)} %chosen_ref.1) | copy-start | bytes 13828
  20.3 73.8 %copy-start.11 = (s32[5]{0:T(128)S(1)}, s32[5]{0:T(128)}, u32[]{:S(2)}) copy-start(s32[5]{0:T(128)} %constant.88.clone) | copy-start | bytes 64
  20.3 73.8 %copy-start.12 = (s32[5]{0:T(128)S(1)}, s32[5]{0:T(128)}, u32[]{:S(2)}) copy-start(s32[5]{0:T(128)} %constant.87.clone) | copy-start | bytes 64
  20.3 74.6 %copy-start.10 = (bf16[8192]{0:T(1024)(128)(2,1)S(1)}, bf16[8192]{0:T(1024)(128)(2,1)}, u32[]{:S(2)}) copy-start(bf16[8192]{0:T(1024)(128)(2,1)} %param.10) | copy-start | bytes 49156
  52.2 3.1 %copy-start.7 = (bf16[1024,768]{1,0:T(8,128)(2,1)}, bf16[1024,768]{1,0:T(8,128)(2,1)S(1)}, u32[]{:S(2)}) copy-start(bf16[1024,768]{1,0:T(8,128)(2,1)S(1)} %collective-permute-done.1.refs_9_) | copy-start | bytes 4718596
  52.2 42.0 %collective-permute-start.3 = (bf16[512,768]{1,0:T(8,128)(2,1)S(1)}, bf16[512,768]{1,0:T(8,128)(2,1)S(1)}, u32[]{:S(2)}, u32[]{:S(2)}) collective-permute-start(bf16[512,768]{1,0:T(8,128)(2,1)S(1)} %slice.54), channel_id=1, source_target_pairs={{0,32},{16,48},{32,64},{48,80},{64,96},{80,112},{96,0},{112,16},{1... | collective-permute-start | bytes 2359304 | tf_op jit(solution)/shard_map/ppermute | solution.py:357
  55.3 39.0 %collective-permute-start.4 = (bf16[512,768]{1,0:T(8,128)(2,1)}, bf16[512,768]{1,0:T(8,128)(2,1)S(1)}, u32[]{:S(2)}, u32[]{:S(2)}) collective-permute-start(bf16[512,768]{1,0:T(8,128)(2,1)} %slice.55), channel_id=1, source_target_pairs={{0,96},{16,112},{32,0},{48,16},{64,32},{80,48},{96,64},{112,80},{1... | collective-permute-start | bytes 2359304 | tf_op jit(solution)/shard_map/ppermute | solution.py:358
  55.9 56.6 %collective-permute-start.5 = (bf16[1024,768]{1,0:T(8,128)(2,1)}, bf16[1024,768]{1,0:T(8,128)(2,1)}, u32[]{:S(2)}, u32[]{:S(2)}) collective-permute-start(bf16[1024,768]{1,0:T(8,128)(2,1)} %copy-done.5), channel_id=1, source_target_pairs={{0,16},{16,0},{32,48},{48,32},{64,80},{80,64},{96,112},{112,96},{1... | collective-permute-start | bytes 4718600 | tf_op jit(solution)/shard_map/ppermute | solution.py:386
  59.2 53.4 %collective-permute-start.6 = (bf16[1024,768]{1,0:T(8,128)(2,1)}, bf16[1024,768]{1,0:T(8,128)(2,1)}, u32[]{:S(2)}, u32[]{:S(2)}) collective-permute-start(bf16[1024,768]{1,0:T(8,128)(2,1)} %copy-done.7), channel_id=1, source_target_pairs={{0,16},{16,0},{32,48},{48,32},{64,80},{80,64},{96,112},{112,96},{1... | collective-permute-start | bytes 4718600 | tf_op jit(solution)/shard_map/ppermute | solution.py:386
  87.6 24.9 %collective-permute-start.7 = (bf16[1024,768]{1,0:T(8,128)(2,1)}, bf16[1024,768]{1,0:T(8,128)(2,1)}, u32[]{:S(2)}, u32[]{:S(2)}) collective-permute-start(bf16[1024,768]{1,0:T(8,128)(2,1)} %collective-permute-done.2.refs_10_), channel_id=1, source_target_pairs={{0,16},{16,0},{32,48},{48,32},{64,80},{80,64},{96,112},{112,96},{1... | collective-permute-start | bytes 4718600 | tf_op jit(solution)/shard_map/ppermute | solution.py:386
  94.2 18.3 %collective-permute-start.8 = (bf16[512,768]{1,0:T(8,128)(2,1)S(1)}, bf16[512,768]{1,0:T(8,128)(2,1)}, u32[]{:S(2)}, u32[]{:S(2)}) collective-permute-start(bf16[512,768]{1,0:T(8,128)(2,1)S(1)} %collective-permute-done.3.refs_11_), channel_id=1, source_target_pairs={{0,16},{16,0},{32,48},{48,32},{64,80},{80,64},{96,112},{112,96},{1... | collective-permute-start | bytes 2359304 | tf_op jit(solution)/shard_map/ppermute | solution.py:386
  94.3 3.0 %copy-start.2 = (bf16[512,768]{1,0:T(8,128)(2,1)}, bf16[512,768]{1,0:T(8,128)(2,1)S(1)}, u32[]{:S(2)}) copy-start(bf16[512,768]{1,0:T(8,128)(2,1)S(1)} %collective-permute-done.4.refs_12_) | copy-start | bytes 2359300
  94.3 18.2 %collective-permute-start.9 = (bf16[512,768]{1,0:T(8,128)(2,1)S(1)}, bf16[512,768]{1,0:T(8,128)(2,1)}, u32[]{:S(2)}, u32[]{:S(2)}) collective-permute-start(bf16[512,768]{1,0:T(8,128)(2,1)S(1)} %collective-permute-done.4.refs_12_), channel_id=1, source_target_pairs={{0,16},{16,0},{32,48},{48,32},{64,80},{80,64},{96,112},{112,96},{1... | collective-permute-start | bytes 2359304 | tf_op jit(solution)/shard_map/ppermute | solution.py:386
  128.0 1.1 copy-start.3
  129.1 20.9 %copy-start = (bf16[8192,128]{1,0:T(8,128)(2,1)S(1)}, bf16[8192,128]{1,0:T(8,128)(2,1)}, u32[]{:S(2)}) copy-start(bf16[8192,128]{1,0:T(8,128)(2,1)} %get-tuple-element.18.key_ref) | copy-start | bytes 6291460
  193.4 1.1 copy-start.4
  194.5 12.9 %copy-start.1 = (bf16[8192,128]{1,0:T(8,128)(2,1)S(1)}, bf16[8192,128]{1,0:T(8,128)(2,1)}, u32[]{:S(2)}) copy-start(bf16[8192,128]{1,0:T(8,128)(2,1)} %get-tuple-element.18.key_ref) | copy-start | bytes 6291460
Sparse Core Ops, SparseCore 0:
  9.5 118.3 all-gather.3
  130.2 63.1 all-gather.5

commit v4 on v3

--- a/solution.py
+++ b/solution.py
@@ -17,6 +17,7 @@
 SLOTS = 128
 HIDDEN_POSITION = 4 * LENGTH
 EARLY = 6
+NEAR = 12
 TILE = 64
 ROWS = 384
 GROUP = 4
@@ -55,10 +56,9 @@
     return vectors * cosine + pltpu.roll(vectors, HD // 2, 1) * signed_sine
 
 
-def prepare_kernel(
-    holds_key_ref, own_ref, partner_ref, cosine_ref, sine_ref, chosen_ref, key_ref, value_ref, place_ref
-):
-    step = pl.program_id(0)
+def prepare_kernel(first, holds_key_ref, own_ref, partner_ref, cosine_ref, sine_ref, chosen_ref, *refs):
+    key_ref, value_ref, place_ref = refs[-3:]
+    step = first + pl.program_id(0)
     holds_key = holds_key_ref[0] == 1
     own = own_ref[...]
     partner = partner_ref[...]
@@ -74,11 +74,11 @@
     place_ref[...] = jnp.where(replaced, HIDDEN_POSITION, place)
 
 
-def prepare(holds_key, own, partner, cosine, signed_sine, chosen):
-    block = pl.BlockSpec((SPAN, HD), lambda step, flag: (step, 0))
-    angle = pl.BlockSpec((1, 1, HD), lambda step, flag: (step, 0, 0))
+def prepare(first, holds_key, own, partner, cosine, signed_sine, chosen, earlier):
+    block = pl.BlockSpec((SPAN, HD), lambda step, flag: (first + step, 0))
+    angle = pl.BlockSpec((1, 1, HD), lambda step, flag: (first + step, 0, 0))
     return pl.pallas_call(
-        prepare_kernel,
+        functools.partial(prepare_kernel, first),
         out_shape=(
             jax.ShapeDtypeStruct((LENGTH, HD), jnp.bfloat16),
             jax.ShapeDtypeStruct((HD, LENGTH), jnp.bfloat16),
@@ -86,23 +86,25 @@
         ),
         grid_spec=pltpu.PrefetchScalarGridSpec(
             num_scalar_prefetch=1,
-            grid=(NCHUNK,),
+            grid=(partner.shape[0] // SPAN,),
             in_specs=[
                 block,
-                block,
+                pl.BlockSpec((SPAN, HD), lambda step, flag: (step, 0)),
                 angle,
                 angle,
                 pl.BlockSpec((1, chosen.shape[1]), lambda step, flag: (0, 0)),
-            ],
+            ]
+            + [pl.BlockSpec(memory_space=pl.ANY)] * len(earlier),
             out_specs=(
                 block,
-                pl.BlockSpec((HD, SPAN), lambda step, flag: (0, step)),
+                pl.BlockSpec((HD, SPAN), lambda step, flag: (0, first + step)),
                 block,
             ),
         ),
-        cost_estimate=pl.CostEstimate(flops=10**7, bytes_accessed=12 * 2**20, transcendentals=0),
+        input_output_aliases={6 + number: number for number in range(len(earlier))},
+        cost_estimate=pl.CostEstimate(flops=10**7, bytes_accessed=6 * 2**20, transcendentals=0),
         name="prepare",
-    )(holds_key, own, partner, cosine, signed_sine, chosen)
+    )(holds_key, own, partner, cosine, signed_sine, chosen, *earlier)
 
 
 def project_kernel(offsets, token_count, weight_count, done, *refs):
@@ -149,8 +151,10 @@
     for copy in weight_copies:
         copy.wait()
 
+    height = slots // max(1, slots // ROWS)
+
     def project_rows(tile, carry):
-        rows = pl.ds(pl.multiple_of(tile * ROWS, ROWS), ROWS)
+        rows = pl.ds(pl.multiple_of(tile * height, height), height)
         scale = jnp.concatenate([squares[rows, :]] * (width // HD), axis=1)
 
         def add_blocks(group, carry):
@@ -172,7 +176,7 @@
         return lax.fori_loop(0, blocks // GROUP, add_blocks, carry)
 
     total[...] = jnp.zeros_like(total)
-    lax.fori_loop(0, slots // ROWS, project_rows, 0)
+    lax.fori_loop(0, slots // height, project_rows, 0)
     cosine, signed_sine = cosine_ref[...], sine_ref[...]
     for head in range(HEADS):
         part = total[:, head * HD : (head + 1) * HD]
@@ -368,11 +372,14 @@
     chosen = selected[0]
     slot_count = chosen.shape[0]
     early = EARLY * SLOTS
+    middle = NEAR * SPAN
+    near_cache = lax.ppermute(own_cache[:middle], "col", flipped(16))
+    early_tokens = lax.all_gather(tokens[0, :early], "col", axis=0)
     other_keyval = lax.ppermute(w_keyval, "col", flipped(16))
-    early_tokens = lax.all_gather(tokens[0, :early], "col", axis=0)
     late_tokens, other_keyval = lax.optimization_barrier((tokens[0, early:], other_keyval))
     late_tokens = lax.all_gather(late_tokens, "col", axis=0)
-    other_cache = lax.ppermute(own_cache, "col", flipped(16))
+    far_cache, early_tokens = lax.optimization_barrier((own_cache[middle:], early_tokens))
+    far_cache = lax.ppermute(far_cache, "col", flipped(16))
 
     weights = jnp.concatenate(
         [
@@ -397,14 +404,19 @@
     cosine, signed_sine = angles(chosen.astype(jnp.float32), HD)
     span_starts = jnp.arange(NCHUNK, dtype=jnp.int32) * SPAN - anchor[0]
     span_cosine, span_sine = angles(span_starts.astype(jnp.float32), HD)
-    keys, values, key_places = prepare(
-        holds_key.astype(jnp.int32)[None],
-        own_cache,
-        other_cache,
-        span_cosine[:, None],
-        span_sine[:, None],
-        chosen[None],
-    )
+    prepared = ()
+    for first_span, partner in ((0, near_cache), (NEAR, far_cache)):
+        prepared = prepare(
+            first_span,
+            holds_key.astype(jnp.int32)[None],
+            own_cache,
+            partner,
+            span_cosine[:, None],
+            span_sine[:, None],
+            chosen[None],
+            prepared,
+        )
+    keys, values, key_places = prepared
     grouped = chosen.reshape(-1, SLOTS)
     farthest = jnp.max(jnp.where(grouped < LENGTH, grouped, -1), axis=1)
     key_blocks = (farthest + KEYS) // KEYS
@@ -422,6 +434,8 @@
         (0, early, [early_tokens], (0,), absolute),
         (early, slot_count, [late_tokens], (0,), absolute),
     ):
+        if results:
+            results[0], pieces = lax.optimization_barrier((results[0], pieces))
         queries, *fresh = project(
             pieces,
             piece_offsets,

time: 245 us -> 238 us (0.971)
  the two profiles are of different devices: /device:TPU:5 before, /device:TPU:7 now
where the time goes in v4:
time: 238 us; the launch traced here: 234 us
  Pallas kernels  103 us (43%)
  waiting for transfers between devices  76.2 us (32%)
  starting transfers between devices  16.7 us (7%)
  local copies, waits for them, and re-layouts  16.2 us (7%)
  between operations  13.8 us (6%)
  other arithmetic  8.05 us (3%)
    pallas_call x2, Pallas kernels, attend(): pl.pallas_call(functools.partial(attend_kernel, first), out_shape=jax.Sha...  53.5 us
    pallas_call x2, Pallas kernels, project(): pl.pallas_call(functools.partial(project_kernel, offsets, len(token_piece...  33.5 us
    ppermute x1, waiting for transfers between devices, ring(): behind = lax.ppermute(block, axis, shift(1))  29.4 us
    all_gather x1, waiting for transfers between devices, shards(): early_tokens = lax.all_gather(tokens[0, :early], 'col', axis=0)  22.8 us
    pallas_call x2, Pallas kernels, prepare(): pl.pallas_call(functools.partial(prepare_kernel, first), out_shape=(jax.S...  15.8 us
    ppermute x1, waiting for transfers between devices, shards(): near_cache = lax.ppermute(own_cache[:middle], 'col', flipped(16))  14 us
    ppermute x5, starting transfers between devices, shards(): theirs = [lax.ppermute(piece, 'row', flipped(8)) for piece in mine]  9.07 us
    unnamed x38, local copies, waits for them, and re-layouts  7.17 us
  transfers between devices with their start and end apart: 14, of which 5 were waited for; matrix products, arithmetic and copies ran while one was open for 6% of the time, Pallas kernels for 27%

profile of v4, /device:TPU:7, one launch (start us, length us, event | category | flops | bytes accessed | tf_op | source)
XLA Modules:
  0.0 233.7 jit_solution(18044581348124262636)
XLA Ops:
  6.5 2.2 slice.55
  8.8 1.7 collective-permute-start
  10.5 1.8 slice_bitcast_fusion.2
  12.3 4.1 %collective-permute-done = bf16[1024,128]{1,0:T(8,128)(2,1)S(1)} collective-permute-done((bf16[1024,128]{1,0:T(8,128)(2,1)S(1)}, bf16[1024,128]{1,0:T(8,128)(2,1)S(1)}, u32[]{:S(2)}, u32[]{:S(2)}) %collective-permute-start) | collective-permute-done | bytes 262176 | tf_op jit(solution)/shard_map/ppermute | solution.py:378
  17.1 1.2 collective-permute-start.2
  18.6 1.3 slice_bitcast_fusion
  19.9 1.3 collective-permute-start.11
  22.1 29.4 %collective-permute-done.1.refs_9_ = bf16[1024,768]{1,0:T(8,128)(2,1)} collective-permute-done((bf16[1024,768]{1,0:T(8,128)(2,1)S(1)}, bf16[1024,768]{1,0:T(8,128)(2,1)}, u32[]{:S(2)}, u32[]{:S(2)}) %collective-permute-start.1) | collective-permute-done | bytes 1572896 | tf_op jit(solution)/shard_map/ppermute | solution.py:359
  51.4 1.2 slice.70
  52.6 1.7 collective-permute-start.3
  54.3 1.2 slice.71
  55.7 2.8 %collective-permute-start.5 = (bf16[1024,768]{1,0:T(8,128)(2,1)}, bf16[1024,768]{1,0:T(8,128)(2,1)}, u32[]{:S(2)}, u32[]{:S(2)}) collective-permute-start(bf16[1024,768]{1,0:T(8,128)(2,1)} %copy-done.10), channel_id=1, source_target_pairs={{0,16},{16,0},{32,48},{48,32},{64,80},{80,64},{96,112},{112,96},{1... | collective-permute-start | bytes 4718600 | tf_op jit(solution)/shard_map/ppermute | solution.py:393
  58.6 14.0 %collective-permute-done.11.partner_ref = bf16[6144,128]{1,0:T(8,128)(2,1)} collective-permute-done((bf16[6144,128]{1,0:T(8,128)(2,1)}, bf16[6144,128]{1,0:T(8,128)(2,1)}, u32[]{:S(2)}, u32[]{:S(2)}) %collective-permute-start.11) | collective-permute-done | bytes 1572896 | tf_op jit(solution)/shard_map/ppermute | solution.py:376
  72.6 5.7 %collective-permute-start.7 = (bf16[1024,768]{1,0:T(8,128)(2,1)}, bf16[1024,768]{1,0:T(8,128)(2,1)}, u32[]{:S(2)}, u32[]{:S(2)}) collective-permute-start(bf16[1024,768]{1,0:T(8,128)(2,1)} %collective-permute-done.2.refs_10_), channel_id=1, source_target_pairs={{0,16},{16,0},{32,48},{48,32},{64,80},{80,64},{96,112},{112,96},{1... | collective-permute-start | bytes 4718600 | tf_op jit(solution)/shard_map/ppermute | solution.py:393
  78.3 3.1 %fusion.2 = (f32[1152,64]{1,0:T(8,128)S(1)}, f32[1152,64]{1,0:T(8,128)S(1)}, f32[1152,64]{1,0:T(8,128)}) fusion(f32[64]{0:T(128)S(1)} %multiply_exponential_fusion, f32[1152]{0:T(1024)S(1)} %convert_element_type.16), kind=kLoop, calls=%fused_computation.17 | loop fusion | flops 147456 | bytes 889600 | tf_op jit(solution)/shard_map/neg | solution.py:51
  82.3 1.3 pad_maximum_fusion.1
  83.6 1.3 fusion
  84.9 1.1 slice_bitcast_fusion.1
  86.0 11.3 %prepare.2 = (bf16[8192,128]{1,0:T(8,128)(2,1)}, bf16[128,8192]{1,0:T(8,128)(2,1)}, s32[8192,128]{1,0:T(8,128)}) custom-call(s32[1]{0:T(128)} %bitcast.2.holds_key_ref, bf16[8192,128]{1,0:T(8,128)(2,1)} %bitcast.23, bf16[6144,128]{1,0:T(8,128)(2,1)} %collective-permute-done.11.partner_ref, f32[16,1,128]{2,1,0:T(1,128)} %bitcast.25, f32[16,1,128]{2,1,0:T(1,128)} %bitcast.27, ...), custom_call_target="tpu_custom_call" | custom-call | flops 10000000 | bytes 6291456 | tf_op jit(solution)/shard_map/prepare/pallas_call | solution.py:80
  97.3 22.8 %all-gather.4.cloned.1.call-done.refs_7_ = bf16[16,768,512]{2,1,0:T(8,128)(2,1)} async-done(((bf16[1,768,512]{2,1,0:T(8,128)(2,1)}), bf16[16,768,512]{2,1,0:T(8,128)(2,1)}) %all-gather.4.cloned.1.call-update) | async-done | bytes 12582928 | tf_op jit(solution)/shard_map/all_gather | solution.py:377
  120.2 1.3 collective-permute-start.10
  121.5 1.1 copy-done.3
  122.6 20.6 %project.2 = (bf16[4,768,128]{2,1,0:T(8,128)(2,1)S(1)}, bf16[1024,128]{1,0:T(8,128)(2,1)S(1)}, bf16[128,1024]{1,0:T(8,128)(2,1)S(1)}) custom-call(s32[16]{0:T(128)S(1)} %iota.18.refs_0_, s32[10]{0:T(128)S(1)} %pad_add_fusion.refs_1_, bf16[16,1,512]{2,1,0:T(2,128)(2,1)S(1)} %reshape.33.refs_2_, f32[768,128]{1,0:T(8,128)S(1)} %get-tuple-element.52.refs_3_, ...), custom_call_target="tpu_custom_call" | custom-call | flops 19327352832 | bytes 25165824 | tf_op jit(solution)/shard_map/project/pallas_call | solution.py:205
  144.9 4.5 %prepare.3 = (bf16[8192,128]{1,0:T(8,128)(2,1)}, bf16[128,8192]{1,0:T(8,128)(2,1)}, s32[8192,128]{1,0:T(8,128)}) custom-call(s32[1]{0:T(128)} %bitcast.2.holds_key_ref, bf16[8192,128]{1,0:T(8,128)(2,1)} %bitcast.24, bf16[2048,128]{1,0:T(8,128)(2,1)} %copy-done.12, ...), custom_call_target="tpu_custom_call", output_to_operand_aliasing={{0}: (6, {}), {1}: (7, {}), {2}: (8, {})} | custom-call | flops 10000000 | bytes 6291456 | tf_op jit(solution)/shard_map/prepare/pallas_call | solution.py:80
  149.7 1.6 copy-done
  151.3 1.1 copy-done.6
  152.4 27.3 %attend.2 = bf16[768,512]{1,0:T(8,128)(2,1)S(1)} custom-call(s32[6]{0:T(128)S(1)} %bitcast.22, bf16[4,768,128]{2,1,0:T(8,128)(2,1)S(1)} %copy-done.6, s32[1,768]{1,0:T(1,128)S(1)} %slice.59.chosen_ref, bf16[8192,128]{1,0:T(8,128)(2,1)S(1)} %copy-done, bf16[128,8192]{1,0:T(8,128)(2,1)} %get-tuple-element.31.value_ref, ...), custom_call_target="tpu_custom_call" | custom-call | flops 6442450944 | bytes 12582912 | tf_op jit(solution)/shard_map/attend/pallas_call | solution.py:323
  179.7 5.8 %all-gather.6.cloned.1.call-done = bf16[6144,512]{1,0:T(8,128)(2,1)} async-done(((bf16[384,512]{1,0:T(8,128)(2,1)}), bf16[6144,512]{1,0:T(8,128)(2,1)}) %all-gather.6.cloned.1.call-update) | async-done | bytes 6291472 | tf_op jit(solution)/shard_map/all_gather | solution.py:380
  185.5 1.1 copy-done.4
  186.7 12.9 %project.3 = (bf16[4,384,128]{2,1,0:T(8,128)(2,1)S(1)}, bf16[1536,128]{1,0:T(8,128)(2,1)S(1)}, bf16[128,1536]{1,0:T(8,128)(2,1)S(1)}) custom-call(s32[16]{0:T(128)S(1)} %iota.21.refs_0_, s32[10]{0:T(128)S(1)} %pad_add_fusion.refs_1_, bf16[16,1,512]{2,1,0:T(2,128)(2,1)S(1)} %reshape.33.refs_2_, f32[384,128]{1,0:T(8,128)S(1)} %get-tuple-element.54.refs_3_, ...), custom_call_target="tpu_custom_call" | custom-call | flops 9663676416 | bytes 18874368 | tf_op jit(solution)/shard_map/project/pallas_call | solution.py:205
  199.6 26.2 %attend.3 = bf16[384,512]{1,0:T(8,128)(2,1)S(1)} custom-call(s32[3]{0:T(128)S(1)} %slice.62.blocks_ref, bf16[4,384,128]{2,1,0:T(8,128)(2,1)S(1)} %get-tuple-element.38.query_ref, s32[1,384]{1,0:T(1,128)S(1)} %slice.65.chosen_ref, bf16[8192,128]{1,0:T(8,128)(2,1)S(1)} %copy-done.1, bf16[128,8192]{1,0:T(8,128)(2,1)} %get-tuple-element.31.value_ref, ...), custom_call_target="tpu_custom_call" | custom-call | flops 3221225472 | bytes 12582912 | tf_op jit(solution)/shard_map/attend/pallas_call | solution.py:323
  225.8 1.1 maximum_bitcast_fusion
  (74 shorter events, 4.9 us)
Async XLA Ops:
  6.5 2.2 copy-start.13
  6.5 10.0 %copy-start.11 = (bf16[1024,512]{1,0:T(8,128)(2,1)S(1)}, bf16[1024,512]{1,0:T(8,128)(2,1)}, u32[]{:S(2)}) copy-start(bf16[1024,512]{1,0:T(8,128)(2,1)} %param.11) | copy-start | bytes 3145732
  6.5 113.6 %all-gather.4.cloned.1.call-start = ((), (), s32[]{:S(2)}) async-start(), calls=%async_computation | async-start | bytes 13369344 | tf_op jit(solution)/shard_map/all_gather | solution.py:377
  8.7 176.8 %all-gather.6.cloned.1.call-start = ((), (), s32[]{:S(2)}) async-start(), calls=%async_computation.1 | async-start | bytes 6684672 | tf_op jit(solution)/shard_map/all_gather | solution.py:380
  8.8 7.6 %collective-permute-start = (bf16[1024,128]{1,0:T(8,128)(2,1)S(1)}, bf16[1024,128]{1,0:T(8,128)(2,1)S(1)}, u32[]{:S(2)}, u32[]{:S(2)}) collective-permute-start(bf16[1024,128]{1,0:T(8,128)(2,1)S(1)} %copy-done.13), channel_id=1, source_target_pairs={{0,1},{1,0},{2,3},{3,2},{4,5},{5,4},{6,7},{7,6},{8,9},{9,8},{10,11... | collective-permute-start | bytes 786440 | tf_op jit(solution)/shard_map/ppermute | solution.py:378
  16.5 2.2 copy-start.7
  16.7 36.0 %copy-start.10 = (bf16[1024,768]{1,0:T(8,128)(2,1)}, bf16[1024,768]{1,0:T(8,128)(2,1)S(1)}, u32[]{:S(2)}) copy-start(bf16[1024,768]{1,0:T(8,128)(2,1)S(1)} %pad_maximum_fusion.refs_8_) | copy-start | bytes 4718596
  16.7 4.5 %copy-start.14 = (s32[1,1152]{1,0:T(1,128)S(1)}, s32[1,1152]{1,0:T(1,128)}, u32[]{:S(2)}) copy-start(s32[1,1152]{1,0:T(1,128)} %chosen_ref.3) | copy-start | bytes 13828
  16.7 4.5 %copy-start.18 = (s32[1,16]{1,0:T(1,128)S(1)}, s32[1,16]{1,0:T(1,128)}, u32[]{:S(2)}) copy-start(s32[1,16]{1,0:T(1,128)} %param.15) | copy-start | bytes 196
  16.7 5.3 %copy-start.16 = (s32[5]{0:T(128)S(1)}, s32[5]{0:T(128)}, u32[]{:S(2)}) copy-start(s32[5]{0:T(128)} %constant.88.clone) | copy-start | bytes 64
  16.7 5.3 %copy-start.17 = (s32[5]{0:T(128)S(1)}, s32[5]{0:T(128)}, u32[]{:S(2)}) copy-start(s32[5]{0:T(128)} %constant.87.clone) | copy-start | bytes 64
  16.7 34.7 %collective-permute-start.1 = (bf16[1024,768]{1,0:T(8,128)(2,1)S(1)}, bf16[1024,768]{1,0:T(8,128)(2,1)}, u32[]{:S(2)}, u32[]{:S(2)}) collective-permute-start(bf16[1024,768]{1,0:T(8,128)(2,1)S(1)} %pad_maximum_fusion.refs_8_), channel_id=1, source_target_pairs={{0,32},{16,48},{32,64},{48,80},{64,96},{80,112},{96,0},{112,16},{1... | collective-permute-start | bytes 4718600 | tf_op jit(solution)/shard_map/ppermute | solution.py:359
  17.1 37.2 %collective-permute-start.2 = (bf16[1024,768]{1,0:T(8,128)(2,1)S(1)}, bf16[1024,768]{1,0:T(8,128)(2,1)}, u32[]{:S(2)}, u32[]{:S(2)}) collective-permute-start(bf16[1024,768]{1,0:T(8,128)(2,1)S(1)} %pad_maximum_fusion.refs_8_), channel_id=1, source_target_pairs={{0,96},{16,112},{32,0},{48,16},{64,32},{80,48},{96,64},{112,80},{1... | collective-permute-start | bytes 4718600 | tf_op jit(solution)/shard_map/ppermute | solution.py:360
  19.9 52.7 %collective-permute-start.11 = (bf16[6144,128]{1,0:T(8,128)(2,1)}, bf16[6144,128]{1,0:T(8,128)(2,1)}, u32[]{:S(2)}, u32[]{:S(2)}) collective-permute-start(bf16[6144,128]{1,0:T(8,128)(2,1)} %slice_bitcast_fusion), channel_id=1, source_target_pairs={{0,1},{1,0},{2,3},{3,2},{4,5},{5,4},{6,7},{7,6},{8,9},{9,8},{10,11... | collective-permute-start | bytes 4718600 | tf_op jit(solution)/shard_map/ppermute | solution.py:376
  22.1 60.1 %copy-start.15 = (bf16[8192]{0:T(1024)(128)(2,1)S(1)}, bf16[8192]{0:T(1024)(128)(2,1)}, u32[]{:S(2)}) copy-start(bf16[8192]{0:T(1024)(128)(2,1)} %param.10) | copy-start | bytes 49156
  52.6 28.8 %collective-permute-start.3 = (bf16[512,768]{1,0:T(8,128)(2,1)S(1)}, bf16[512,768]{1,0:T(8,128)(2,1)S(1)}, u32[]{:S(2)}, u32[]{:S(2)}) collective-permute-start(bf16[512,768]{1,0:T(8,128)(2,1)S(1)} %slice.70), channel_id=1, source_target_pairs={{0,32},{16,48},{32,64},{48,80},{64,96},{80,112},{96,0},{112,16},{1... | collective-permute-start | bytes 2359304 | tf_op jit(solution)/shard_map/ppermute | solution.py:361
  55.5 26.0 %collective-permute-start.4 = (bf16[512,768]{1,0:T(8,128)(2,1)S(1)}, bf16[512,768]{1,0:T(8,128)(2,1)S(1)}, u32[]{:S(2)}, u32[]{:S(2)}) collective-permute-start(bf16[512,768]{1,0:T(8,128)(2,1)S(1)} %slice.71), channel_id=1, source_target_pairs={{0,96},{16,112},{32,0},{48,16},{64,32},{80,48},{96,64},{112,80},{1... | collective-permute-start | bytes 2359304 | tf_op jit(solution)/shard_map/ppermute | solution.py:362
  55.7 64.5 %collective-permute-start.5 = (bf16[1024,768]{1,0:T(8,128)(2,1)}, bf16[1024,768]{1,0:T(8,128)(2,1)}, u32[]{:S(2)}, u32[]{:S(2)}) collective-permute-start(bf16[1024,768]{1,0:T(8,128)(2,1)} %copy-done.10), channel_id=1, source_target_pairs={{0,16},{16,0},{32,48},{48,32},{64,80},{80,64},{96,112},{112,96},{1... | collective-permute-start | bytes 4718600 | tf_op jit(solution)/shard_map/ppermute | solution.py:393
  58.5 63.0 %collective-permute-start.6 = (bf16[1024,768]{1,0:T(8,128)(2,1)}, bf16[1024,768]{1,0:T(8,128)(2,1)}, u32[]{:S(2)}, u32[]{:S(2)}) collective-permute-start(bf16[1024,768]{1,0:T(8,128)(2,1)} %collective-permute-done.1.refs_9_), channel_id=1, source_target_pairs={{0,16},{16,0},{32,48},{48,32},{64,80},{80,64},{96,112},{112,96},{1... | collective-permute-start | bytes 4718600 | tf_op jit(solution)/shard_map/ppermute | solution.py:393
  72.6 48.8 %collective-permute-start.7 = (bf16[1024,768]{1,0:T(8,128)(2,1)}, bf16[1024,768]{1,0:T(8,128)(2,1)}, u32[]{:S(2)}, u32[]{:S(2)}) collective-permute-start(bf16[1024,768]{1,0:T(8,128)(2,1)} %collective-permute-done.2.refs_10_), channel_id=1, source_target_pairs={{0,16},{16,0},{32,48},{48,32},{64,80},{80,64},{96,112},{112,96},{1... | collective-permute-start | bytes 4718600 | tf_op jit(solution)/shard_map/ppermute | solution.py:393
  81.5 0.8 copy-start.8
  81.5 40.0 %collective-permute-start.8 = (bf16[512,768]{1,0:T(8,128)(2,1)S(1)}, bf16[512,768]{1,0:T(8,128)(2,1)}, u32[]{:S(2)}, u32[]{:S(2)}) collective-permute-start(bf16[512,768]{1,0:T(8,128)(2,1)S(1)} %collective-permute-done.3.refs_11_), channel_id=1, source_target_pairs={{0,16},{16,0},{32,48},{48,32},{64,80},{80,64},{96,112},{112,96},{1... | collective-permute-start | bytes 2359304 | tf_op jit(solution)/shard_map/ppermute | solution.py:393
  81.5 3.4 %copy-start.2 = (bf16[512,768]{1,0:T(8,128)(2,1)}, bf16[512,768]{1,0:T(8,128)(2,1)S(1)}, u32[]{:S(2)}) copy-start(bf16[512,768]{1,0:T(8,128)(2,1)S(1)} %collective-permute-done.4.refs_12_) | copy-start | bytes 2359300
  81.5 39.9 %collective-permute-start.9 = (bf16[512,768]{1,0:T(8,128)(2,1)S(1)}, bf16[512,768]{1,0:T(8,128)(2,1)}, u32[]{:S(2)}, u32[]{:S(2)}) collective-permute-start(bf16[512,768]{1,0:T(8,128)(2,1)S(1)} %collective-permute-done.4.refs_12_), channel_id=1, source_target_pairs={{0,16},{16,0},{32,48},{48,32},{64,80},{80,64},{96,112},{112,96},{1... | collective-permute-start | bytes 2359304 | tf_op jit(solution)/shard_map/ppermute | solution.py:393
  82.2 1.4 copy-start.9
  120.2 24.0 %collective-permute-start.10 = (bf16[2048,128]{1,0:T(8,128)(2,1)S(1)}, bf16[2048,128]{1,0:T(8,128)(2,1)S(1)}, u32[]{:S(2)}, u32[]{:S(2)}) collective-permute-start(bf16[2048,128]{1,0:T(8,128)(2,1)S(1)} %slice_bitcast_fusion.1), channel_id=1, source_target_pairs={{0,1},{1,0},{2,3},{3,2},{4,5},{5,4},{6,7},{7,6},{8,9},{9,8},{10,11... | collective-permute-start | bytes 1572872 | tf_op jit(solution)/shard_map/ppermute | solution.py:382
  121.5 1.1 copy-start.3
  143.2 0.9 copy-start.5
  149.7 1.6 copy-start
  151.3 1.1 copy-start.6
  185.5 1.1 copy-start.4
  186.7 12.9 %copy-start.1 = (bf16[8192,128]{1,0:T(8,128)(2,1)S(1)}, bf16[8192,128]{1,0:T(8,128)(2,1)}, u32[]{:S(2)}) copy-start(bf16[8192,128]{1,0:T(8,128)(2,1)} %get-tuple-element.30.key_ref) | copy-start | bytes 6291460
  (1 other events, 0.8 us)
Sparse Core Ops, SparseCore 0:
  9.5 110.5 all-gather.3
  122.3 63.1 all-gather.5

commit v5 on v4

--- a/solution.py
+++ b/solution.py
@@ -56,9 +56,8 @@
     return vectors * cosine + pltpu.roll(vectors, HD // 2, 1) * signed_sine
 
 
-def prepare_kernel(first, holds_key_ref, own_ref, partner_ref, cosine_ref, sine_ref, chosen_ref, *refs):
-    key_ref, value_ref, place_ref = refs[-3:]
-    step = first + pl.program_id(0)
+def prepare_kernel(holds_key_ref, own_ref, partner_ref, cosine_ref, sine_ref, *refs):
+    key_ref, value_ref = refs[-2:]
     holds_key = holds_key_ref[0] == 1
     own = own_ref[...]
     partner = partner_ref[...]
@@ -66,23 +65,49 @@
     stored_value = jnp.where(holds_key, partner, own).astype(jnp.float32)
     key_ref[...] = rotate(stored_key, cosine_ref[0], sine_ref[0]).astype(jnp.bfloat16)
     value_ref[...] = stored_value.T.astype(jnp.bfloat16)
-    place = step * SPAN + lax.broadcasted_iota(jnp.int32, (SPAN, HD), 0)
-    seen = jnp.zeros((SPAN, HD), jnp.int32)
-    for start in range(0, chosen_ref.shape[1], HD):
-        seen = jnp.where(place == chosen_ref[0:1, start : start + HD], 1, seen)
-    replaced = jnp.max(seen, axis=1, keepdims=True) > 0
-    place_ref[...] = jnp.where(replaced, HIDDEN_POSITION, place)
-
-
-def prepare(first, holds_key, own, partner, cosine, signed_sine, chosen, earlier):
+
+
+def mark_kernel(chosen_ref, place_ref):
+    step = pl.program_id(0)
+
+    @pl.when(step < NCHUNK)
+    def _():
+        place = step * SPAN + lax.broadcasted_iota(jnp.int32, (SPAN, HD), 0)
+        seen = jnp.zeros((SPAN, HD), jnp.int32)
+        for start in range(0, chosen_ref.shape[1], HD):
+            seen = jnp.where(place == chosen_ref[0:1, start : start + HD], 1, seen)
+        replaced = jnp.max(seen, axis=1, keepdims=True) > 0
+        place_ref[...] = jnp.where(replaced, HIDDEN_POSITION, place)
+
+    @pl.when(step >= NCHUNK)
+    def _():
+        for part in range(0, SPAN, HD):
+            start = pl.multiple_of((step - NCHUNK) * SPAN + part, HD)
+            fresh = jnp.broadcast_to(chosen_ref[0:1, pl.ds(start, HD)], (HD, HD))
+            place_ref[part : part + HD, :] = fresh.astype(jnp.float32).T.astype(jnp.int32)
+
+
+def mark(chosen):
+    total = LENGTH + chosen.shape[1]
+    return pl.pallas_call(
+        mark_kernel,
+        out_shape=jax.ShapeDtypeStruct((total, HD), jnp.int32),
+        grid=(total // SPAN,),
+        in_specs=[pl.BlockSpec((1, chosen.shape[1]), lambda step: (0, 0))],
+        out_specs=pl.BlockSpec((SPAN, HD), lambda step: (step, 0)),
+        cost_estimate=pl.CostEstimate(flops=10**7, bytes_accessed=5 * 2**20, transcendentals=0),
+        name="mark",
+    )(chosen)
+
+
+def prepare(first, holds_key, own, partner, cosine, signed_sine, earlier):
     block = pl.BlockSpec((SPAN, HD), lambda step, flag: (first + step, 0))
     angle = pl.BlockSpec((1, 1, HD), lambda step, flag: (first + step, 0, 0))
     return pl.pallas_call(
-        functools.partial(prepare_kernel, first),
+        prepare_kernel,
         out_shape=(
             jax.ShapeDtypeStruct((LENGTH, HD), jnp.bfloat16),
             jax.ShapeDtypeStruct((HD, LENGTH), jnp.bfloat16),
-            jax.ShapeDtypeStruct((LENGTH, HD), jnp.int32),
         ),
         grid_spec=pltpu.PrefetchScalarGridSpec(
             num_scalar_prefetch=1,
@@ -92,24 +117,22 @@
                 pl.BlockSpec((SPAN, HD), lambda step, flag: (step, 0)),
                 angle,
                 angle,
-                pl.BlockSpec((1, chosen.shape[1]), lambda step, flag: (0, 0)),
             ]
             + [pl.BlockSpec(memory_space=pl.ANY)] * len(earlier),
             out_specs=(
                 block,
                 pl.BlockSpec((HD, SPAN), lambda step, flag: (0, first + step)),
-                block,
             ),
         ),
-        input_output_aliases={6 + number: number for number in range(len(earlier))},
+        input_output_aliases={5 + number: number for number in range(len(earlier))},
         cost_estimate=pl.CostEstimate(flops=10**7, bytes_accessed=6 * 2**20, transcendentals=0),
         name="prepare",
-    )(holds_key, own, partner, cosine, signed_sine, chosen, *earlier)
+    )(holds_key, own, partner, cosine, signed_sine, *earlier)
 
 
 def project_kernel(offsets, token_count, weight_count, done, *refs):
-    token_place_ref, weight_place_ref, gain_ref, cosine_ref, sine_ref, old_key_ref, old_value_ref = refs[:7]
-    refs = refs[7:]
+    weight_place_ref, gain_ref, cosine_ref, sine_ref = refs[:4]
+    refs = refs[4:]
     token_refs, refs = refs[:token_count], refs[token_count:]
     weight_refs, refs = refs[:weight_count], refs[weight_count:]
     query_ref, key_ref, value_ref, held, weights, total, squares, token_sem, weight_sem = refs
@@ -118,7 +141,7 @@
     for piece, ref in enumerate(token_refs):
         for part in range(ref.shape[0]):
             number = len(token_copies)
-            where = held.at[token_place_ref[number], pl.ds(offsets[piece], ref.shape[1]), :]
+            where = held.at[part, pl.ds(offsets[piece], ref.shape[1]), :]
             token_copies.append(pltpu.make_async_copy(ref.at[part], where, token_sem.at[number]))
     weight_copies = []
     for piece, ref in enumerate(weight_refs):
@@ -130,9 +153,8 @@
     squares[...] = jnp.zeros_like(squares)
     number = 0
     for piece, ref in enumerate(token_refs):
-        for _ in range(ref.shape[0]):
+        for block in range(ref.shape[0]):
             token_copies[number].wait()
-            block = token_place_ref[number]
             number += 1
 
             def add_squares(tile, carry, block=block, offset=offsets[piece]):
@@ -181,9 +203,6 @@
     for head in range(HEADS):
         part = total[:, head * HD : (head + 1) * HD]
         query_ref[head] = rotate(part, cosine, signed_sine).astype(jnp.bfloat16)
-    if done:
-        key_ref[:done, :] = old_key_ref[:done, :]
-        value_ref[:, :done] = old_value_ref[:, :done]
     key_ref[done : done + slots, :] = rotate(
         total[:, HEADS * HD : (HEADS + 1) * HD], cosine, signed_sine
     ).astype(jnp.bfloat16)
@@ -193,7 +212,7 @@
         value_ref[:, done + slots :] = jnp.zeros_like(value_ref[:, done + slots :])
 
 
-def project(token_pieces, offsets, token_places, gain, cosine, signed_sine, weight_pieces, weight_places, done, old):
+def project(token_pieces, offsets, gain, cosine, signed_sine, weight_pieces, weight_places, done):
     slots = cosine.shape[0]
     width = token_pieces[0].shape[-1]
     blocks = gain.shape[0]
@@ -209,7 +228,7 @@
             jax.ShapeDtypeStruct((fresh, HD), jnp.bfloat16),
             jax.ShapeDtypeStruct((HD, fresh), jnp.bfloat16),
         ),
-        in_specs=[scalars, scalars, whole, whole, whole, whole, whole]
+        in_specs=[scalars, whole, whole, whole]
         + [remote] * (len(token_pieces) + len(weight_pieces)),
         out_specs=(whole, whole, whole),
         scratch_shapes=[
@@ -217,7 +236,7 @@
             pltpu.VMEM((blocks * width, columns), jnp.bfloat16),
             pltpu.VMEM((slots, columns), jnp.float32),
             pltpu.VMEM((slots, HD), jnp.float32),
-            pltpu.SemaphoreType.DMA((token_places.shape[0],)),
+            pltpu.SemaphoreType.DMA((blocks * len(token_pieces),)),
             pltpu.SemaphoreType.DMA((len(weight_pieces),)),
         ],
         compiler_params=pltpu.CompilerParams(vmem_limit_bytes=48 * 2**20),
@@ -227,131 +246,328 @@
             transcendentals=0,
         ),
         name="project",
-    )(token_places, weight_places, gain, cosine, signed_sine, *old, *token_pieces, *weight_pieces)
-
-
-def attend_kernel(
-    first,
-    blocks_ref,
-    query_ref,
-    chosen_ref,
-    key_ref,
-    value_ref,
-    place_ref,
-    fresh_key_ref,
-    fresh_value_ref,
-    fresh_place_ref,
-    out_ref,
-    peak,
-    denominator,
-    numerator,
-    held,
+    )(weight_places, gain, cosine, signed_sine, *token_pieces, *weight_pieces)
+
+
+def attend_slots(
+    asked, chosen, stored, slots_seen, keys, values, places, out_ref, peak, denominator, numerator, score_slots
 ):
-    step = pl.program_id(0)
-    rows = HEADS * SLOTS
+    limit = jnp.concatenate([chosen] * HEADS, axis=1)
     peak[...] = jnp.full_like(peak, masked_score)
     denominator[...] = jnp.zeros_like(denominator)
     numerator[...] = jnp.zeros_like(numerator)
-    queries = query_ref[...].reshape(rows, HD)
-    limit = jnp.concatenate([chosen_ref[...]] * HEADS, axis=1)
-
-    def score(keys, block, slot):
-        start = pl.multiple_of(block * KEYS, KEYS)
-        held[slot] = lax.dot_general(
-            keys[pl.ds(start, KEYS), :],
-            queries,
+    count = stored + (slots_seen + KEYS - 1) // KEYS
+
+    def start_of(block):
+        block = jnp.minimum(block, count - 1)
+        block = jnp.where(block < stored, block, block - stored + LENGTH // KEYS)
+        return pl.multiple_of(block * KEYS, KEYS)
+
+    def score(block, slot):
+        score_slots[slot] = lax.dot_general(
+            keys[pl.ds(start_of(block), KEYS), :],
+            asked,
             (((1,), (1,)), ((), ())),
             preferred_element_type=jnp.float32,
         )
 
-    def gather(values, places, block, slot):
-        start = pl.multiple_of(block * KEYS, KEYS)
+    def gather(block, slot):
+        start = start_of(block)
         place = jnp.concatenate([places[pl.ds(start, KEYS), :]] * HEADS, axis=1)
-        scores = jnp.where(place <= limit, held[slot], masked_score)
+        scores = jnp.where(place <= limit, score_slots[slot], masked_score)
         old_peak = peak[...]
         new_peak = jnp.maximum(old_peak, jnp.max(scores, axis=0, keepdims=True))
         rescale = jnp.exp2((old_peak - new_peak) * exponent_scale)
-        weights = jnp.exp2((scores - new_peak) * exponent_scale)
-        denominator[...] = denominator[...] * rescale + jnp.sum(weights, axis=0, keepdims=True)
+        exponentials = jnp.exp2((scores - new_peak) * exponent_scale)
+        denominator[...] = denominator[...] * rescale + jnp.sum(
+            exponentials, axis=0, keepdims=True
+        )
         numerator[...] = numerator[...] * rescale + jnp.dot(
             values[:, pl.ds(start, KEYS)],
-            weights.astype(jnp.bfloat16),
+            exponentials.astype(jnp.bfloat16),
             preferred_element_type=jnp.float32,
         )
         peak[...] = new_peak
 
-    def walk(keys, values, places, count):
-        last = jnp.maximum(count - 1, 0)
-        score(keys, 0, 0)
-
-        def pair(turn, carry):
-            block = 2 * turn
-            score(keys, jnp.minimum(block + 1, last), 1)
-            gather(values, places, block, 0)
-            score(keys, jnp.minimum(block + 2, last), 0)
-            gather(values, places, block + 1, 1)
-            return carry
-
-        lax.fori_loop(0, count // 2, pair, 0)
-
-        @pl.when(count % 2 == 1)
-        def _():
-            gather(values, places, count - 1, 0)
-
-    walk(key_ref, value_ref, place_ref, blocks_ref[step])
-    walk(
-        fresh_key_ref,
-        fresh_value_ref,
-        fresh_place_ref,
-        ((first + step + 1) * SLOTS + KEYS - 1) // KEYS,
-    )
+    score(0, 0)
+
+    def pair(turn, carry):
+        block = 2 * turn
+        score(block + 1, 1)
+        gather(block, 0)
+        score(block + 2, 0)
+        gather(block + 1, 1)
+        return carry
+
+    lax.fori_loop(0, count // 2, pair, 0)
+
+    @pl.when(count % 2 == 1)
+    def _():
+        gather(count - 1, 0)
+
     outcome = jnp.where(limit < LENGTH, numerator[...] / denominator[...], 0.0)
     for head in range(HEADS):
         part = outcome[:, head * SLOTS : (head + 1) * SLOTS]
         out_ref[:, head * HD : (head + 1) * HD] = part.T.astype(jnp.bfloat16)
 
 
-def attend(first, key_blocks, queries, chosen, keys, values, places, fresh_keys, fresh_values, fresh_places):
+def attend_kernel(first, blocks_ref, query_ref, chosen_ref, *refs):
+    stored_refs, (out_ref, *scratch) = refs[:5], refs[-9:]
+    keys, values, places, peak, denominator, numerator, score_slots, sem = scratch
+    step = pl.program_id(0)
+    fresh = stored_refs[3].shape[0]
+
+    @pl.when(step == 0)
+    def _():
+        old, new = pl.ds(0, LENGTH), pl.ds(LENGTH, fresh)
+        wheres = (keys.at[old, :], values.at[:, old], places, keys.at[new, :], values.at[:, new])
+        held_places = stored_refs[2].at[pl.ds(0, LENGTH + fresh), :]
+        sources = (*stored_refs[:2], held_places, *stored_refs[3:])
+        copies = [
+            pltpu.make_async_copy(source, where, sem.at[number])
+            for number, (source, where) in enumerate(zip(sources, wheres))
+        ]
+        for copy in copies:
+            copy.start()
+        for copy in copies:
+            copy.wait()
+
+    attend_slots(
+        query_ref[...].reshape(HEADS * SLOTS, HD), chosen_ref[...], blocks_ref[step],
+        (first + step + 1) * SLOTS,
+        keys, values, places, out_ref, peak, denominator, numerator, score_slots,
+    )
+
+
+def attend(first, key_blocks, queries, chosen, stored, total_slots):
     slots = queries.shape[1]
     rows = HEADS * SLOTS
-
-    def still(array):
-        return pl.BlockSpec(
-            array.shape, lambda step, counts: (0, 0), pipeline_mode=pl.Buffered(1)
-        )
-
+    length = LENGTH + stored[3].shape[0]
     return pl.pallas_call(
         functools.partial(attend_kernel, first),
-        out_shape=jax.ShapeDtypeStruct((slots, HEADS * HD), jnp.bfloat16),
+        out_shape=jax.ShapeDtypeStruct((total_slots, HEADS * HD), jnp.bfloat16),
         grid_spec=pltpu.PrefetchScalarGridSpec(
             num_scalar_prefetch=1,
             grid=(slots // SLOTS,),
             in_specs=[
                 pl.BlockSpec((HEADS, SLOTS, HD), lambda step, counts: (0, step, 0)),
                 pl.BlockSpec((1, SLOTS), lambda step, counts: (0, step)),
-                still(keys),
-                still(values),
-                still(places),
-                still(fresh_keys),
-                still(fresh_values),
-                still(fresh_places),
-            ],
-            out_specs=pl.BlockSpec((SLOTS, HEADS * HD), lambda step, counts: (step, 0)),
+            ]
+            + [pl.BlockSpec(memory_space=pl.ANY)] * 5,
+            out_specs=pl.BlockSpec((SLOTS, HEADS * HD), lambda step, counts: (first + step, 0)),
             scratch_shapes=[
+                pltpu.VMEM((length, HD), jnp.bfloat16),
+                pltpu.VMEM((HD, length), jnp.bfloat16),
+                pltpu.VMEM((length, HD), jnp.int32),
                 pltpu.VMEM((1, rows), jnp.float32),
                 pltpu.VMEM((1, rows), jnp.float32),
                 pltpu.VMEM((HD, rows), jnp.float32),
                 pltpu.VMEM((2, KEYS, rows), jnp.float32),
+                pltpu.SemaphoreType.DMA((5,)),
             ],
         ),
-        compiler_params=pltpu.CompilerParams(vmem_limit_bytes=48 * 2**20),
+        compiler_params=pltpu.CompilerParams(vmem_limit_bytes=56 * 2**20),
         cost_estimate=pl.CostEstimate(
             flops=slots * HEADS * LENGTH * HD * 2,
             bytes_accessed=12 * 2**20,
             transcendentals=slots * HEADS * LENGTH // 2,
         ),
         name="attend",
-    )(key_blocks, queries, chosen, keys, values, places, fresh_keys, fresh_values, fresh_places)
+    )(key_blocks, queries, chosen, *stored)
+
+
+def blend_kernel(first, offsets, token_count, weight_count, *refs):
+    blocks_ref, weight_place_ref = refs[:2]
+    gain_ref, cosine_ref, sine_ref, chosen_ref, old_key_ref, old_value_ref = refs[2:8]
+    cache_key_ref, cache_value_ref, cache_place_ref = refs[8:11]
+    refs = refs[11:]
+    token_refs, refs = refs[:token_count], refs[token_count:]
+    weight_refs, refs = refs[:weight_count], refs[weight_count:]
+    out_ref, fresh_key_ref, fresh_value_ref, held, weights, total, squares, queries = refs[-18:-10]
+    keys, values, places, peak, denominator, numerator, score_slots = refs[-10:-3]
+    token_sem, weight_sem, cache_sem = refs[-3:]
+    step = pl.program_id(0)
+    done = first * SLOTS
+    blocks, slots, width = held.shape
+
+    @pl.when(step == 0)
+    def _():
+        token_copies = []
+        for piece, ref in enumerate(token_refs):
+            for part in range(ref.shape[0]):
+                number = len(token_copies)
+                where = held.at[part, pl.ds(offsets[piece], ref.shape[1]), :]
+                token_copies.append(pltpu.make_async_copy(ref.at[part], where, token_sem.at[number]))
+        weight_copies = []
+        for piece, ref in enumerate(weight_refs):
+            start = pl.multiple_of(weight_place_ref[piece] * width, width)
+            where = weights.at[pl.ds(start, ref.shape[0]), :]
+            weight_copies.append(pltpu.make_async_copy(ref, where, weight_sem.at[piece]))
+        fresh = fresh_key_ref.shape[0]
+        cache_copies = [
+            pltpu.make_async_copy(cache_key_ref, keys.at[pl.ds(0, LENGTH), :], cache_sem.at[0]),
+            pltpu.make_async_copy(cache_value_ref, values.at[:, pl.ds(0, LENGTH)], cache_sem.at[1]),
+            pltpu.make_async_copy(
+                cache_place_ref.at[pl.ds(0, LENGTH + fresh), :], places, cache_sem.at[2]
+            ),
+        ]
+        for copy in token_copies + weight_copies + cache_copies:
+            copy.start()
+        squares[...] = jnp.zeros_like(squares)
+        number = 0
+        for piece, ref in enumerate(token_refs):
+            for block in range(ref.shape[0]):
+                token_copies[number].wait()
+                number += 1
+
+                def add_squares(tile, carry, block=block, offset=offsets[piece]):
+                    rows = pl.ds(pl.multiple_of(offset + tile * TILE, TILE), TILE)
+                    hidden = held[block, rows, :].astype(jnp.float32)
+                    hidden = hidden * hidden
+                    part = hidden[:, :HD]
+                    for start in range(HD, width, HD):
+                        part = part + hidden[:, start : start + HD]
+                    squares[rows, :] += part
+                    return carry
+
+                lax.fori_loop(0, ref.shape[1] // TILE, add_squares, 0)
+        mean_square = jnp.sum(squares[...], axis=1, keepdims=True) * (1.0 / (blocks * width))
+        squares[...] = jnp.broadcast_to(lax.rsqrt(mean_square + epsilon), squares.shape)
+        for copy in weight_copies:
+            copy.wait()
+        height = slots // max(1, slots // ROWS)
+
+        def project_rows(tile, carry):
+            rows = pl.ds(pl.multiple_of(tile * height, height), height)
+            scale = jnp.concatenate([squares[rows, :]] * (width // HD), axis=1)
+
+            def add_blocks(group, carry):
+                normed = []
+                for part in range(GROUP):
+                    block = group * GROUP + part
+                    hidden = held[block, rows, :].astype(jnp.float32) * scale
+                    normed.append(
+                        (hidden * gain_ref[block].astype(jnp.float32)).astype(jnp.bfloat16)
+                    )
+                depth = GROUP * width
+                start = pl.multiple_of(group * depth, depth)
+                product = jnp.dot(
+                    jnp.concatenate(normed, axis=1),
+                    weights[pl.ds(start, depth), :],
+                    preferred_element_type=jnp.float32,
+                )
+                total[rows, :] = jnp.where(group == 0, 0.0, total[rows, :]) + product
+                return carry
+
+            return lax.fori_loop(0, blocks // GROUP, add_blocks, carry)
+
+        total[...] = jnp.zeros_like(total)
+        lax.fori_loop(0, slots // height, project_rows, 0)
+        cosine, signed_sine = cosine_ref[...], sine_ref[...]
+        for head in range(HEADS):
+            part = total[:, head * HD : (head + 1) * HD]
+            queries[head] = rotate(part, cosine, signed_sine).astype(jnp.bfloat16)
+        if done:
+            fresh_key_ref[:done, :] = old_key_ref[:done, :]
+            fresh_value_ref[:, :done] = old_value_ref[:, :done]
+        fresh_key_ref[done : done + slots, :] = rotate(
+            total[:, HEADS * HD : (HEADS + 1) * HD], cosine, signed_sine
+        ).astype(jnp.bfloat16)
+        fresh_value_ref[:, done : done + slots] = total[:, (HEADS + 1) * HD :].T.astype(jnp.bfloat16)
+        if done + slots < fresh:
+            fresh_key_ref[done + slots :, :] = jnp.zeros((fresh - done - slots, HD), jnp.bfloat16)
+            fresh_value_ref[:, done + slots :] = jnp.zeros((HD, fresh - done - slots), jnp.bfloat16)
+        keys[LENGTH:, :] = fresh_key_ref[...]
+        values[:, LENGTH:] = fresh_value_ref[...]
+        for copy in cache_copies:
+            copy.wait()
+
+    @pl.when(step > 0)
+    def _():
+        rows = HEADS * SLOTS
+        own = pl.ds(pl.multiple_of((step - 1) * SLOTS, SLOTS), SLOTS)
+        asked = queries[:, own, :].reshape(rows, HD)
+        attend_slots(
+            asked, chosen_ref[...], blocks_ref[step - 1], (first + step) * SLOTS,
+            keys, values, places, out_ref, peak, denominator, numerator, score_slots,
+        )
+
+
+def blend(
+    first, key_blocks, pieces, offsets, weight_pieces, weight_places, gain, cosine,
+    signed_sine, chosen, old, keys, values, key_places, total_slots, earlier,
+):
+    slots = cosine.shape[0]
+    width = pieces[0].shape[-1]
+    blocks = gain.shape[0]
+    columns = (HEADS + 2) * HD
+    rows = HEADS * SLOTS
+    fresh = -(-(first * SLOTS + slots) // KEYS) * KEYS
+
+    def still(array):
+        origin = (0,) * array.ndim
+        return pl.BlockSpec(
+            array.shape, lambda step, *tables: origin, pipeline_mode=pl.Buffered(1)
+        )
+
+    remote = pl.BlockSpec(memory_space=pl.ANY)
+    operands = [
+        key_blocks, weight_places, gain, cosine, signed_sine, chosen, *old,
+        keys, values, key_places, *pieces, *weight_pieces, *earlier,
+    ]
+    return pl.pallas_call(
+        functools.partial(blend_kernel, first, offsets, len(pieces), len(weight_pieces)),
+        out_shape=(
+            jax.ShapeDtypeStruct((total_slots, HEADS * HD), jnp.bfloat16),
+            jax.ShapeDtypeStruct((fresh, HD), jnp.bfloat16),
+            jax.ShapeDtypeStruct((HD, fresh), jnp.bfloat16),
+        ),
+        grid_spec=pltpu.PrefetchScalarGridSpec(
+            num_scalar_prefetch=2,
+            grid=(1 + slots // SLOTS,),
+            in_specs=[
+                still(gain),
+                still(cosine),
+                still(signed_sine),
+                pl.BlockSpec((1, SLOTS), lambda step, *tables: (0, jnp.maximum(step - 1, 0))),
+                still(old[0]),
+                still(old[1]),
+            ]
+            + [remote] * (3 + len(pieces) + len(weight_pieces) + len(earlier)),
+            out_specs=(
+                pl.BlockSpec(
+                    (SLOTS, HEADS * HD), lambda step, *tables: (first + jnp.maximum(step - 1, 0), 0)
+                ),
+                pl.BlockSpec((fresh, HD), lambda step, *tables: (0, 0)),
+                pl.BlockSpec((HD, fresh), lambda step, *tables: (0, 0)),
+            ),
+            scratch_shapes=[
+                pltpu.VMEM((blocks, slots, width), jnp.bfloat16),
+                pltpu.VMEM((blocks * width, columns), jnp.bfloat16),
+                pltpu.VMEM((slots, columns), jnp.float32),
+                pltpu.VMEM((slots, HD), jnp.float32),
+                pltpu.VMEM((HEADS, slots, HD), jnp.bfloat16),
+                pltpu.VMEM((LENGTH + fresh, HD), jnp.bfloat16),
+                pltpu.VMEM((HD, LENGTH + fresh), jnp.bfloat16),
+                pltpu.VMEM((LENGTH + fresh, HD), jnp.int32),
+                pltpu.VMEM((1, rows), jnp.float32),
+                pltpu.VMEM((1, rows), jnp.float32),
+                pltpu.VMEM((HD, rows), jnp.float32),
+                pltpu.VMEM((2, KEYS, rows), jnp.float32),
+                pltpu.SemaphoreType.DMA((blocks * len(pieces),)),
+                pltpu.SemaphoreType.DMA((len(weight_pieces),)),
+                pltpu.SemaphoreType.DMA((3,)),
+            ],
+        ),
+        input_output_aliases={len(operands) - 1: 0} if earlier else {},
+        compiler_params=pltpu.CompilerParams(vmem_limit_bytes=56 * 2**20),
+        cost_estimate=pl.CostEstimate(
+            flops=4 * slots * blocks * width * columns + slots * HEADS * LENGTH * HD * 2,
+            bytes_accessed=2 * blocks * width * (slots + columns) + 8 * 2**20,
+            transcendentals=slots * HEADS * LENGTH // 2,
+        ),
+        name="blend",
+    )(*operands)
 
 
 def ring(block, axis, shift):
@@ -413,55 +629,53 @@
             partner,
             span_cosine[:, None],
             span_sine[:, None],
-            chosen[None],
             prepared,
         )
-    keys, values, key_places = prepared
+    keys, values = prepared
+    padded = -(-slot_count // KEYS) * KEYS - slot_count
+    key_places = mark(jnp.pad(chosen[None], ((0, 0), (0, padded)), constant_values=HIDDEN_POSITION))
     grouped = chosen.reshape(-1, SLOTS)
     farthest = jnp.max(jnp.where(grouped < LENGTH, grouped, -1), axis=1)
     key_blocks = (farthest + KEYS) // KEYS
-    padded = -(-slot_count // KEYS) * KEYS - slot_count
-    fresh_places = jnp.broadcast_to(
-        jnp.pad(chosen, (0, padded), constant_values=HIDDEN_POSITION)[:, None],
-        (slot_count + padded, HD),
-    )
     gain = norm_gain.reshape(NCHUNK, 1, -1)
-    nothing = (jnp.zeros((16, HD), jnp.bfloat16), jnp.zeros((16, HD), jnp.bfloat16))
-    absolute = jnp.arange(NCHUNK, dtype=jnp.int32)
-    results = []
-    fresh = nothing
-    for start, stop, pieces, piece_offsets, piece_places in (
-        (0, early, [early_tokens], (0,), absolute),
-        (early, slot_count, [late_tokens], (0,), absolute),
-    ):
-        if results:
-            results[0], pieces = lax.optimization_barrier((results[0], pieces))
-        queries, *fresh = project(
-            pieces,
-            piece_offsets,
-            piece_places,
-            gain,
-            cosine[start:stop],
-            signed_sine[start:stop],
-            mine + theirs,
-            weight_places,
-            start,
-            fresh,
-        )
-        results.append(
-            attend(
-                start // SLOTS,
-                key_blocks[start // SLOTS : stop // SLOTS],
-                queries,
-                chosen[None, start:stop],
-                keys,
-                values,
-                key_places,
-                *fresh,
-                fresh_places,
-            )
-        )
-    return jnp.concatenate(results, axis=0)[None]
+    queries, *fresh = project(
+        [early_tokens],
+        (0,),
+        gain,
+        cosine[:early],
+        signed_sine[:early],
+        mine + theirs,
+        weight_places,
+        0,
+    )
+    attended = attend(
+        0,
+        key_blocks[:EARLY],
+        queries,
+        chosen[None, :early],
+        (keys, values, key_places, *fresh),
+        slot_count,
+    )
+    attended, late_tokens = lax.optimization_barrier((attended, late_tokens))
+    attended, *_ = blend(
+        EARLY,
+        key_blocks[EARLY:],
+        [late_tokens],
+        (0,),
+        mine + theirs,
+        weight_places,
+        gain,
+        cosine[early:],
+        signed_sine[early:],
+        chosen[None, early:],
+        fresh,
+        keys,
+        values,
+        key_places,
+        slot_count,
+        (attended,),
+    )
+    return attended[None]
 
 
 def solution(mesh):

time: 238 us -> 237 us (level)
  the two profiles are of different devices: /device:TPU:7 before, /device:TPU:0 now
where the time goes in v5:
time: 237 us; the launch traced here: 235 us
  Pallas kernels  114 us (48%)
  waiting for transfers between devices  70.7 us (30%)
  local copies, waits for them, and re-layouts  13.9 us (6%)
  between operations  13.7 us (6%)
  starting transfers between devices  13.4 us (6%)
  other arithmetic  9.2 us (4%)
    pallas_call x1, Pallas kernels, blend(): pl.pallas_call(functools.partial(blend_kernel, first, offsets, len(pieces...  43.1 us
    ppermute x1, waiting for transfers between devices, ring(): behind = lax.ppermute(block, axis, shift(1))  31 us
    pallas_call x1, Pallas kernels, attend(): pl.pallas_call(functools.partial(attend_kernel, first), out_shape=jax.Sha...  26.9 us
    pallas_call x1, Pallas kernels, project(): pl.pallas_call(functools.partial(project_kernel, offsets, len(token_piece...  20.4 us
    ppermute x1, waiting for transfers between devices, shards(): near_cache = lax.ppermute(own_cache[:middle], 'col', flipped(16))  17.2 us
    pallas_call x2, Pallas kernels, prepare(): pl.pallas_call(prepare_kernel, out_shape=(jax.ShapeDtypeStruct((LENGTH, H...  12.4 us
    pallas_call x1, Pallas kernels, mark(): pl.pallas_call(mark_kernel, out_shape=jax.ShapeDtypeStruct((total, HD), j...  11.4 us
    all_gather x1, waiting for transfers between devices, shards(): early_tokens = lax.all_gather(tokens[0, :early], 'col', axis=0)  9.21 us
  transfers between devices with their start and end apart: 14, of which 5 were waited for; matrix products, arithmetic and copies ran while one was open for 8% of the time, Pallas kernels for 30%

profile of v5, /device:TPU:0, one launch (start us, length us, event | category | flops | bytes accessed | tf_op | source)
XLA Modules:
  0.0 235.1 jit_solution(16735170765425737409)
XLA Ops:
  6.5 2.1 slice.58
  8.7 2.1 collective-permute-start
  10.8 1.8 slice_bitcast_fusion.2
  12.6 4.5 %collective-permute-done = bf16[1024,128]{1,0:T(8,128)(2,1)S(1)} collective-permute-done((bf16[1024,128]{1,0:T(8,128)(2,1)S(1)}, bf16[1024,128]{1,0:T(8,128)(2,1)S(1)}, u32[]{:S(2)}, u32[]{:S(2)}) %collective-permute-start) | collective-permute-done | bytes 262176 | tf_op jit(solution)/shard_map/ppermute | solution.py:594
  17.2 1.4 pad_maximum_fusion.refs_5_.refs_12_
  18.6 1.6 collective-permute-start.1
  20.2 1.7 collective-permute-start.2
  22.0 1.8 collective-permute-start.11
  24.1 0.7 pad_maximum_fusion.5
  24.8 31.0 %collective-permute-done.1.refs_6_.refs_13_ = bf16[1024,768]{1,0:T(8,128)(2,1)} collective-permute-done((bf16[1024,768]{1,0:T(8,128)(2,1)}, bf16[1024,768]{1,0:T(8,128)(2,1)}, u32[]{:S(2)}, u32[]{:S(2)}) %collective-permute-start.1) | collective-permute-done | bytes 1572896 | tf_op jit(solution)/shard_map/ppermute | solution.py:575
  55.8 1.2 slice.66
  57.2 1.2 slice.67
  58.4 3.1 %collective-permute-start.4 = (bf16[512,768]{1,0:T(8,128)(2,1)S(1)}, bf16[512,768]{1,0:T(8,128)(2,1)S(1)}, u32[]{:S(2)}, u32[]{:S(2)}) collective-permute-start(bf16[512,768]{1,0:T(8,128)(2,1)S(1)} %slice.67), channel_id=1, source_target_pairs={{0,96},{16,112},{32,0},{48,16},{64,32},{80,48},{96,64},{112,80},{1... | collective-permute-start | bytes 2359304 | tf_op jit(solution)/shard_map/ppermute | solution.py:578
  62.2 17.2 %collective-permute-done.11.partner_ref = bf16[6144,128]{1,0:T(8,128)(2,1)} collective-permute-done((bf16[6144,128]{1,0:T(8,128)(2,1)S(1)}, bf16[6144,128]{1,0:T(8,128)(2,1)}, u32[]{:S(2)}, u32[]{:S(2)}) %collective-permute-start.11) | collective-permute-done | bytes 1572896 | tf_op jit(solution)/shard_map/ppermute | solution.py:592
  79.5 3.3 %fusion = (f32[1152,64]{1,0:T(8,128)S(1)}, f32[1152,64]{1,0:T(8,128)}, f32[1152,64]{1,0:T(8,128)}) fusion(f32[64]{0:T(128)S(1)} %multiply_exponential_fusion, f32[1152]{0:T(1024)S(1)} %convert_reduce_fusion), kind=kLoop, calls=%fused_computation.12 | loop fusion | flops 147456 | bytes 889600 | tf_op jit(solution)/shard_map/neg | solution.py:51
  83.6 0.8 slice.53.refs_5_
  86.1 11.4 %mark.1.refs_2_.refs_10_ = s32[9728,128]{1,0:T(8,128)} custom-call(s32[1,1536]{1,0:T(1,128)} %pad.4.chosen_ref), custom_call_target="tpu_custom_call" | custom-call | flops 10000000 | bytes 5242880 | tf_op jit(solution)/shard_map/mark/pallas_call | solution.py:92
  97.5 2.1 pad_maximum_fusion.3
  99.7 1.3 pad_maximum_fusion.1
  101.0 1.9 slice_bitcast_fusion.1
  102.9 8.7 %prepare.2 = (bf16[8192,128]{1,0:T(8,128)(2,1)}, bf16[128,8192]{1,0:T(8,128)(2,1)}) custom-call(s32[1]{0:T(128)} %bitcast.2.holds_key_ref, bf16[8192,128]{1,0:T(8,128)(2,1)} %bitcast.21, bf16[6144,128]{1,0:T(8,128)(2,1)} %collective-permute-done.11.partner_ref, f32[16,1,128]{2,1,0:T(1,128)} %bitcast.23, f32[16,1,128]{2,1,0:T(1,128)} %bitcast.25), custom_call_target="tpu_custom_call" | custom-call | flops 10000000 | bytes 6291456 | tf_op jit(solution)/shard_map/prepare/pallas_call | solution.py:106
  111.6 9.2 %all-gather.4.cloned.1.call-done.refs_4_ = bf16[16,768,512]{2,1,0:T(8,128)(2,1)} async-done(((bf16[1,768,512]{2,1,0:T(8,128)(2,1)}), bf16[16,768,512]{2,1,0:T(8,128)(2,1)}) %all-gather.4.cloned.1.call-update) | async-done | bytes 12582928 | tf_op jit(solution)/shard_map/all_gather | solution.py:593
  120.8 1.5 collective-permute-start.10
  122.3 20.4 %project.1 = (bf16[4,768,128]{2,1,0:T(8,128)(2,1)S(1)}, bf16[1024,128]{1,0:T(8,128)(2,1)S(1)}, bf16[128,1024]{1,0:T(8,128)(2,1)S(1)}) custom-call(s32[10]{0:T(128)S(1)} %pad_add_fusion.refs_0_.refs_1_, bf16[16,1,512]{2,1,0:T(2,128)(2,1)S(1)} %reshape.33.refs_1_.refs_2_, f32[768,128]{1,0:T(8,128)S(1)} %get-tuple-element.44.refs_2_, ...), custom_call_target="tpu_custom_call" | custom-call | flops 19327352832 | bytes 25165824 | tf_op jit(solution)/shard_map/project/pallas_call | solution.py:224
  142.7 0.9 copy-done.5
  143.6 0.7 copy-done.6
  144.3 0.7 copy-done.7
  145.0 0.8 copy-done.13
  145.8 3.7 %prepare.3 = (bf16[8192,128]{1,0:T(8,128)(2,1)}, bf16[128,8192]{1,0:T(8,128)(2,1)}) custom-call(s32[1]{0:T(128)} %bitcast.2.holds_key_ref, bf16[8192,128]{1,0:T(8,128)(2,1)} %bitcast.22, bf16[2048,128]{1,0:T(8,128)(2,1)} %copy-done.13, f32[16,1,128]{2,1,0:T(1,128)} %bitcast.24, ...), custom_call_target="tpu_custom_call", output_to_operand_aliasing={{0}: (5, {}), {1}: (6, {})} | custom-call | flops 10000000 | bytes 6291456 | tf_op jit(solution)/shard_map/prepare/pallas_call | solution.py:106
  149.5 26.9 %attend.1.refs_22_ = bf16[1152,512]{1,0:T(8,128)(2,1)} custom-call(s32[6]{0:T(128)} %bitcast.28, bf16[4,768,128]{2,1,0:T(8,128)(2,1)} %copy-done.5, s32[1,768]{1,0:T(1,128)} %slice.65.chosen_ref, bf16[8192,128]{1,0:T(8,128)(2,1)} %get-tuple-element.26.refs_0_.refs_8_, bf16[128,8192]{1,0:T(8,128)(2,1)} %get-tuple-element.27.refs_1_.refs_9_, ...), custom_call_target="tpu_custom_call" | custom-call | flops 6442450944 | bytes 12582912 | tf_op jit(solution)/shard_map/attend/pallas_call | solution.py:346
  176.4 8.7 %all-gather.6.cloned.1.call-done = bf16[6144,512]{1,0:T(8,128)(2,1)} async-done(((bf16[384,512]{1,0:T(8,128)(2,1)}), bf16[6144,512]{1,0:T(8,128)(2,1)}) %all-gather.6.cloned.1.call-update) | async-done | bytes 6291472 | tf_op jit(solution)/shard_map/all_gather | solution.py:596
  185.2 43.1 %blend.1 = (bf16[1152,512]{1,0:T(8,128)(2,1)}, bf16[1536,128]{1,0:T(8,128)(2,1)}, bf16[128,1536]{1,0:T(8,128)(2,1)}) custom-call(s32[3]{0:T(128)} %slice.50.refs_0_, s32[10]{0:T(128)} %copy-done.4, bf16[16,1,512]{2,1,0:T(2,128)(2,1)} %copy-done, f32[384,128]{1,0:T(8,128)} %get-tuple-element.46.refs_3_, ...), custom_call_target="tpu_custom_call", output_to_operand_aliasing={{0}: (22, {})} | custom-call | flops 12884901888 | bytes 27262976 | tf_op jit(solution)/shard_map/blend/pallas_call | solution.py:518
  (73 shorter events, 4.0 us)
Async XLA Ops:
  6.5 2.2 copy-start.14
  6.5 114.3 %all-gather.4.cloned.1.call-start = ((), (), s32[]{:S(2)}) async-start(), calls=%async_computation | async-start | bytes 13369344 | tf_op jit(solution)/shard_map/all_gather | solution.py:593
  8.6 8.6 %copy-start.12 = (bf16[1024,512]{1,0:T(8,128)(2,1)S(1)}, bf16[1024,512]{1,0:T(8,128)(2,1)}, u32[]{:S(2)}) copy-start(bf16[1024,512]{1,0:T(8,128)(2,1)} %param.11) | copy-start | bytes 3145732
  8.7 176.5 %all-gather.6.cloned.1.call-start = ((), (), s32[]{:S(2)}) async-start(), calls=%async_computation.1 | async-start | bytes 6684672 | tf_op jit(solution)/shard_map/all_gather | solution.py:596
  8.7 8.4 %collective-permute-start = (bf16[1024,128]{1,0:T(8,128)(2,1)S(1)}, bf16[1024,128]{1,0:T(8,128)(2,1)S(1)}, u32[]{:S(2)}, u32[]{:S(2)}) collective-permute-start(bf16[1024,128]{1,0:T(8,128)(2,1)S(1)} %copy-done.14), channel_id=1, source_target_pairs={{0,1},{1,0},{2,3},{3,2},{4,5},{5,4},{6,7},{7,6},{8,9},{9,8},{10,11... | collective-permute-start | bytes 786440 | tf_op jit(solution)/shard_map/ppermute | solution.py:594
  17.2 4.7 %copy-start.8 = (bf16[1,8192,128]{2,1,0:T(8,128)(2,1)S(1)}, bf16[1,8192,128]{2,1,0:T(8,128)(2,1)}, u32[]{:S(2)}) copy-start(bf16[1,8192,128]{2,1,0:T(8,128)(2,1)} %param.13) | copy-start | bytes 6291460
  18.6 5.2 %copy-start.15 = (s32[1,1152]{1,0:T(1,128)S(1)}, s32[1,1152]{1,0:T(1,128)}, u32[]{:S(2)}) copy-start(s32[1,1152]{1,0:T(1,128)} %param.14) | copy-start | bytes 13828
  18.6 5.3 %copy-start.19 = (s32[1,16]{1,0:T(1,128)S(1)}, s32[1,16]{1,0:T(1,128)}, u32[]{:S(2)}) copy-start(s32[1,16]{1,0:T(1,128)} %param.15) | copy-start | bytes 196
  18.6 6.1 %copy-start.17 = (s32[5]{0:T(128)S(1)}, s32[5]{0:T(128)}, u32[]{:S(2)}) copy-start(s32[5]{0:T(128)} %constant.86.clone) | copy-start | bytes 64
  18.6 6.2 %copy-start.18 = (s32[5]{0:T(128)S(1)}, s32[5]{0:T(128)}, u32[]{:S(2)}) copy-start(s32[5]{0:T(128)} %constant.85.clone) | copy-start | bytes 64
  18.6 37.2 %collective-permute-start.1 = (bf16[1024,768]{1,0:T(8,128)(2,1)}, bf16[1024,768]{1,0:T(8,128)(2,1)}, u32[]{:S(2)}, u32[]{:S(2)}) collective-permute-start(bf16[1024,768]{1,0:T(8,128)(2,1)} %pad_maximum_fusion.refs_5_.refs_12_), channel_id=1, source_target_pairs={{0,32},{16,48},{32,64},{48,80},{64,96},{80,112},{96,0},{112,16},{1... | collective-permute-start | bytes 4718600 | tf_op jit(solution)/shard_map/ppermute | solution.py:575
  20.2 37.0 %collective-permute-start.2 = (bf16[1024,768]{1,0:T(8,128)(2,1)}, bf16[1024,768]{1,0:T(8,128)(2,1)}, u32[]{:S(2)}, u32[]{:S(2)}) collective-permute-start(bf16[1024,768]{1,0:T(8,128)(2,1)} %pad_maximum_fusion.refs_5_.refs_12_), channel_id=1, source_target_pairs={{0,96},{16,112},{32,0},{48,16},{64,32},{80,48},{96,64},{112,80},{1... | collective-permute-start | bytes 4718600 | tf_op jit(solution)/shard_map/ppermute | solution.py:576
  22.0 57.5 %collective-permute-start.11 = (bf16[6144,128]{1,0:T(8,128)(2,1)S(1)}, bf16[6144,128]{1,0:T(8,128)(2,1)}, u32[]{:S(2)}, u32[]{:S(2)}) collective-permute-start(bf16[6144,128]{1,0:T(8,128)(2,1)S(1)} %slice_bitcast_fusion), channel_id=1, source_target_pairs={{0,1},{1,0},{2,3},{3,2},{4,5},{5,4},{6,7},{7,6},{8,9},{9,8},{10,11... | collective-permute-start | bytes 4718600 | tf_op jit(solution)/shard_map/ppermute | solution.py:592
  57.0 28.6 %copy-start.16 = (bf16[8192]{0:T(1024)(128)(2,1)S(1)}, bf16[8192]{0:T(1024)(128)(2,1)}, u32[]{:S(2)}) copy-start(bf16[8192]{0:T(1024)(128)(2,1)} %param.10) | copy-start | bytes 49156
  57.0 25.8 %collective-permute-start.3 = (bf16[512,768]{1,0:T(8,128)(2,1)S(1)}, bf16[512,768]{1,0:T(8,128)(2,1)S(1)}, u32[]{:S(2)}, u32[]{:S(2)}) collective-permute-start(bf16[512,768]{1,0:T(8,128)(2,1)S(1)} %slice.66), channel_id=1, source_target_pairs={{0,32},{16,48},{32,64},{48,80},{64,96},{80,112},{96,0},{112,16},{1... | collective-permute-start | bytes 2359304 | tf_op jit(solution)/shard_map/ppermute | solution.py:577
  58.4 25.0 %collective-permute-start.4 = (bf16[512,768]{1,0:T(8,128)(2,1)S(1)}, bf16[512,768]{1,0:T(8,128)(2,1)S(1)}, u32[]{:S(2)}, u32[]{:S(2)}) collective-permute-start(bf16[512,768]{1,0:T(8,128)(2,1)S(1)} %slice.67), channel_id=1, source_target_pairs={{0,96},{16,112},{32,0},{48,16},{64,32},{80,48},{96,64},{112,80},{1... | collective-permute-start | bytes 2359304 | tf_op jit(solution)/shard_map/ppermute | solution.py:578
  61.6 59.2 %collective-permute-start.5 = (bf16[1024,768]{1,0:T(8,128)(2,1)}, bf16[1024,768]{1,0:T(8,128)(2,1)}, u32[]{:S(2)}, u32[]{:S(2)}) collective-permute-start(bf16[1024,768]{1,0:T(8,128)(2,1)} %pad_maximum_fusion.refs_5_.refs_12_), channel_id=1, source_target_pairs={{0,16},{16,0},{32,48},{48,32},{64,80},{80,64},{96,112},{112,96},{1... | collective-permute-start | bytes 4718600 | tf_op jit(solution)/shard_map/ppermute | solution.py:609
  61.7 60.5 %collective-permute-start.6 = (bf16[1024,768]{1,0:T(8,128)(2,1)}, bf16[1024,768]{1,0:T(8,128)(2,1)}, u32[]{:S(2)}, u32[]{:S(2)}) collective-permute-start(bf16[1024,768]{1,0:T(8,128)(2,1)} %collective-permute-done.1.refs_6_.refs_13_), channel_id=1, source_target_pairs={{0,16},{16,0},{32,48},{48,32},{64,80},{80,64},{96,112},{112,96},{1... | collective-permute-start | bytes 4718600 | tf_op jit(solution)/shard_map/ppermute | solution.py:609
  79.5 42.8 %collective-permute-start.7 = (bf16[1024,768]{1,0:T(8,128)(2,1)}, bf16[1024,768]{1,0:T(8,128)(2,1)}, u32[]{:S(2)}, u32[]{:S(2)}) collective-permute-start(bf16[1024,768]{1,0:T(8,128)(2,1)} %collective-permute-done.2.refs_7_.refs_14_), channel_id=1, source_target_pairs={{0,16},{16,0},{32,48},{48,32},{64,80},{80,64},{96,112},{112,96},{1... | collective-permute-start | bytes 4718600 | tf_op jit(solution)/shard_map/ppermute | solution.py:609
  79.5 18.0 %copy-start.20 = (s32[9]{0:T(128)}, s32[9]{0:T(128)S(1)}, u32[]{:S(2)}) copy-start(s32[9]{0:T(128)S(1)} %and_select_fusion.1) | copy-start | bytes 112
  82.8 14.7 %copy-start.9 = (f32[1152,64]{1,0:T(8,128)}, f32[1152,64]{1,0:T(8,128)S(1)}, u32[]{:S(2)}) copy-start(f32[1152,64]{1,0:T(8,128)S(1)} %get-tuple-element.37) | copy-start | bytes 884740
  82.8 39.5 %copy-start.1 = (bf16[512,768]{1,0:T(8,128)(2,1)}, bf16[512,768]{1,0:T(8,128)(2,1)S(1)}, u32[]{:S(2)}) copy-start(bf16[512,768]{1,0:T(8,128)(2,1)S(1)} %collective-permute-done.3.refs_8_.refs_15_) | copy-start | bytes 2359300
  82.8 39.5 %collective-permute-start.8 = (bf16[512,768]{1,0:T(8,128)(2,1)S(1)}, bf16[512,768]{1,0:T(8,128)(2,1)S(1)}, u32[]{:S(2)}, u32[]{:S(2)}) collective-permute-start(bf16[512,768]{1,0:T(8,128)(2,1)S(1)} %collective-permute-done.3.refs_8_.refs_15_), channel_id=1, source_target_pairs={{0,16},{16,0},{32,48},{48,32},{64,80},{80,64},{96,112},{112,96},{1... | collective-permute-start | bytes 2359304 | tf_op jit(solution)/shard_map/ppermute | solution.py:609
  83.4 38.9 %copy-start.2 = (bf16[512,768]{1,0:T(8,128)(2,1)}, bf16[512,768]{1,0:T(8,128)(2,1)S(1)}, u32[]{:S(2)}) copy-start(bf16[512,768]{1,0:T(8,128)(2,1)S(1)} %collective-permute-done.4.refs_9_.refs_16_) | copy-start | bytes 2359300
  83.4 38.9 %collective-permute-start.9 = (bf16[512,768]{1,0:T(8,128)(2,1)S(1)}, bf16[512,768]{1,0:T(8,128)(2,1)}, u32[]{:S(2)}, u32[]{:S(2)}) collective-permute-start(bf16[512,768]{1,0:T(8,128)(2,1)S(1)} %collective-permute-done.4.refs_9_.refs_16_), channel_id=1, source_target_pairs={{0,16},{16,0},{32,48},{48,32},{64,80},{80,64},{96,112},{112,96},{1... | collective-permute-start | bytes 2359304 | tf_op jit(solution)/shard_map/ppermute | solution.py:609
  83.6 38.7 %copy-start.4 = (s32[10]{0:T(128)}, s32[10]{0:T(128)S(1)}, u32[]{:S(2)}) copy-start(s32[10]{0:T(128)S(1)} %pad_add_fusion.refs_0_.refs_1_) | copy-start | bytes 124
  85.5 36.8 %copy-start = (bf16[16,1,512]{2,1,0:T(2,128)(2,1)}, bf16[16,1,512]{2,1,0:T(2,128)(2,1)S(1)}, u32[]{:S(2)}) copy-start(bf16[16,1,512]{2,1,0:T(2,128)(2,1)S(1)} %reshape.33.refs_1_.refs_2_) | copy-start | bytes 49156
  97.5 2.1 copy-start.10
  97.5 2.1 copy-start.11
  120.8 24.2 %collective-permute-start.10 = (bf16[2048,128]{1,0:T(8,128)(2,1)}, bf16[2048,128]{1,0:T(8,128)(2,1)S(1)}, u32[]{:S(2)}, u32[]{:S(2)}) collective-permute-start(bf16[2048,128]{1,0:T(8,128)(2,1)} %slice_bitcast_fusion.1), channel_id=1, source_target_pairs={{0,1},{1,0},{2,3},{3,2},{4,5},{5,4},{6,7},{7,6},{8,9},{9,8},{10,11... | collective-permute-start | bytes 1572872 | tf_op jit(solution)/shard_map/ppermute | solution.py:598
  122.3 20.4 %copy-start.3 = (bf16[512,768]{1,0:T(8,128)(2,1)}, bf16[512,768]{1,0:T(8,128)(2,1)S(1)}, u32[]{:S(2)}) copy-start(bf16[512,768]{1,0:T(8,128)(2,1)S(1)} %collective-permute-done.8.refs_13_.refs_20_) | copy-start | bytes 2359300
  142.7 0.9 copy-start.5
  (3 other events, 2.2 us)
Sparse Core Ops, SparseCore 0:
  9.5 111.2 all-gather.3
  123.0 62.1 all-gather.5
